TPU v7x, 32 devices: a whole 2x2x4 slice. The times are simulated.
32 devices in a mesh: seq: 2 (over core), dp: 16 (over z, y, x).
Axes of the slice: x: 2, y: 2, z: 4, core: 2. Of those that a mesh axis runs over, the one named last changes fastest.
Arguments:
- visible: bfloat16 [16, 512, 768], P('dp', 'seq'), may hold values from -6 to 6
- segments: int32 [16, 512], P('dp'), may hold values from 0 to 10, as said below
- patch_ids: int32 [16, 512], P('dp'), may hold values from 0 to 195, as said below
- targets: bfloat16 [16, 10, 196, 768], P('dp', 'seq'), may hold values from -6 to 6
- master: float32 [11608064], P(('seq', 'dp'))
- moment_one: float32 [11608064], P(('seq', 'dp')), may hold values from -4.172325e-07 to 4.172325e-07
- moment_two: float32 [11608064], P(('seq', 'dp')), may hold values from 8.614701e-16 to 3.4458804e-15
- step_count: int32 [1], replicated, may hold values from 2 to 20
Outputs:
- new_moment_one: float32 [11608064], P(('seq', 'dp'))
- new_moment_two: float32 [11608064], P(('seq', 'dp'))
- new_master: float32 [11608064], P(('seq', 'dp'))
- new_copy: bfloat16 [11608064], P(('seq', 'dp'))
- grad_norm: float32 [], replicated
- loss: float32 [], replicated
Inputs may be any that keep to these rules, and one draw needn't show every extreme that they name: `segments`: in each sequence each image 0 to 9 holds exactly 49 rows, placed at drawn positions anywhere in the sequence; the other 22 rows are padding and hold 10. `patch_ids`: the 49 rows of one image hold distinct values; padding rows hold 0.
All inputs are finite; a program needn't handle non-finite values.
Results may differ from a plain program's by a relative error of at most 0.0066.
The roundings to bfloat16 on the way count: a program that leaves them out, or rounds other values in their place, can miss the bound.
Values may be sent and summed in bfloat16 or wider, within the bound.
A program may use at most 256 MiB of HBM per device.

v0:
```python
from functools import partial
import math

import jax
import jax.numpy as jnp
from jax import lax
from jax.sharding import PartitionSpec as P

D = 768
HEADS = 12
FF = 3072
DD = 512
DHEADS = 16
DFF = 2048
PIX = 768
PATCHES = 196
VIS = 49
IMG_SEQ = 10


norm_eps = 1e-06
neg_big = -1000000000.0
clip_limit = 0.0001
learn_rate = 0.03
decay_rate = 0.05
adam_eps = 1e-08
beta_mom = 0.5


def layout():
    return [
        ("embed", (PIX, D)),
        ("enc_qkv", (D, 3 * D)),
        ("enc_out", (D, D)),
        ("enc_up", (D, FF)),
        ("enc_down", (FF, D)),
        ("project", (D, DD)),
        ("dec_qkv", (DD, 3 * DD)),
        ("dec_out", (DD, DD)),
        ("dec_up", (DD, DFF)),
        ("dec_down", (DFF, DD)),
        ("pixel", (DD, PIX)),
        ("enc_vecs", (6, D)),
        ("dec_vecs", (7, DD)),
    ]


def unflatten(flat_vec):
    params = {}
    offset = 0
    for entry_name, entry_shape in layout():
        entry_size = entry_shape[0] * entry_shape[1]
        params[entry_name] = flat_vec[offset : offset + entry_size].reshape(entry_shape)
        offset += entry_size
    return params


def sincos(positions, columns):
    half_cols = columns // 2
    frequency = jnp.exp(-math.log(10000.0) * jnp.arange(half_cols, dtype=jnp.float32) / half_cols)
    angles = positions.astype(jnp.float32)[..., None] * frequency
    return jnp.concatenate([jnp.sin(angles), jnp.cos(angles)], axis=-1)


def layer_norm(inputs, norm_gain, norm_shift):
    average = jnp.mean(inputs, axis=-1, keepdims=True)
    centered = inputs - average
    spread = jnp.mean(centered * centered, axis=-1, keepdims=True)
    return centered * lax.rsqrt(spread + norm_eps) * norm_gain + norm_shift


def normalize(pixels):
    average = jnp.mean(pixels, axis=-1, keepdims=True)
    centered = pixels - average
    return centered * lax.rsqrt(jnp.mean(centered * centered, axis=-1, keepdims=True) + norm_eps)


def layer_norm_reverse(inputs, norm_gain, norm_shift, grad_rows):
    _, pullback = jax.vjp(
        layer_norm, inputs, norm_gain.astype(jnp.float32), norm_shift.astype(jnp.float32)
    )
    return pullback(grad_rows)


def gelu_backward(hidden_pre, grad_act):
    _, pullback = jax.vjp(partial(jax.nn.gelu, approximate=False), hidden_pre)
    return pullback(grad_act)[0]


def attend_scores(queries, keys_all, allowed, scale):
    scores = (
        jnp.einsum("bqhd,bkhd->bhqk", queries, keys_all, preferred_element_type=jnp.float32) * scale
    )
    if allowed is not None:
        scores = jnp.where(allowed[:, None], scores, neg_big)
    return scores


def attend_forward(queries, keys_all, values_all, allowed, scale):
    scores = attend_scores(queries, keys_all, allowed, scale)
    top_lse = jax.nn.logsumexp(scores, axis=-1, keepdims=True)
    probs = jnp.exp(scores - top_lse).astype(jnp.bfloat16)
    outputs = jnp.einsum("bhqk,bkhd->bqhd", probs, values_all, preferred_element_type=jnp.float32)
    return (outputs.astype(jnp.bfloat16), top_lse)


def attend_backward(grad_out, queries, keys_all, values_all, allowed, scale, top_lse):
    probs = jnp.exp(attend_scores(queries, keys_all, allowed, scale) - top_lse)
    grad_probs = jnp.einsum(
        "bqhd,bkhd->bhqk", grad_out, values_all, preferred_element_type=jnp.float32
    )
    grad_scores = probs * (grad_probs - jnp.sum(grad_probs * probs, axis=-1, keepdims=True))
    grad_scores = grad_scores.astype(jnp.bfloat16)
    grad_q = (
        jnp.einsum("bhqk,bkhd->bqhd", grad_scores, keys_all, preferred_element_type=jnp.float32)
        * scale
    )
    grad_k = (
        jnp.einsum("bhqk,bqhd->bkhd", grad_scores, queries, preferred_element_type=jnp.float32)
        * scale
    )
    grad_v = jnp.einsum(
        "bhqk,bqhd->bkhd", probs.astype(jnp.bfloat16), grad_out, preferred_element_type=jnp.float32
    )
    return (grad_q, grad_k, grad_v)


def block_forward(inputs, vecs, w_qkv, w_out, w_up, w_down, attention):
    normed_a = layer_norm(inputs, vecs[0], vecs[1]).astype(jnp.bfloat16)
    qkv_rows = jnp.dot(normed_a, w_qkv, preferred_element_type=jnp.float32).astype(jnp.bfloat16)
    attn_out, attn_keep = attention(qkv_rows)
    after_attn = inputs + jnp.dot(attn_out, w_out, preferred_element_type=jnp.float32)
    normed_b = layer_norm(after_attn, vecs[2], vecs[3]).astype(jnp.bfloat16)
    hidden_pre = jnp.dot(normed_b, w_up, preferred_element_type=jnp.float32)
    hidden_act = jax.nn.gelu(hidden_pre, approximate=False).astype(jnp.bfloat16)
    outputs = after_attn + jnp.dot(hidden_act, w_down, preferred_element_type=jnp.float32)
    return (
        outputs,
        (
            inputs,
            normed_a,
            qkv_rows,
            attn_out,
            attn_keep,
            after_attn,
            normed_b,
            hidden_pre,
            hidden_act,
        ),
    )


def block_backward(grad_rows, vecs, w_qkv, w_out, w_up, w_down, saved, attention_back):
    (
        inputs,
        normed_a,
        qkv_rows,
        attn_out,
        attn_keep,
        after_attn,
        normed_b,
        hidden_pre,
        hidden_act,
    ) = saved
    branch_low = grad_rows.astype(jnp.bfloat16)
    grad_down = jnp.dot(hidden_act.T, branch_low, preferred_element_type=jnp.float32)
    grad_act = jnp.dot(branch_low, w_down.T, preferred_element_type=jnp.float32)
    grad_pre = gelu_backward(hidden_pre, grad_act).astype(jnp.bfloat16)
    grad_up = jnp.dot(normed_b.T, grad_pre, preferred_element_type=jnp.float32)
    grad_normed_b = jnp.dot(grad_pre, w_up.T, preferred_element_type=jnp.float32)
    grad_mid, grad_g2, grad_b2 = layer_norm_reverse(after_attn, vecs[2], vecs[3], grad_normed_b)
    grad_mid = grad_rows + grad_mid
    middle_low = grad_mid.astype(jnp.bfloat16)
    grad_out_w = jnp.dot(attn_out.T, middle_low, preferred_element_type=jnp.float32)
    grad_attn = jnp.dot(middle_low, w_out.T, preferred_element_type=jnp.float32).astype(
        jnp.bfloat16
    )
    grad_qkv = attention_back(grad_attn, qkv_rows, attn_keep)
    grad_qkv_w = jnp.dot(normed_a.T, grad_qkv, preferred_element_type=jnp.float32)
    grad_normed_a = jnp.dot(grad_qkv, w_qkv.T, preferred_element_type=jnp.float32)
    grad_in, grad_g1, grad_b1 = layer_norm_reverse(inputs, vecs[0], vecs[1], grad_normed_a)
    vec_grads = [grad_g1, grad_b1, grad_g2, grad_b2]
    return (grad_mid + grad_in, [grad_qkv_w, grad_out_w, grad_up, grad_down], vec_grads)


def shards(visible, segments, patch_ids, targets, master, moment_one, moment_two, step_count):
    seqs, rows_half, _ = visible.shape
    images_half = targets.shape[1]
    part_index = lax.axis_index("seq")
    full_flat = lax.all_gather(master.astype(jnp.bfloat16), ("seq", "dp"), axis=0, tiled=True)
    weights = unflatten(full_flat)
    enc_vecs, decoder_vectors = (weights["enc_vecs"], weights["dec_vecs"])
    head_enc = D // HEADS
    head_dec = DD // DHEADS
    enc_scale = head_enc ** (-0.5)
    dec_scale = head_dec ** (-0.5)
    own_segments = lax.dynamic_slice_in_dim(segments, part_index * rows_half, rows_half, 1)
    own_patches = lax.dynamic_slice_in_dim(patch_ids, part_index * rows_half, rows_half, 1)
    enc_allowed = own_segments[:, :, None] == segments[:, None, :]

    def encoder_split(qkv_rows):
        return qkv_rows.reshape(seqs, rows_half, 3, HEADS, head_enc)

    def encoder_attention(qkv_rows):
        shaped = encoder_split(qkv_rows)
        keys_all, values_all = (
            lax.all_gather(shaped[:, :, 1], "seq", axis=1, tiled=True),
            lax.all_gather(shaped[:, :, 2], "seq", axis=1, tiled=True),
        )
        attn_out, top_lse = attend_forward(
            shaped[:, :, 0], keys_all, values_all, enc_allowed, enc_scale
        )
        return (attn_out.reshape(seqs * rows_half, D), (keys_all, values_all, top_lse))

    def encoder_attention_back(grad_attn, qkv_rows, attn_keep):
        keys_all, values_all, top_lse = attn_keep
        queries = encoder_split(qkv_rows)[:, :, 0]
        grad_q, grad_k, grad_v = attend_backward(
            grad_attn.reshape(seqs, rows_half, HEADS, head_enc),
            queries,
            keys_all,
            values_all,
            enc_allowed,
            enc_scale,
            top_lse,
        )
        grad_k, grad_v = (
            lax.psum_scatter(
                grad_k.astype(jnp.bfloat16), "seq", scatter_dimension=1, tiled=True
            ).astype(jnp.float32),
            lax.psum_scatter(
                grad_v.astype(jnp.bfloat16), "seq", scatter_dimension=1, tiled=True
            ).astype(jnp.float32),
        )
        stacked = jnp.stack([grad_q, grad_k, grad_v], axis=2).astype(jnp.bfloat16)
        return stacked.reshape(seqs * rows_half, 3 * D)

    def decoder_split(qkv_rows):
        return qkv_rows.reshape(-1, PATCHES, 3, DHEADS, head_dec)

    def decoder_attention(qkv_rows):
        shaped = decoder_split(qkv_rows)
        attn_out, top_lse = attend_forward(
            shaped[:, :, 0], shaped[:, :, 1], shaped[:, :, 2], None, dec_scale
        )
        return (attn_out.reshape(-1, DD), top_lse)

    def decoder_attention_back(grad_attn, qkv_rows, top_lse):
        shaped = decoder_split(qkv_rows)
        grad_q, grad_k, grad_v = attend_backward(
            grad_attn.reshape(-1, PATCHES, DHEADS, head_dec),
            shaped[:, :, 0],
            shaped[:, :, 1],
            shaped[:, :, 2],
            None,
            dec_scale,
            top_lse,
        )
        stacked = jnp.stack([grad_q, grad_k, grad_v], axis=2).astype(jnp.bfloat16)
        return stacked.reshape(-1, 3 * DD)

    enc_mats = (weights["enc_qkv"], weights["enc_out"], weights["enc_up"], weights["enc_down"])
    dec_mats = (weights["dec_qkv"], weights["dec_out"], weights["dec_up"], weights["dec_down"])
    vis_rows = visible.reshape(seqs * rows_half, PIX)
    embedded = jnp.dot(vis_rows, weights["embed"], preferred_element_type=jnp.float32)
    embedded = embedded + sincos(own_patches, D).reshape(-1, D)
    encoded, enc_saved = block_forward(embedded, enc_vecs, *enc_mats, encoder_attention)
    final_enc = layer_norm(encoded, enc_vecs[4], enc_vecs[5]).astype(jnp.bfloat16)
    projected = jnp.dot(final_enc, weights["project"], preferred_element_type=jnp.float32).astype(
        jnp.bfloat16
    )
    gathered = lax.all_gather(projected.reshape(seqs, rows_half, DD), "seq", axis=1, tiled=True)
    local_image = segments - part_index * images_half
    valid = (local_image >= 0) & (local_image < images_half)
    dec_rows = images_half * PATCHES
    target_row = jnp.where(valid, local_image * PATCHES + patch_ids, -1)
    selector = (target_row[:, None, :] == jnp.arange(dec_rows)[None, :, None]).astype(jnp.bfloat16)
    placed = jnp.einsum("snr,srd->snd", selector, gathered, preferred_element_type=jnp.float32)
    masked_rows = 1.0 - jnp.sum(selector.astype(jnp.float32), axis=-1)
    dec_in = placed + masked_rows[..., None] * decoder_vectors[6].astype(jnp.float32)
    dec_in = (dec_in + sincos(jnp.arange(dec_rows) % PATCHES, DD)).reshape(seqs * dec_rows, DD)
    decoder_result, dec_saved = block_forward(dec_in, decoder_vectors, *dec_mats, decoder_attention)
    final_dec = layer_norm(decoder_result, decoder_vectors[4], decoder_vectors[5]).astype(
        jnp.bfloat16
    )
    predicted = jnp.dot(final_dec, weights["pixel"], preferred_element_type=jnp.float32)
    error = predicted - normalize(targets.reshape(-1, PIX).astype(jnp.float32))
    mask_flat = masked_rows.reshape(-1)
    mask_total = (PATCHES - VIS) * IMG_SEQ * seqs * lax.axis_size("dp")
    loss_local = jnp.sum(mask_flat * jnp.mean(error * error, axis=-1)) / mask_total
    grad_pred = (mask_flat[:, None] * error * (2.0 / (PIX * mask_total))).astype(jnp.bfloat16)
    grad_pixel = jnp.dot(final_dec.T, grad_pred, preferred_element_type=jnp.float32)
    gradient_last_output = jnp.dot(
        grad_pred, weights["pixel"].T, preferred_element_type=jnp.float32
    )
    gradient_decoder, gradient_decoder_final_gain, gradient_decoder_final_bias = layer_norm_reverse(
        decoder_result, decoder_vectors[4], decoder_vectors[5], gradient_last_output
    )
    grad_dec_in, dec_mat_grads, decoder_vector_gradients = block_backward(
        gradient_decoder, decoder_vectors, *dec_mats, dec_saved, decoder_attention_back
    )
    grad_dec_in = grad_dec_in.reshape(seqs, dec_rows, DD)
    gradient_mask_token = jnp.sum(grad_dec_in * masked_rows[..., None], axis=(0, 1))
    safe_row = jnp.maximum(target_row, 0)
    grad_gathered = jnp.take_along_axis(grad_dec_in, safe_row[..., None], axis=1) * valid[..., None]
    grad_projected = lax.psum_scatter(
        grad_gathered.astype(jnp.bfloat16), "seq", scatter_dimension=1, tiled=True
    ).astype(jnp.float32)
    grad_projected = grad_projected.astype(jnp.bfloat16).reshape(-1, DD)
    grad_proj_w = jnp.dot(final_enc.T, grad_projected, preferred_element_type=jnp.float32)
    grad_enc_final = jnp.dot(
        grad_projected, weights["project"].T, preferred_element_type=jnp.float32
    )
    grad_enc, grad_g3, grad_b3 = layer_norm_reverse(
        encoded, enc_vecs[4], enc_vecs[5], grad_enc_final
    )
    grad_embedded, enc_mat_grads, enc_vec_grads = block_backward(
        grad_enc, enc_vecs, *enc_mats, enc_saved, encoder_attention_back
    )
    grad_embed = jnp.dot(
        vis_rows.T, grad_embedded.astype(jnp.bfloat16), preferred_element_type=jnp.float32
    )
    enc_vec_all = jnp.stack(enc_vec_grads + [grad_g3, grad_b3])
    decoder_vector_full = jnp.stack(
        decoder_vector_gradients
        + [gradient_decoder_final_gain, gradient_decoder_final_bias, gradient_mask_token]
    )
    grad_list = (
        [grad_embed]
        + enc_mat_grads
        + [grad_proj_w]
        + dec_mat_grads
        + [grad_pixel, enc_vec_all, decoder_vector_full]
    )
    grad_flat = jnp.concatenate([piece.reshape(-1) for piece in grad_list])
    grad_shard = lax.psum_scatter(grad_flat, ("seq", "dp"), scatter_dimension=0, tiled=True)
    square_sum, loss_sum = lax.psum((jnp.sum(grad_shard * grad_shard), loss_local), ("seq", "dp"))
    grad_norm = jnp.sqrt(square_sum)
    clipped = grad_shard * jnp.minimum(1.0, clip_limit / (grad_norm + 1e-06))
    new_one = beta_mom * moment_one + (1.0 - beta_mom) * clipped
    new_two = beta_mom * moment_two + (1.0 - beta_mom) * clipped * clipped
    correction = 1.0 - jnp.power(jnp.float32(beta_mom), step_count[0].astype(jnp.float32))
    new_master = master - learn_rate * (
        new_one / correction / (jnp.sqrt(new_two / correction) + adam_eps) + decay_rate * master
    )
    return (new_one, new_two, new_master, new_master.astype(jnp.bfloat16), grad_norm, loss_sum)


def solution(mesh):
    in_specs = (
        P("dp", "seq", None),
        P("dp", None),
        P("dp", None),
        P("dp", "seq", None, None),
        P(("seq", "dp")),
        P(("seq", "dp")),
        P(("seq", "dp")),
        P(),
    )
    out_specs = (P(("seq", "dp")), P(("seq", "dp")), P(("seq", "dp")), P(("seq", "dp")), P(), P())
    return jax.shard_map(shards, mesh=mesh, in_specs=in_specs, out_specs=out_specs, check_vma=False)
```

profile of v0, /device:TPU:0, one launch (start us, length us, event | category | flops | bytes accessed | tf_op | source)
XLA Modules:
  0.0 1998.6 jit_solution(3461657952615783006)
XLA Ops:
  8.8 9.0 reshape.1153
  36.1 241.3 %all-gather.6.cloned.1.call-done = bf16[32,1,362752]{2,1,0:T(2,128)(2,1)} async-done(((bf16[1,1,362752]{2,1,0:T(2,128)(2,1)}), bf16[32,1,362752]{2,1,0:T(2,128)(2,1)}) %all-gather.6.cloned.1.call-update) | async-done | bytes 23216144 | tf_op jit(solution)/shard_map/all_gather | solution.py:190
  277.4 489.7 %reduce.13 = bf16[32,362752]{1,0:T(8,128)(2,1)} reduce(bf16[32,1,362752]{2,1,0:T(2,128)(2,1)} %all-gather.6.cloned.1.call-done, bf16[]{:T(256)} %constant.58), dimensions={1}, to_apply=%all-gather.3.reduce_sub_computation | reduce | bytes 46432256 | tf_op jit(solution)/shard_map/all_gather | solution.py:190
  767.1 55.2 %reshape.1154 = bf16[11608064]{0:T(1024)(128)(2,1)} reshape(bf16[32,362752]{1,0:T(8,128)(2,1)} %reduce.13) | data formatting | bytes 46432256
  830.7 8.8 fusion.88
  846.5 7.8 reshape.1088
  877.8 8.2 reshape.1095
  886.0 9.2 reshape.1096
  895.3 11.3 multiply_convert_fusion.3
  928.3 7.5 reshape.1100
  939.3 7.5 multiply_reduce_fusion.1
  946.9 9.9 exponential_reduce_fusion
  956.9 8.7 fusion.19
  983.8 23.2 %multiply_convert_fusion.1 = (bf16[980,2048]{1,0:T(8,128)(2,1)S(1)}, f32[980,2048]{1,0:T(8,128)}, f32[980,2048]{1,0:T(8,128)}) fusion(bf16[512,2048]{1,0:T(8,128)(2,1)} %slice.196, f32[980,512]{1,0:T(8,128)S(1)} %get-tuple-element.94, f32[512]{0:T(512)} %get-tuple-element.52, f32[512]{0:T(512)S(1)} %copy-done.90, f32[980]{0:T(1024)S(1)} %fusion.56, ...), kind=kOutput, calls=%fused_computation.10 | convolution fusion | flops 2188175360 | bytes 24186528 | tf_op jit(solution)/shard_map/dot_general | solution.py:134
  1022.5 8.2 add_convert_fusion
  1045.2 9.2 convolution_bitcast_fusion.3
  1054.5 11.8 multiply_reduce_fusion
  1066.2 12.1 multiply_convert_fusion
  1083.1 6.7 copy.73
  1089.8 9.8 convert_element_type.353
  1099.7 6.1 multiply_reduce_fusion.8
  1127.5 5.2 copy.86
  1145.5 6.4 add_convert_fusion.1
  1156.4 5.6 fusion.20
  1183.0 5.8 copy.83
  1188.8 5.2 fusion.68
  1193.9 10.7 reshape.1111
  1228.0 8.0 reshape.1108
  1236.1 6.0 constant_dynamic-update-slice_fusion.11
  1274.3 667.8 %all-reduce.4.cloned.1.call-done = f32[11608064]{0:T(1024)} async-done(((f32[11608064]{0:T(1024)}), f32[11608064]{0:T(1024)}) %all-reduce.4.cloned.1.call-update) | async-done | bytes 46432272
  1944.5 40.0 %all-reduce.1 = (f32[]{:T(128)}, f32[]{:T(128)}) all-reduce(f32[]{:T(128)} %multiply_reduce_fusion.15, f32[]{:T(128)S(6)} %div.205), channel_id=1, replica_groups=mesh['seq'=2,'dp'=16] {'seq','dp'}, use_global_device_ids=true, to_apply=%region_51.52 | all-reduce | flops 2 | bytes 16 | tf_op jit(solution)/shard_map/psum | solution.py:337
  1985.2 5.5 fusion.76
  (509 shorter events, 251.6 us)
Async XLA Ops:
  7.2 847.2 %copy-start = (bf16[1,256,768]{2,1,0:T(8,128)(2,1)S(1)}, bf16[1,256,768]{2,1,0:T(8,128)(2,1)}, u32[]{:S(2)}) copy-start(bf16[1,256,768]{2,1,0:T(8,128)(2,1)} %param.8) | copy-start | bytes 1179652
  7.2 10.8 copy-start.14
  7.2 270.2 %all-gather.6.cloned.1.call-start = ((), (), s32[]{:S(2)}) async-start(), calls=%async_computation.6 | async-start | bytes 47883264 | tf_op jit(solution)/shard_map/all_gather | solution.py:190
  17.9 1124.9 %reduce-scatter.4.cloned.1.call-start = ((), (), s32[]{:S(2)}) async-start(), calls=%async_computation.3 | async-start | bytes 786432 | tf_op jit(solution)/shard_map/reduce_scatter | solution.py:306
  825.1 16.1 copy-start.2
  830.7 24.5 %copy-start.69 = (f32[768]{0:T(1024)}, f32[768]{0:T(1024)S(1)}, u32[]{:S(2)}) copy-start(f32[768]{0:T(1024)S(1)} %get-tuple-element.66) | copy-start | bytes 9220
  830.7 24.5 %copy-start.76 = (f32[768]{0:T(1024)}, f32[768]{0:T(1024)S(1)}, u32[]{:S(2)}) copy-start(f32[768]{0:T(1024)S(1)} %get-tuple-element.65) | copy-start | bytes 9220
  830.7 64.5 %copy-start.71 = (f32[768]{0:T(1024)}, f32[768]{0:T(1024)S(1)}, u32[]{:S(2)}) copy-start(f32[768]{0:T(1024)S(1)} %get-tuple-element.64) | copy-start | bytes 9220
  830.7 64.5 %copy-start.78 = (f32[768]{0:T(1024)}, f32[768]{0:T(1024)S(1)}, u32[]{:S(2)}) copy-start(f32[768]{0:T(1024)S(1)} %get-tuple-element.63) | copy-start | bytes 9220
  855.0 21.8 %copy-start.5 = (f32[256,768]{1,0:T(8,128)}, f32[256,768]{1,0:T(8,128)S(1)}, u32[]{:S(2)}) copy-start(f32[256,768]{1,0:T(8,128)S(1)} %get-tuple-element.81) | copy-start | bytes 2359300
  877.5 29.1 %copy-start.22 = (f32[256,768]{1,0:T(8,128)}, f32[256,768]{1,0:T(8,128)S(1)}, u32[]{:S(2)}) copy-start(f32[256,768]{1,0:T(8,128)S(1)} %get-tuple-element.85) | copy-start | bytes 2359300
  877.5 17.7 copy-start.94
  877.8 17.5 copy-start.116
  895.3 11.4 copy-start.45
  939.3 17.5 copy-start.12
  983.8 23.2 %copy-start.59 = (bf16[2048,512]{1,0:T(8,128)(2,1)S(1)}, bf16[2048,512]{1,0:T(8,128)(2,1)}, u32[]{:S(2)}) copy-start(bf16[2048,512]{1,0:T(8,128)(2,1)} %slice.198) | copy-start | bytes 6291460
  1021.8 13.2 copy-start.32
  1021.8 13.2 copy-start.112
  1045.2 9.3 copy-start.13
  1066.2 12.1 copy-start.25
  1089.8 9.8 copy-start.86
  1089.8 9.9 copy-start.109
  1089.8 9.9 copy-start.137
  1121.4 90.4 %reduce-scatter.8.cloned.1.call-start = ((), (), s32[]{:S(2)}) async-start(), calls=%async_computation.5 | async-start | bytes 1179648 | tf_op jit(solution)/shard_map/reduce_scatter | solution.py:231
  1162.0 49.8 %reduce-scatter.6.cloned.1.call-start = ((), (), s32[]{:S(2)}) async-start(), calls=%async_computation.4 | async-start | bytes 1179648 | tf_op jit(solution)/shard_map/reduce_scatter | solution.py:228
  1173.2 768.8 %all-reduce.4.cloned.1.call-start = ((), (), s32[]{:S(2)}) async-start(), calls=%async_computation.7 | async-start | bytes 92864512
  1193.9 10.7 copy-start.100
  1193.9 10.7 copy-start.102
  1193.9 10.7 copy-start.123
  1236.1 9.9 slice-start.4
  1272.1 713.1 %copy-start.43 = (f32[362752]{0:T(1024)S(1)}, f32[362752]{0:T(1024)}, u32[]{:S(2)}) copy-start(f32[362752]{0:T(1024)} %param.12) | copy-start | bytes 4353028
  1272.1 713.1 %copy-start.66 = (f32[362752]{0:T(1024)S(1)}, f32[362752]{0:T(1024)}, u32[]{:S(2)}) copy-start(f32[362752]{0:T(1024)} %param.14) | copy-start | bytes 4353028
  (138 other events, 597.0 us)
Sparse Core Ops, SparseCore 0:
  18.0 259.3 all-gather.5
  1121.5 6.1 reduce-scatter.3
  1162.1 6.4 reduce-scatter.7
  1173.3 6.8 reduce-scatter.5
  1272.3 669.7 all-reduce.3
where the time goes:
time: 2010 us; the launch traced here: 2000 us
  waiting for transfers between devices  909 us (45%)
  other arithmetic  556 us (28%)
  local copies, waits for them, and re-layouts  280 us (14%)
  matrix products  187 us (9%)
  blocking collectives  47 us (2%)
    unnamed x6, waiting for transfers between devices  668 us
    all_gather x1, other arithmetic, shards(): lax.all_gather(master.astype(jnp.bfloat16), ('seq', 'dp'), axis=0, tiled=...  490 us
    all_gather x1, waiting for transfers between devices, shards(): lax.all_gather(master.astype(jnp.bfloat16), ('seq', 'dp'), axis=0, tiled=...  241 us
    unnamed x345, local copies, waits for them, and re-layouts  129 us
  transfers between devices with their start and end apart: 5, of which 2 were waited for; matrix products, arithmetic and copies ran while one was open for 4% of the time, Pallas kernels for 0%

commit v1 on v0

v1 whole, which is shorter than its diff:
```python
from functools import partial
import math

import jax
import jax.numpy as jnp
import ml_dtypes
import numpy as np
from jax import lax
from jax.experimental import pallas as pl
from jax.experimental.pallas import tpu as pltpu
from jax.sharding import PartitionSpec as P

D = 768
HEADS = 12
FF = 3072
DD = 512
DHEADS = 16
DFF = 2048
PIX = 768
PATCHES = 196
VIS = 49
IMG_SEQ = 10


norm_eps = 1e-06
neg_big = -1000000000.0
clip_limit = 0.0001
learn_rate = 0.03
decay_rate = 0.05
adam_eps = 1e-08
beta_mom = 0.5


def layout():
    return [
        ("embed", (PIX, D)),
        ("enc_qkv", (D, 3 * D)),
        ("enc_out", (D, D)),
        ("enc_up", (D, FF)),
        ("enc_down", (FF, D)),
        ("project", (D, DD)),
        ("dec_qkv", (DD, 3 * DD)),
        ("dec_out", (DD, DD)),
        ("dec_up", (DD, DFF)),
        ("dec_down", (DFF, DD)),
        ("pixel", (DD, PIX)),
        ("enc_vecs", (6, D)),
        ("dec_vecs", (7, DD)),
    ]


def unflatten(flat_vec):
    params = {}
    offset = 0
    for entry_name, entry_shape in layout():
        entry_size = entry_shape[0] * entry_shape[1]
        params[entry_name] = flat_vec[offset : offset + entry_size].reshape(entry_shape)
        offset += entry_size
    return params


MESH = pl.DeviceIdType.MESH
LANES = 128
A_HALF = 1104
A_ROWS = 2 * A_HALF
B_HALF = 320
B_ROWS = 2 * B_HALF
SHARD_ROWS = 2834
PAD_ROWS = A_ROWS + B_ROWS
STAGE_ROWS = 64
PARTS = {
    "a": (0, A_ROWS),
    "a1": (0, A_HALF),
    "a2": (A_HALF, A_HALF),
    "b": (A_ROWS, B_ROWS),
    "b1": (A_ROWS, B_HALF),
    "b2": (A_ROWS + B_HALF, B_HALF),
}


def rows_of(part):
    return pl.ds(*PARTS[part])


class Place:
    def __init__(self):
        self.core = lax.axis_index("seq")
        self.chip = lax.axis_index("dp")
        chip = self.chip
        self.z = chip // 4
        y, x = (chip // 2) % 2, chip % 2
        self.col = chip % 4
        self.col_x = self.col + 1 - 2 * x
        self.col_y = self.col + 2 - 4 * y
        self.col_d = self.col_x + 2 - 4 * y
        self.side = self.z // 2
        sign = 1 - 2 * self.side
        self.inner = self.z + self.side * (3 - 2 * self.z)
        self.outer_chip, self.middle_chip = self.inner == 0, self.inner == 1
        self.to_x = (self.core, 4 * self.z + self.col_x)
        self.to_y = (self.core, 4 * self.z + self.col_y)
        self.to_far = (self.core, chip + 4 * sign)
        self.to_near = (self.core, chip - 4 * sign * self.inner)
        self.to_core = (1 - self.core, chip)

    def plane(self, mirrored):
        return mirrored + self.side * (3 - 2 * mirrored)

    def greet(self):
        barrier = pltpu.get_barrier_semaphore()
        for device in (self.to_x, self.to_y, self.to_far, self.to_core):
            pl.semaphore_signal(barrier, inc=1, device_id=device, device_id_type=MESH)

        @pl.when(self.middle_chip)
        def _():
            pl.semaphore_signal(barrier, inc=1, device_id=self.to_near, device_id_type=MESH)

        pl.semaphore_wait(barrier, 4 + self.inner)


def maybe(when, action):
    if when is None:
        action()
    else:
        pl.when(when)(action)


class Outbox:
    def __init__(self):
        self.sent = []

    def send(self, src, dst, send_sem, recv_sem, device, when=None):
        def build():
            return pltpu.make_async_remote_copy(
                src_ref=src,
                dst_ref=dst,
                send_sem=send_sem,
                recv_sem=recv_sem,
                device_id=device,
                device_id_type=MESH,
            )

        maybe(when, lambda: build().start())
        self.sent.append((when, build))

    def finish(self):
        for when, build in self.sent:
            maybe(when, lambda: build().wait_send())


def arrived(ref, sem, device, when=None):
    def wait():
        pltpu.make_async_remote_copy(
            src_ref=ref,
            dst_ref=ref,
            send_sem=sem,
            recv_sem=sem,
            device_id=device,
            device_id_type=MESH,
        ).wait_recv()

    maybe(when, wait)


def gather_exchange(held, recv, core_recv, send_x, send_y, send_far, send_near, core_send):
    at = Place()
    at.greet()
    out = Outbox()
    middle = at.middle_chip

    def block(chip, part):
        return held.at[at.core * 16 + chip, rows_of(part)]

    def move(chip, part, slot, sems_out, device, when=None):
        ref = block(chip, part)
        out.send(ref, ref, sems_out.at[chip, slot], recv.at[chip, slot], device, when)

    def to_partner(chip):
        ref = block(chip, "a")
        out.send(ref, ref, core_send.at[chip, 0], core_recv.at[chip, 0], at.to_core)

    def got(chip, part, slot):
        arrived(block(chip, part), recv.at[chip, slot], at.to_x)

    def b_plane(mirrored, core=None):
        first = 4 * at.plane(mirrored)
        core = at.core if core is None else core
        return held.at[pl.ds(core * 16 + first, 4), rows_of("b")], first

    def move_b(mirrored, sems_out, device, when=None):
        ref, first = b_plane(mirrored)
        out.send(ref, ref, sems_out.at[first, 2], recv.at[first, 2], device, when)

    def got_b(mirrored):
        ref, first = b_plane(mirrored)
        arrived(ref, recv.at[first, 2], at.to_x)

    def partner_b(mirrored):
        ref, first = b_plane(mirrored)
        out.send(ref, ref, core_send.at[first, 1], core_recv.at[first, 1], at.to_core)

    def relay(mirrored):
        first = 4 * at.plane(mirrored)
        got(first + at.col_x, "a1", 0)
        move(first + at.col_x, "a1", 0, send_y, at.to_y)
        got(first + at.col_y, "a2", 1)
        move(first + at.col_y, "a2", 1, send_x, at.to_x)

    def settle(mirrored):
        first = 4 * at.plane(mirrored)
        got(first + at.col_x, "a2", 1)
        to_partner(first + at.col_x)
        got(first + at.col_y, "a1", 0)
        to_partner(first + at.col_y)
        got(first + at.col_d, "a1", 0)
        got(first + at.col_d, "a2", 1)
        to_partner(first + at.col_d)

    def spread(mirrored, sems_on, device_on):
        chip = 4 * at.plane(mirrored) + at.col
        for slot, part in enumerate(("a1", "a2")):
            got(chip, part, slot)
            move(chip, part, slot, sems_on, device_on, middle)
            move(chip, part, slot, send_x, at.to_x)
            move(chip, part, slot, send_y, at.to_y)
        to_partner(chip)

    own = at.chip
    own_plane = 4 * at.z
    chip_x, chip_y, chip_d = own_plane + at.col_x, own_plane + at.col_y, own_plane + at.col_d
    for slot, part in enumerate(("a1", "a2")):
        move(own, part, slot, send_far, at.to_far)
        move(own, part, slot, send_near, at.to_near, middle)
    move(own, "b", 2, send_x, at.to_x)
    move(own, "b", 2, send_y, at.to_y)
    move(own, "a1", 0, send_x, at.to_x)
    move(own, "a2", 1, send_y, at.to_y)
    move(own, "a2", 1, send_x, at.to_x)
    move(own, "a1", 0, send_y, at.to_y)
    to_partner(own)

    got(chip_x, "b", 2)
    move(chip_x, "b1", 2, send_y, at.to_y)
    got(chip_y, "b", 2)
    move(chip_y, "b2", 3, send_x, at.to_x)
    relay(at.inner)
    got(chip_d, "b1", 2)
    got(chip_d, "b2", 3)
    first, second, third = 1 - at.inner, 2, 3
    spread(first, send_far, at.to_far)
    move_b(at.inner, send_far, at.to_far)
    move_b(at.inner, send_near, at.to_near, middle)
    partner_b(at.inner)
    settle(at.inner)
    relay(first)
    spread(second, send_near, at.to_near)
    got_b(first)
    move_b(first, send_far, at.to_far, middle)
    partner_b(first)
    settle(first)
    relay(second)
    spread(third, send_near, at.to_near)
    got_b(second)
    move_b(second, send_near, at.to_near, middle)
    partner_b(second)
    settle(second)
    relay(third)
    got_b(third)
    move_b(third, send_near, at.to_near, middle)
    partner_b(third)
    settle(third)
    other = 1 - at.core
    for chip in range(16):
        arrived(held.at[other * 16 + chip, rows_of("a")], core_recv.at[chip, 0], at.to_core)
    for plane in range(4):
        ref = held.at[pl.ds(other * 16 + 4 * plane, 4), rows_of("b")]
        arrived(ref, core_recv.at[4 * plane, 1], at.to_core)
    out.finish()


def matrix_entries():
    entries, offset = [], 0
    for entry_name, entry_shape in layout():
        entries.append((offset // LANES, entry_shape[0], entry_shape[1] // LANES))
        offset += entry_shape[0] * entry_shape[1]
    return entries


SPLIT_ENTRY, SPLIT_ROW = 4, 704


def gather_kernel(master_ref, *refs):
    outs, (held, flat, stage, out_sem, *sems) = refs[:13], refs[13:]
    me = lax.axis_index("seq") * 16 + lax.axis_index("dp")
    held[me, pl.ds(SHARD_ROWS - 2, 16), :] = jnp.zeros((16, LANES), jnp.bfloat16)
    held[me, pl.ds(0, SHARD_ROWS), :] = master_ref[...].astype(jnp.bfloat16)
    gather_exchange(held, *sems)
    entries = matrix_entries()

    def unpack(first, count):
        def one(index, _):
            shard, piece = index // (PAD_ROWS // 32), index % (PAD_ROWS // 32)
            start = pl.multiple_of(piece * 32, 32)
            flat[pl.ds(shard * SHARD_ROWS + piece * 32, 32), :] = held[
                first + shard, pl.ds(start, 32), :
            ].astype(jnp.float32)
            return 0

        lax.fori_loop(0, count * (PAD_ROWS // 32), one, 0)

    def place(entry, row_start, row_stop, base):
        offset, _, groups = entries[entry]
        out = outs[entry]
        count = (row_stop - row_start) // STAGE_ROWS
        local = offset + row_start * groups - base

        def copy(slot, step):
            row = pl.multiple_of(row_start + step * STAGE_ROWS, 16)
            return pltpu.make_async_copy(
                stage.at[slot, :, pl.ds(0, groups * LANES)],
                out.at[pl.ds(row, STAGE_ROWS), :],
                out_sem.at[slot],
            )

        def one(step, _):
            slot = step % 2

            @pl.when(step >= 2)
            def _():
                copy(slot, step - 2).wait()

            for group in range(groups):
                stage[slot, :, pl.ds(group * LANES, LANES)] = flat[
                    pl.ds(local + step * (STAGE_ROWS * groups) + group, STAGE_ROWS, stride=groups), :
                ].astype(jnp.bfloat16)
            copy(slot, step).start()
            return 0

        lax.fori_loop(0, count, one, 0)
        for step in range(max(count - 2, 0), count):
            copy(step % 2, step).wait()

    unpack(0, 17)
    for entry in range(SPLIT_ENTRY):
        place(entry, 0, entries[entry][1], 0)
    place(SPLIT_ENTRY, 0, SPLIT_ROW, 0)
    base = 16 * SHARD_ROWS
    unpack(16, 16)
    place(SPLIT_ENTRY, SPLIT_ROW, entries[SPLIT_ENTRY][1], base)
    for entry in range(SPLIT_ENTRY + 1, 11):
        place(entry, 0, entries[entry][1], base)
    for entry in (11, 12):
        offset, rows, groups = entries[entry]
        for group in range(groups):
            outs[entry][:, pl.ds(group * LANES, LANES)] = flat[
                pl.ds(offset - base + group, rows, stride=groups), :
            ]


def gather_weights(master_rows):
    shapes = [entry_shape for _, entry_shape in layout()]
    hbm = pl.BlockSpec(memory_space=pl.ANY)
    vmem = pl.BlockSpec(memory_space=pltpu.VMEM)
    widest = max(shape[1] for shape in shapes)
    sixteen = pltpu.SemaphoreType.DMA((16, 4))
    return pl.pallas_call(
        gather_kernel,
        out_shape=[jax.ShapeDtypeStruct(s, jnp.bfloat16) for s in shapes[:11]]
        + [jax.ShapeDtypeStruct(s, jnp.float32) for s in shapes[11:]],
        in_specs=[vmem],
        out_specs=[hbm] * 11 + [vmem] * 2,
        scratch_shapes=[
            pltpu.VMEM((32, PAD_ROWS, LANES), jnp.bfloat16),
            pltpu.VMEM((17 * SHARD_ROWS + 30, LANES), jnp.float32),
            pltpu.VMEM((2, STAGE_ROWS, widest), jnp.bfloat16),
            pltpu.SemaphoreType.DMA((2,)),
            sixteen,
            pltpu.SemaphoreType.DMA((16, 2)),
            sixteen,
            sixteen,
            sixteen,
            sixteen,
            pltpu.SemaphoreType.DMA((16, 2)),
        ],
        compiler_params=pltpu.CompilerParams(
            collective_id=0, has_side_effects=True, vmem_limit_bytes=60 * 1024 * 1024
        ),
        name="gather_weights",
    )(master_rows)


def reduce_kernel(
    grad_ref,
    loss_ref,
    shard_ref,
    total_ref,
    own,
    theirs,
    from_x,
    from_y,
    pass_x,
    pass_y,
    far_a,
    near_a,
    far_b,
    near_b,
    scalars,
    load_sem,
    core_send,
    core_recv,
    send_x,
    send_y,
    send_z,
    recv_x,
    recv_y,
    recv_z,
    tiny_send,
    tiny_recv,
):
    at = Place()
    far, near = at.to_far, at.to_near
    outer, middle = at.outer_chip, at.middle_chip
    tail = pl.ds(SHARD_ROWS - 2, 16)
    for index in range(16):
        own[index, tail, :] = jnp.zeros((16, LANES), jnp.bfloat16)
        theirs[index, tail, :] = jnp.zeros((16, LANES), jnp.bfloat16)
    at.greet()
    out = Outbox()
    order = (3, 2, 1 - at.inner, at.inner)
    body = pl.ds(0, SHARD_ROWS)

    def shard_rows(core, chip):
        return grad_ref.at[pl.ds((core * 16 + chip) * SHARD_ROWS, SHARD_ROWS)]

    def load(chip):
        return pltpu.make_async_copy(
            shard_rows(at.core, chip), own.at[chip, body], load_sem.at[chip]
        )

    for mirrored in order:
        for column in range(4):
            chip = 4 * at.plane(mirrored) + column
            out.send(
                shard_rows(1 - at.core, chip),
                theirs.at[chip, body],
                core_send.at[chip],
                core_recv.at[chip],
                at.to_core,
            )
            load(chip).start()

    def combine(dst, start, terms, size, chunk):
        def one(step, _):
            row = pl.multiple_of(step * chunk, 16)
            total = None
            for ref, first in terms:
                piece = ref[pl.ds(pl.multiple_of(first + row, 16), chunk), :].astype(jnp.float32)
                total = piece if total is None else total + piece
            dst[pl.ds(pl.multiple_of(start + row, 16), chunk), :] = total.astype(dst.dtype)
            return 0

        lax.fori_loop(0, size // chunk, one, 0)

    def pair(mirrored):
        for column in range(4):
            chip = 4 * at.plane(mirrored) + column
            load(chip).wait()
            arrived(theirs.at[chip, body], core_recv.at[chip], at.to_core)
            combine(
                own.at[chip], 0, [(own.at[chip], 0), (theirs.at[chip], 0)], PAD_ROWS, 32
            )

    def chips(mirrored):
        first = 4 * at.plane(mirrored)
        return (
            first // 4,
            first + at.col,
            first + at.col_x,
            first + at.col_y,
            first + at.col_d,
        )

    def part(chip, name):
        return own.at[chip, rows_of(name)]

    halves = {"a": ("a1", "a2", A_HALF, 0), "b": ("b1", "b2", B_HALF, A_ROWS)}

    def open_plane(plane, ids, kind, slot):
        _, chip_x, chip_y, chip_d = ids
        one, two, half, begin = halves[kind]
        rows = pl.ds(begin, half)
        more = pl.ds(begin + half, half)
        out.send(part(chip_d, one), pass_y.at[plane, rows], send_y.at[plane, slot], recv_y.at[plane, slot], at.to_y)
        out.send(part(chip_d, two), pass_x.at[plane, rows], send_x.at[plane, slot], recv_x.at[plane, slot], at.to_x)
        out.send(part(chip_x, two), from_x.at[plane, more], send_x.at[plane, slot + 1], recv_x.at[plane, slot + 1], at.to_x)
        out.send(part(chip_y, one), from_y.at[plane, rows], send_y.at[plane, slot + 1], recv_y.at[plane, slot + 1], at.to_y)

    def relay_plane(plane, ids, kind, slot):
        _, chip_x, chip_y, _ = ids
        one, two, half, begin = halves[kind]
        rows = pl.ds(begin, half)
        more = pl.ds(begin + half, half)
        chunk = half // 4 if kind == "b" else half // 3
        arrived(pass_y.at[plane, rows], recv_y.at[plane, slot], at.to_y)
        combine(
            own.at[chip_x], begin, [(own.at[chip_x], begin), (pass_y.at[plane], begin)], half, chunk
        )
        out.send(part(chip_x, one), from_x.at[plane, rows], send_x.at[plane, slot + 2], recv_x.at[plane, slot + 2], at.to_x)
        arrived(pass_x.at[plane, rows], recv_x.at[plane, slot], at.to_x)
        combine(
            own.at[chip_y],
            begin + half,
            [(own.at[chip_y], begin + half), (pass_x.at[plane], begin)],
            half,
            chunk,
        )
        out.send(part(chip_y, two), from_y.at[plane, more], send_y.at[plane, slot + 2], recv_y.at[plane, slot + 2], at.to_y)

    def close_plane(plane, kind, slot):
        _, _, half, begin = halves[kind]
        rows = pl.ds(begin, half)
        more = pl.ds(begin + half, half)
        arrived(from_x.at[plane, more], recv_x.at[plane, slot + 1], at.to_x)
        arrived(from_y.at[plane, rows], recv_y.at[plane, slot + 1], at.to_y)
        arrived(from_x.at[plane, rows], recv_x.at[plane, slot + 2], at.to_x)
        arrived(from_y.at[plane, more], recv_y.at[plane, slot + 2], at.to_y)

    def begin_a(mirrored):
        plane, *ids = chips(mirrored)
        open_plane(plane, ids, "a", 0)

    def relay_a(mirrored):
        plane, *ids = chips(mirrored)
        relay_plane(plane, ids, "a", 0)

    def close_a(mirrored):
        close_plane(chips(mirrored)[0], "a", 0)

    def plane_terms(plane, chip):
        return [(own.at[chip], 0), (from_x.at[plane], 0), (from_y.at[plane], 0)]

    def start_line_a(mirrored, when):
        plane, chip, *_ = chips(mirrored)

        def add():
            combine(own.at[chip], 0, plane_terms(plane, chip), A_ROWS, A_HALF // 3)

        maybe(when, add)
        out.send(part(chip, "a"), near_a.at[plane], send_z.at[plane, 0], recv_z.at[plane, 0], far, when)

    def pass_line_a(mirrored, source, slot, target, target_buffer, target_slot):
        plane, chip, *_ = chips(mirrored)
        arrived(source.at[plane], recv_z.at[plane, slot], at.to_x, middle)

        def add():
            terms = plane_terms(plane, chip) + [(source.at[plane], 0)]
            combine(own.at[chip], 0, terms, A_ROWS, A_HALF // 3)

        maybe(middle, add)
        out.send(
            part(chip, "a"),
            target_buffer.at[plane],
            send_z.at[plane, 0],
            recv_z.at[plane, target_slot],
            target,
            middle,
        )

    def b_rows(plane):
        return own.at[pl.ds(4 * plane, 4), rows_of("b")]

    def start_line_b(mirrored):
        plane = at.plane(mirrored)
        out.send(b_rows(plane), near_b.at[plane], send_z.at[plane, 2], recv_z.at[plane, 2], far, outer)

    def add_b(plane, source):
        for column in range(4):
            chip = 4 * plane + column
            combine(
                own.at[chip],
                A_ROWS,
                [(own.at[chip], A_ROWS), (source.at[plane, column], 0)],
                B_ROWS,
                B_ROWS // 4,
            )

    def pass_line_b(mirrored, source, slot, target, target_buffer, target_slot):
        plane = at.plane(mirrored)
        arrived(source.at[plane], recv_z.at[plane, slot], at.to_x, middle)
        maybe(middle, lambda: add_b(plane, source))
        out.send(
            b_rows(plane),
            target_buffer.at[plane],
            send_z.at[plane, 2],
            recv_z.at[plane, target_slot],
            target,
            middle,
        )

    for step in range(3):
        pair(order[step])
        begin_a(order[step])
        start_line_b(order[step])
        if step >= 1:
            relay_a(order[step - 1])
        if step == 2:
            close_a(order[0])
            start_line_a(order[0], outer)
    pair(order[3])
    begin_a(order[3])
    relay_a(order[2])
    close_a(order[1])
    start_line_a(order[1], outer)
    pass_line_b(order[0], near_b, 2, far, far_b, 3)
    pass_line_b(order[1], near_b, 2, far, far_b, 3)
    pass_line_a(order[0], near_a, 0, far, far_a, 1)
    relay_a(order[3])
    pass_line_b(order[2], far_b, 3, near, far_b, 3)
    own_plane, chip, chip_x, chip_y, chip_d = chips(at.inner)
    arrived(far_b.at[own_plane], recv_z.at[own_plane, 3], at.to_x)
    add_b(own_plane, far_b)
    arrived(near_b.at[own_plane], recv_z.at[own_plane, 2], at.to_x, middle)
    maybe(middle, lambda: add_b(own_plane, near_b))
    ids = (chip, chip_x, chip_y, chip_d)
    open_plane(own_plane, ids, "b", 3)
    close_a(order[2])
    start_line_a(order[2], outer)
    pass_line_a(order[1], near_a, 0, far, far_a, 1)
    pass_line_a(order[2], far_a, 1, near, far_a, 1)
    relay_plane(own_plane, ids, "b", 3)
    close_a(order[3])
    terms = plane_terms(own_plane, chip)
    arrived(near_a.at[own_plane], recv_z.at[own_plane, 0], at.to_x, middle)

    @pl.when(outer)
    def _():
        near_a[own_plane] = jnp.zeros((A_ROWS, LANES), jnp.bfloat16)

    arrived(far_a.at[own_plane], recv_z.at[own_plane, 1], at.to_x)
    terms_line = terms + [(near_a.at[own_plane], 0), (far_a.at[own_plane], 0)]
    combine(shard_ref, 0, terms_line, A_ROWS, A_HALF // 3)
    close_plane(own_plane, "b", 3)
    terms_b = [(ref, A_ROWS) for ref, _ in terms]
    combine(shard_ref, A_ROWS, terms_b, B_ROWS, B_ROWS // 4)

    def squares(step, carry):
        piece = shard_ref[pl.ds(pl.multiple_of(step * 32, 32), 32), :]
        piece = piece * piece
        return carry + jnp.sum(piece.reshape(4, 8, LANES), axis=0)

    square = lax.fori_loop(0, PAD_ROWS // 32, squares, jnp.zeros((8, LANES), jnp.float32))
    me = at.core * 16 + at.chip
    scalars[me, 0] = square
    scalars[me, 1] = jnp.broadcast_to(loss_ref[...], (8, LANES))
    barrier_free_devices = []
    for step in range(1, 32):
        peer = (me + step) % 32
        barrier_free_devices.append(peer)
        out.send(
            scalars.at[me],
            scalars.at[me],
            tiny_send.at[step],
            tiny_recv.at[me],
            (peer // 16, peer % 16),
        )
    for step in range(1, 32):
        peer = (me + step) % 32
        arrived(scalars.at[peer], tiny_recv.at[peer], at.to_x)
    total_ref[...] = jnp.sum(scalars[...], axis=0)
    out.finish()


def reduce_gradients(grad_rows, loss_row):
    hbm = pl.BlockSpec(memory_space=pl.ANY)
    vmem = pl.BlockSpec(memory_space=pltpu.VMEM)
    low = jnp.bfloat16
    shard_total, totals = pl.pallas_call(
        reduce_kernel,
        out_shape=[
            jax.ShapeDtypeStruct((PAD_ROWS, LANES), jnp.float32),
            jax.ShapeDtypeStruct((2, 8, LANES), jnp.float32),
        ],
        in_specs=[hbm, vmem],
        out_specs=[vmem, vmem],
        scratch_shapes=[pltpu.VMEM((16, PAD_ROWS, LANES), low)] * 2
        + [pltpu.VMEM((4, PAD_ROWS, LANES), low)] * 4
        + [pltpu.VMEM((4, A_ROWS, LANES), low)] * 2
        + [pltpu.VMEM((4, 4, B_ROWS, LANES), low)] * 2
        + [pltpu.VMEM((32, 2, 8, LANES), jnp.float32)]
        + [pltpu.SemaphoreType.DMA((16,))] * 3
        + [pltpu.SemaphoreType.DMA((4, 6))] * 2
        + [pltpu.SemaphoreType.DMA((4, 3))]
        + [pltpu.SemaphoreType.DMA((4, 6))] * 2
        + [pltpu.SemaphoreType.DMA((4, 4))]
        + [pltpu.SemaphoreType.DMA((32,))] * 2,
        compiler_params=pltpu.CompilerParams(
            collective_id=1, has_side_effects=True, vmem_limit_bytes=56 * 1024 * 1024
        ),
        name="reduce_gradients",
    )(grad_rows, loss_row)
    return shard_total[:SHARD_ROWS].reshape(-1), jnp.sum(totals[0]), totals[1, 0, 0]


LOW = jnp.bfloat16
FULL = jnp.float32
TILE = 256
NEG = neg_big
ROOT_HALF = math.sqrt(0.5)
BELL = 1.0 / math.sqrt(2.0 * math.pi)


def dot_nn(left, right):
    return lax.dot_general(left, right, (((1,), (0,)), ((), ())), preferred_element_type=FULL)


def dot_nt(left, right):
    return lax.dot_general(left, right, (((1,), (1,)), ((), ())), preferred_element_type=FULL)


def dot_tn(left, right):
    return lax.dot_general(left, right, (((0,), (0,)), ((), ())), preferred_element_type=FULL)


def loop(count, body):
    def one(step, carry):
        body(step)
        return carry

    lax.fori_loop(0, count, one, 0)


def span(step, size):
    return pl.ds(pl.multiple_of(step * size, size), size)


def norm_parts(rows):
    average = jnp.mean(rows, axis=-1, keepdims=True)
    centered = rows - average
    scale = lax.rsqrt(jnp.mean(centered * centered, axis=-1, keepdims=True) + norm_eps)
    return centered * scale, scale


def norm_into(dst, src, gain, shift, rows, chunk):
    def one(step):
        at = span(step, chunk)
        unit, _ = norm_parts(src[at, :])
        dst[at, :] = (unit * gain + shift).astype(LOW)

    loop(rows // chunk, one)


def norm_back(dst, src, grad, residual, gain, gain_grad, shift_grad, rows, chunk):
    width = src.shape[1]

    def one(step, carry):
        at = span(step, chunk)
        unit, scale = norm_parts(src[at, :])
        upper = grad[at, :]
        gains = carry[0] + jnp.sum((upper * unit).reshape(chunk // 8, 8, width), axis=0)
        shifts = carry[1] + jnp.sum(upper.reshape(chunk // 8, 8, width), axis=0)
        upper = upper * gain
        lower = scale * (
            upper
            - jnp.mean(upper, axis=-1, keepdims=True)
            - unit * jnp.mean(upper * unit, axis=-1, keepdims=True)
        )
        if residual is not None:
            lower = lower + residual[at, :]
        dst[at, :] = lower
        return gains, shifts

    zero = jnp.zeros((8, width), FULL)
    gains, shifts = lax.fori_loop(0, rows // chunk, one, (zero, zero))
    gain_grad[...] = jnp.sum(gains, axis=0, keepdims=True)
    shift_grad[...] = jnp.sum(shifts, axis=0, keepdims=True)


def product_into(dst, left, right, columns, tile=TILE, residual=None):
    def one(step):
        at = span(step, tile)
        value = dot_nn(left[...], right[:, at])
        if residual is not None:
            value = value + residual[:, at]
        dst[:, at] = value.astype(dst.dtype)

    loop(columns // tile, one)


def product_t_into(dst, left, right, columns, tile=TILE):
    def one(step):
        at = span(step, tile)
        dst[:, at] = dot_nt(left[...], right[at, :]).astype(dst.dtype)

    loop(columns // tile, one)


def up_into(act, slope, left, w_up, columns, tile):
    def one(step):
        at = span(step, tile)
        hidden = dot_nn(left[...], w_up[:, at])
        share = 0.5 * (1.0 + lax.erf(hidden * ROOT_HALF))
        act[:, at] = (hidden * share).astype(LOW)
        slope[:, at] = share + hidden * (BELL * jnp.exp(-0.5 * hidden * hidden))

    loop(columns // tile, one)


def down_back_into(grad_pre, branch, w_down, slope, columns, tile):
    def one(step):
        at = span(step, tile)
        grad_pre[:, at] = (dot_nt(branch[...], w_down[at, :]) * slope[:, at]).astype(LOW)

    loop(columns // tile, one)


def weight_grad(out, out_row, left, right, turned, piled, stage, stage_sem):
    rows, columns = left.shape[1], right.shape[1]
    groups = columns // LANES
    steps = rows // TILE
    count = TILE * groups
    depth = left.shape[0]

    def copy(slot, step):
        return pltpu.make_async_copy(
            stage.at[slot, pl.ds(0, count)],
            out.at[pl.ds(pl.multiple_of(out_row + step * count, 512), count)],
            stage_sem.at[slot],
        )

    def one(step):
        slot = step % 2
        turned[:, pl.ds(0, depth)] = left[:, span(step, TILE)].T

        def across(tile):
            value = dot_nn(turned[:, pl.ds(0, depth)], right[:, span(tile, TILE)])
            for half in range(2):
                piled[pl.ds(tile * 2 + half, TILE, stride=groups), :] = value[
                    :, half * LANES : (half + 1) * LANES
                ]

        loop(columns // TILE, across)

        @pl.when(step >= 2)
        def _():
            copy(slot, step - 2).wait()

        def shrink(piece):
            at = span(piece, TILE)
            stage[slot, at, :] = piled[at, :].astype(LOW)

        loop(groups, shrink)
        copy(slot, step).start()

    loop(steps, one)
    for step in range(max(steps - 2, 0), steps):
        copy(step % 2, step).wait()


def head_masks(head_size, dtype):
    lane = lax.broadcasted_iota(jnp.int32, (1, LANES), 1) // head_size
    return [(lane == head).astype(dtype) for head in range(LANES // head_size)]


def stacked(rows, masks):
    return jnp.concatenate([rows * mask for mask in masks], axis=0)


def unstacked(rows, masks, size):
    total = None
    for index, mask in enumerate(masks):
        piece = rows[index * size : (index + 1) * size] * mask
        total = piece if total is None else total + piece
    return total


def soft_rows(queries, keys, allowed, scale):
    scores = jnp.where(allowed, dot_nt(queries, keys) * scale, NEG)
    scores = scores - jnp.max(scores, axis=-1, keepdims=True)
    powers = jnp.exp(scores)
    return powers / jnp.sum(powers, axis=-1, keepdims=True)


def attend_into(dst, qkv, rows, at, width, allowed, head_size):
    masks = head_masks(head_size, LOW)
    size = rows.size
    column = lambda part: pl.ds(pl.multiple_of(part * width + at * LANES, LANES), LANES)
    queries = stacked(qkv[rows, column(0)], masks)
    probs = soft_rows(queries, qkv[rows, column(1)], allowed, head_size**-0.5).astype(LOW)
    values = dot_nn(probs, qkv[rows, column(2)])
    dst[rows, column(0)] = unstacked(values, head_masks(head_size, FULL), size).astype(LOW)


def attend_back_into(dst, grad, qkv, rows, at, width, allowed, head_size):
    masks = head_masks(head_size, LOW)
    lanes = head_masks(head_size, FULL)
    size = rows.size
    scale = head_size**-0.5
    column = lambda part: pl.ds(pl.multiple_of(part * width + at * LANES, LANES), LANES)
    queries = stacked(qkv[rows, column(0)], masks)
    keys = qkv[rows, column(1)]
    probs = soft_rows(queries, keys, allowed, scale)
    grads = stacked(grad[rows, column(0)], masks)
    slopes = dot_nt(grads, qkv[rows, column(2)])
    slopes = probs * (slopes - jnp.sum(slopes * probs, axis=-1, keepdims=True))
    slopes = slopes.astype(LOW)
    dst[rows, column(0)] = (unstacked(dot_nn(slopes, keys), lanes, size) * scale).astype(LOW)
    dst[rows, column(1)] = (dot_tn(slopes, queries) * scale).astype(LOW)
    dst[rows, column(2)] = dot_tn(probs.astype(LOW), grads).astype(LOW)


def fetch(pairs, sems):
    for index, (src, dst) in enumerate(pairs):
        pltpu.make_async_copy(src, dst, sems.at[index]).start()

    def ready(index):
        src, dst = pairs[index]
        pltpu.make_async_copy(src, dst, sems.at[index]).wait()

    return ready


def position_table(columns, padded):
    half = columns // 2
    frequency = np.exp(
        np.float32(-math.log(10000.0)) * np.arange(half, dtype=np.float32) / np.float32(half)
    ).astype(np.float32)
    angles = np.arange(PATCHES, dtype=np.float32)[:, None] * frequency
    table = np.zeros((padded, columns), np.float32)
    table[:PATCHES] = np.concatenate(
        [np.sin(angles.astype(np.float64)), np.cos(angles.astype(np.float64))], axis=-1
    )
    return table


def split_low(table):
    parts, rest = [], table.astype(np.float64)
    for _ in range(3):
        part = rest.astype(ml_dtypes.bfloat16)
        parts.append(part)
        rest = rest - part.astype(np.float64)
    return np.stack(parts)


ROWS = 256
ENC_CHUNK = 64
FETCHED = ("embed", "enc_qkv", "enc_out", "enc_up", "enc_down", "project")


def encoder_forward_kernel(
    part_ref,
    visible_ref,
    segments_ref,
    patches_ref,
    table_ref,
    vecs_ref,
    w_embed_hbm,
    w_qkv_hbm,
    w_out_hbm,
    w_up_hbm,
    w_down_hbm,
    w_proj_hbm,
    vis_rows,
    embedded,
    normed_a,
    qkv_rows,
    attn_out,
    after_attn,
    normed_b,
    slope,
    hidden_act,
    encoded,
    final_enc,
    projected,
    row_facts,
    column_facts,
    w_embed,
    w_qkv,
    w_out,
    w_up,
    w_down,
    w_proj,
    sems,
):
    ready = fetch(
        [
            (w_embed_hbm, w_embed),
            (w_qkv_hbm, w_qkv),
            (w_out_hbm, w_out),
            (w_up_hbm, w_up),
            (w_down_hbm, w_down),
            (w_proj_hbm, w_proj),
        ],
        sems,
    )
    part = part_ref[0]
    total = segments_ref.shape[1]
    images = IMG_SEQ // 2
    spare = ROWS - images * VIS
    segments = segments_ref[...]
    image = segments - part * images
    inside = (image >= 0) & (image < images)
    padding = segments == IMG_SEQ
    flags = jnp.concatenate(
        [
            inside.astype(FULL),
            padding.astype(FULL),
            jnp.zeros((6, total), FULL),
        ],
        axis=0,
    ).astype(LOW)
    row = lax.broadcasted_iota(jnp.int32, (total, total), 0)
    column = lax.broadcasted_iota(jnp.int32, (total, total), 1)
    counts = dot_nn(flags, (row <= column).astype(FULL).astype(LOW)).astype(jnp.int32)
    inside_count, padding_count = counts[0:1], counts[1:2]
    padding_slot = padding_count - part * spare
    chosen = inside | (padding & (padding_slot >= 1) & (padding_slot <= spare))
    slot = inside_count + jnp.clip(padding_slot, 0, spare) - 1
    slot = jnp.where(chosen, slot, -1)
    select = (lax.broadcasted_iota(jnp.int32, (ROWS, total), 0) == slot).astype(FULL).astype(LOW)
    facts = jnp.concatenate(
        [segments.astype(FULL), patches_ref[...].astype(FULL), jnp.zeros((LANES - 2, total), FULL)],
        axis=0,
    ).astype(LOW)
    row_facts[...] = dot_nt(facts[0:16], select)
    column_facts[...] = dot_nt(select, facts)
    vis_rows[...] = dot_nn(select, visible_ref[...]).astype(LOW)
    patch = column_facts[:, 1:2].astype(jnp.int32)
    spot = (lax.broadcasted_iota(jnp.int32, (ROWS, table_ref.shape[1]), 1) == patch).astype(FULL).astype(LOW)
    embedded[...] = dot_nn(spot, table_ref[0]) + dot_nn(spot, table_ref[1]) + dot_nn(spot, table_ref[2])
    ready(0)
    product_into(embedded, vis_rows, w_embed, D, residual=embedded)
    vec = lambda index: vecs_ref[index : index + 1, :]
    norm_into(normed_a, embedded, vec(0), vec(1), ROWS, ENC_CHUNK)
    ready(1)
    product_into(qkv_rows, normed_a, w_qkv, 3 * D)
    allowed = column_facts[:, 0:1] == row_facts[0:1, :]
    allowed = jnp.concatenate([allowed.astype(FULL)] * 2, axis=0) > 0.5
    loop(
        D // LANES,
        lambda at: attend_into(attn_out, qkv_rows, pl.ds(0, ROWS), at, D, allowed, D // HEADS),
    )
    ready(2)
    product_into(after_attn, attn_out, w_out, D, residual=embedded)
    norm_into(normed_b, after_attn, vec(2), vec(3), ROWS, ENC_CHUNK)
    ready(3)
    up_into(hidden_act, slope, normed_b, w_up, FF, 512)
    ready(4)
    product_into(encoded, hidden_act, w_down, D, residual=after_attn)
    norm_into(final_enc, encoded, vec(4), vec(5), ROWS, ENC_CHUNK)
    ready(5)
    product_into(projected, final_enc, w_proj, DD)


def encoder_forward(part, visible_rows, segments, patch_ids, weights):
    hbm = pl.BlockSpec(memory_space=pl.ANY)
    vmem = pl.BlockSpec(memory_space=pltpu.VMEM)
    smem = pl.BlockSpec(memory_space=pltpu.SMEM)
    table = jnp.asarray(split_low(position_table(D, 256)))
    low, full = (lambda *s: jax.ShapeDtypeStruct(s, LOW)), (lambda *s: jax.ShapeDtypeStruct(s, FULL))
    mats = [weights[entry] for entry in FETCHED]
    return pl.pallas_call(
        encoder_forward_kernel,
        out_shape=[
            low(ROWS, PIX),
            full(ROWS, D),
            low(ROWS, D),
            low(ROWS, 3 * D),
            low(ROWS, D),
            full(ROWS, D),
            low(ROWS, D),
            full(ROWS, FF),
            low(ROWS, FF),
            full(ROWS, D),
            low(ROWS, D),
            low(ROWS, DD),
            full(16, ROWS),
            full(ROWS, LANES),
        ],
        in_specs=[smem] + [vmem] * 5 + [hbm] * 6,
        out_specs=[vmem] * 14,
        scratch_shapes=[pltpu.VMEM(mat.shape, LOW) for mat in mats] + [pltpu.SemaphoreType.DMA((6,))],
        compiler_params=pltpu.CompilerParams(vmem_limit_bytes=56 * 1024 * 1024),
        name="encoder_forward",
    )(part, visible_rows, segments, patch_ids, table, weights["enc_vecs"], *mats)


def encoder_backward_kernel(
    vis_rows,
    embedded,
    normed_a,
    qkv_rows,
    attn_out,
    after_attn,
    normed_b,
    slope,
    hidden_act,
    encoded,
    final_enc,
    row_facts,
    column_facts,
    grad_projected,
    vecs_ref,
    decoder_vecs,
    w_qkv_hbm,
    w_out_hbm,
    w_up_hbm,
    w_down_hbm,
    w_proj_hbm,
    partial_ref,
    flat_ref,
    w_qkv,
    w_out,
    w_up,
    w_down,
    w_proj,
    grad_rows,
    upper,
    branch,
    grad_pre,
    middle,
    grad_attn,
    grad_qkv,
    vec_grads,
    turned,
    piled,
    stage,
    vec_stage,
    stage_sem,
    sems,
):
    del partial_ref
    ready = fetch(
        [
            (w_proj_hbm, w_proj),
            (w_down_hbm, w_down),
            (w_up_hbm, w_up),
            (w_out_hbm, w_out),
            (w_qkv_hbm, w_qkv),
        ],
        sems,
    )
    entries = matrix_entries()
    vec = lambda index: vecs_ref[index : index + 1, :]
    grad_of = lambda index: vec_grads.at[pl.ds(index, 1), :]

    def emit(entry, left, right):
        weight_grad(flat_ref, entries[entry][0], left, right, turned, piled, stage, stage_sem)

    emit(5, final_enc, grad_projected)
    ready(0)
    product_t_into(upper, grad_projected, w_proj, D)
    norm_back(grad_rows, encoded, upper, None, vec(4), grad_of(4), grad_of(5), ROWS, ENC_CHUNK)
    branch[...] = grad_rows[...].astype(LOW)
    emit(4, hidden_act, branch)
    ready(1)
    down_back_into(grad_pre, branch, w_down, slope, FF, 512)
    emit(3, normed_b, grad_pre)
    ready(2)
    product_t_into(upper, grad_pre, w_up, D)
    norm_back(grad_rows, after_attn, upper, grad_rows, vec(2), grad_of(2), grad_of(3), ROWS, ENC_CHUNK)
    middle[...] = grad_rows[...].astype(LOW)
    emit(2, attn_out, middle)
    ready(3)
    product_t_into(grad_attn, middle, w_out, D)
    allowed = column_facts[:, 0:1] == row_facts[0:1, :]
    allowed = jnp.concatenate([allowed.astype(FULL)] * 2, axis=0) > 0.5
    loop(
        D // LANES,
        lambda at: attend_back_into(
            grad_qkv, grad_attn, qkv_rows, pl.ds(0, ROWS), at, D, allowed, D // HEADS
        ),
    )
    emit(1, normed_a, grad_qkv)
    ready(4)
    product_t_into(upper, grad_qkv, w_qkv, D)
    norm_back(grad_rows, embedded, upper, grad_rows, vec(0), grad_of(0), grad_of(1), ROWS, ENC_CHUNK)
    branch[...] = grad_rows[...].astype(LOW)
    emit(0, vis_rows, branch)
    groups = D // LANES
    for index in range(6):
        for group in range(groups):
            piled[pl.ds(index * groups + group, 1), :] = vec_grads[
                pl.ds(index, 1), pl.ds(group * LANES, LANES)
            ]
    base, groups = 6 * groups, DD // LANES
    for index in range(7):
        for group in range(groups):
            piled[pl.ds(base + index * groups + group, 1), :] = decoder_vecs[
                pl.ds(index, 1), pl.ds(group * LANES, LANES)
            ]
    vec_stage[...] = piled[pl.ds(0, 64), :].astype(LOW)
    copy = pltpu.make_async_copy(vec_stage, flat_ref.at[pl.ds(entries[11][0], 64)], stage_sem.at[0])
    copy.start()
    copy.wait()


def encoder_backward(saved, grad_projected, weights, decoder_vec_grads, flat):
    hbm = pl.BlockSpec(memory_space=pl.ANY)
    vmem = pl.BlockSpec(memory_space=pltpu.VMEM)
    mats = [weights[entry] for entry in FETCHED[1:]]
    inputs = [*saved, grad_projected, weights["enc_vecs"], decoder_vec_grads, *mats, flat]
    low, full = (lambda *s: pltpu.VMEM(s, LOW)), (lambda *s: pltpu.VMEM(s, FULL))
    return pl.pallas_call(
        encoder_backward_kernel,
        out_shape=jax.ShapeDtypeStruct(flat.shape, LOW),
        in_specs=[vmem] * 16 + [hbm] * 6,
        out_specs=hbm,
        input_output_aliases={len(inputs) - 1: 0},
        scratch_shapes=[low(*mat.shape) for mat in mats]
        + [
            full(ROWS, D),
            full(ROWS, D),
            low(ROWS, D),
            low(ROWS, FF),
            low(ROWS, D),
            low(ROWS, D),
            low(ROWS, 3 * D),
            full(8, D),
            low(TILE, ROWS),
            full(TILE * FF // LANES, LANES),
            low(2, TILE * FF // LANES, LANES),
            low(64, LANES),
            pltpu.SemaphoreType.DMA((2,)),
            pltpu.SemaphoreType.DMA((5,)),
        ],
        compiler_params=pltpu.CompilerParams(vmem_limit_bytes=60 * 1024 * 1024),
        name="encoder_backward",
    )(*inputs)


IMAGES = 5
IMG_ROWS = 208
DEC_ROWS = IMAGES * IMG_ROWS


def decoder_kernel(
    part_ref,
    projected,
    row_facts,
    targets_ref,
    table_ref,
    vecs_ref,
    w_qkv_hbm,
    w_out_hbm,
    w_up_hbm,
    w_down_hbm,
    w_pix_hbm,
    flat_ref,
    grad_projected,
    vec_grads,
    loss_ref,
    w_qkv,
    w_out,
    w_up,
    w_down,
    w_pix,
    dec_in,
    low_rows,
    qkv_rows,
    attn_out,
    after_attn,
    normed_b,
    slope,
    hidden_act,
    decoded,
    final_dec,
    grad_pred,
    upper,
    masked,
    turned,
    piled,
    stage,
    stage_sem,
    sems,
    *,
    mask_total,
):
    ready = fetch(
        [
            (w_qkv_hbm, w_qkv),
            (w_out_hbm, w_out),
            (w_up_hbm, w_up),
            (w_down_hbm, w_down),
            (w_pix_hbm, w_pix),
        ],
        sems,
    )
    entries = matrix_entries()
    vec = lambda index: vecs_ref[index : index + 1, :]
    grad_of = lambda index: vec_grads.at[pl.ds(index, 1), :]
    part = part_ref[0]
    image_of = row_facts[0:1, :].astype(jnp.int32) - part * IMAGES
    patch_of = row_facts[1:2, :].astype(jnp.int32)
    patch = lax.broadcasted_iota(jnp.int32, (IMG_ROWS, ROWS), 0)

    def selector(index):
        return ((patch_of == patch) & (image_of == index)).astype(FULL)

    def place(index):
        at = span(index, IMG_ROWS)
        select = selector(index)
        real = (patch[:, 0:1] < PATCHES).astype(FULL)
        hidden = real * (1.0 - jnp.sum(select, axis=-1, keepdims=True))
        masked[at, :] = jnp.broadcast_to(hidden, (IMG_ROWS, LANES))
        dec_in[at, :] = dot_nn(select.astype(LOW), projected[...]) + hidden * vec(6) + table_ref[...]

    loop(IMAGES, place)
    norm_into(low_rows, dec_in, vec(0), vec(1), DEC_ROWS, IMG_ROWS)
    ready(0)
    product_into(qkv_rows, low_rows, w_qkv, 3 * DD)
    head_size = DD // DHEADS
    heads = LANES // head_size
    allowed = lax.broadcasted_iota(jnp.int32, (heads * IMG_ROWS, IMG_ROWS), 1) < PATCHES
    groups = DD // LANES

    def attend(step):
        rows = span(step // groups, IMG_ROWS)
        attend_into(attn_out, qkv_rows, rows, step % groups, DD, allowed, head_size)

    loop(IMAGES * groups, attend)
    ready(1)
    product_into(after_attn, attn_out, w_out, DD, residual=dec_in)
    norm_into(normed_b, after_attn, vec(2), vec(3), DEC_ROWS, IMG_ROWS)
    ready(2)
    up_into(hidden_act, slope, normed_b, w_up, DFF, TILE)
    ready(3)
    product_into(decoded, hidden_act, w_down, DD, residual=after_attn)
    norm_into(final_dec, decoded, vec(4), vec(5), DEC_ROWS, IMG_ROWS)
    ready(4)
    loss_ref[...] = jnp.zeros_like(loss_ref)

    def compare(index):
        at = span(index, IMG_ROWS)
        image = pl.ds(0, PATCHES)
        goal, _ = norm_parts(targets_ref[index].astype(FULL))
        goal = jnp.concatenate([goal, jnp.zeros((IMG_ROWS - PATCHES, PIX), FULL)], axis=0)
        error = dot_nn(final_dec[at, :], w_pix[...]) - goal
        weight = masked[at, 0:1]
        rows = jnp.mean(error * error, axis=-1, keepdims=True) * weight
        loss_ref[...] = loss_ref[...] + jnp.sum(rows) * (1.0 / mask_total)
        grad_pred[at, :] = (weight * error * (2.0 / (PIX * mask_total))).astype(LOW)

    loop(IMAGES, compare)

    def emit(entry, left, right):
        weight_grad(flat_ref, entries[entry][0], left, right, turned, piled, stage, stage_sem)

    emit(10, final_dec, grad_pred)
    product_t_into(upper, grad_pred, w_pix, DD)
    grad_rows, branch = decoded, final_dec
    norm_back(grad_rows, decoded, upper, None, vec(4), grad_of(4), grad_of(5), DEC_ROWS, IMG_ROWS)
    branch[...] = grad_rows[...].astype(LOW)
    emit(9, hidden_act, branch)
    grad_pre = hidden_act
    down_back_into(grad_pre, branch, w_down, slope, DFF, TILE)
    emit(8, normed_b, grad_pre)
    product_t_into(upper, grad_pre, w_up, DD)
    norm_back(grad_rows, after_attn, upper, grad_rows, vec(2), grad_of(2), grad_of(3), DEC_ROWS, IMG_ROWS)
    branch[...] = grad_rows[...].astype(LOW)
    emit(7, attn_out, branch)
    grad_attn, grad_qkv = normed_b, grad_pre.at[:, pl.ds(0, 3 * DD)]
    product_t_into(grad_attn, branch, w_out, DD)

    def attend_back(step):
        rows = span(step // groups, IMG_ROWS)
        attend_back_into(grad_qkv, grad_attn, qkv_rows, rows, step % groups, DD, allowed, head_size)

    loop(IMAGES * groups, attend_back)
    emit(6, low_rows, grad_qkv)
    product_t_into(upper, grad_qkv, w_qkv, DD)
    norm_back(grad_rows, dec_in, upper, grad_rows, vec(0), grad_of(0), grad_of(1), DEC_ROWS, IMG_ROWS)
    upper[pl.ds(0, ROWS), :] = jnp.zeros((ROWS, DD), FULL)

    def collect(index, token):
        at = span(index, IMG_ROWS)
        rows = grad_rows[at, :]
        token = token + jnp.sum((rows * masked[at, 0:1]).reshape(IMG_ROWS // 8, 8, DD), axis=0)
        upper[pl.ds(0, ROWS), :] = upper[pl.ds(0, ROWS), :] + dot_tn(
            selector(index).astype(LOW), rows.astype(LOW)
        )
        return token

    token = lax.fori_loop(0, IMAGES, collect, jnp.zeros((8, DD), FULL))
    grad_of(6)[...] = jnp.sum(token, axis=0, keepdims=True)
    grad_projected[...] = upper[pl.ds(0, ROWS), :].astype(LOW)


def decoder_step(part, projected, row_facts, targets, weights, mask_total, flat_rows):
    hbm = pl.BlockSpec(memory_space=pl.ANY)
    vmem = pl.BlockSpec(memory_space=pltpu.VMEM)
    smem = pl.BlockSpec(memory_space=pltpu.SMEM)
    table = jnp.asarray(position_table(DD, IMG_ROWS))
    mats = [weights[entry] for entry in ("dec_qkv", "dec_out", "dec_up", "dec_down", "pixel")]
    low, full = (lambda *s: pltpu.VMEM(s, LOW)), (lambda *s: pltpu.VMEM(s, FULL))
    return pl.pallas_call(
        partial(decoder_kernel, mask_total=mask_total),
        out_shape=[
            jax.ShapeDtypeStruct((flat_rows, LANES), LOW),
            jax.ShapeDtypeStruct((ROWS, DD), LOW),
            jax.ShapeDtypeStruct((8, DD), FULL),
            jax.ShapeDtypeStruct((1, LANES), FULL),
        ],
        in_specs=[smem] + [vmem] * 5 + [hbm] * 5,
        out_specs=[hbm] + [vmem] * 3,
        scratch_shapes=[low(*mat.shape) for mat in mats]
        + [
            full(DEC_ROWS, DD),
            low(DEC_ROWS, DD),
            low(DEC_ROWS, 3 * DD),
            low(DEC_ROWS, DD),
            full(DEC_ROWS, DD),
            low(DEC_ROWS, DD),
            full(DEC_ROWS, DFF),
            low(DEC_ROWS, DFF),
            full(DEC_ROWS, DD),
            low(DEC_ROWS, DD),
            low(DEC_ROWS, PIX),
            full(DEC_ROWS, DD),
            full(DEC_ROWS, LANES),
            low(TILE, DEC_ROWS),
            full(TILE * DFF // LANES, LANES),
            low(2, TILE * DFF // LANES, LANES),
            pltpu.SemaphoreType.DMA((2,)),
            pltpu.SemaphoreType.DMA((5,)),
        ],
        compiler_params=pltpu.CompilerParams(vmem_limit_bytes=62 * 1024 * 1024),
        name="decoder_step",
    )(part, projected, row_facts, targets, table, weights["dec_vecs"], *mats)


def shards(visible, segments, patch_ids, targets, master, moment_one, moment_two, step_count):
    part = lax.axis_index("seq")
    in_kernels = master.shape[0] == SHARD_ROWS * LANES and lax.axis_size("dp") == 16
    if in_kernels:
        gathered = gather_weights(master.reshape(SHARD_ROWS, LANES))
        weights = {entry[0]: array for entry, array in zip(layout(), gathered)}
    else:
        full_flat = lax.all_gather(master.astype(LOW), ("seq", "dp"), axis=0, tiled=True)
        weights = unflatten(full_flat)
        weights["enc_vecs"] = weights["enc_vecs"].astype(FULL)
        weights["dec_vecs"] = weights["dec_vecs"].astype(FULL)
    visible_rows = lax.all_gather(visible[0], "seq", axis=0, tiled=True)
    part_row = part.reshape(1).astype(jnp.int32)
    mask_total = (PATCHES - VIS) * IMG_SEQ * visible.shape[0] * lax.axis_size("dp")
    *saved, projected, row_facts, column_facts = encoder_forward(
        part_row, visible_rows, segments, patch_ids, weights
    )
    flat_rows = master.shape[0] * lax.axis_size("dp") * lax.axis_size("seq") // LANES
    flat, grad_projected, decoder_vec_grads, loss_row = decoder_step(
        part_row, projected, row_facts, targets[0], weights, mask_total, flat_rows
    )
    flat = encoder_backward(
        [*saved, row_facts, column_facts], grad_projected, weights, decoder_vec_grads, flat
    )
    if in_kernels:
        grad_shard, square_sum, loss_sum = reduce_gradients(flat, loss_row)
    else:
        grad_flat = flat.astype(FULL).reshape(-1)
        grad_shard = lax.psum_scatter(grad_flat, ("seq", "dp"), scatter_dimension=0, tiled=True)
        square_sum, loss_sum = lax.psum(
            (jnp.sum(grad_shard * grad_shard), loss_row[0, 0]), ("seq", "dp")
        )
    grad_norm = jnp.sqrt(square_sum)
    clipped = grad_shard * jnp.minimum(1.0, clip_limit / (grad_norm + 1e-06))
    new_one = beta_mom * moment_one + (1.0 - beta_mom) * clipped
    new_two = beta_mom * moment_two + (1.0 - beta_mom) * clipped * clipped
    correction = 1.0 - jnp.power(jnp.float32(beta_mom), step_count[0].astype(jnp.float32))
    new_master = master - learn_rate * (
        new_one / correction / (jnp.sqrt(new_two / correction) + adam_eps) + decay_rate * master
    )
    return (new_one, new_two, new_master, new_master.astype(jnp.bfloat16), grad_norm, loss_sum)


def solution(mesh):
    in_specs = (
        P("dp", "seq", None),
        P("dp", None),
        P("dp", None),
        P("dp", "seq", None, None),
        P(("seq", "dp")),
        P(("seq", "dp")),
        P(("seq", "dp")),
        P(),
    )
    out_specs = (P(("seq", "dp")), P(("seq", "dp")), P(("seq", "dp")), P(("seq", "dp")), P(), P())
    return jax.shard_map(shards, mesh=mesh, in_specs=in_specs, out_specs=out_specs, check_vma=False)
```

time: 2010 us -> 545 us (0.27)
  waiting for transfers between devices: 909 us -> 0 us
  other arithmetic: 556 us -> 6.25 us
  Pallas kernels: 0 us -> 531 us
  local copies, waits for them, and re-layouts: 280 us -> 1.2 us
  matrix products: 187 us -> 0 us
  blocking collectives: 47 us -> 2.66 us
    unnamed x6 -> x0, waiting for transfers between devices: 668 us -> none
    pallas_call x0 -> x5, Pallas kernels: none -> 531 us  [the longest x1 220 us: gather_weights(): pl.pallas_call(gather_kernel, out_shape=[jax.ShapeDtypeStruct(s, jnp.bflo...]
    all_gather x1 -> x0, other arithmetic: 490 us -> none  [shards(): lax.all_gather(master.astype(jnp.bfloat16), ('seq', 'dp'), axis=0, tiled=...]
    all_gather x1 -> x0, waiting for transfers between devices: 241 us -> none  [shards(): lax.all_gather(master.astype(jnp.bfloat16), ('seq', 'dp'), axis=0, tiled=...]
    dot_general x45 -> x0, matrix products: 187 us -> none  [the longest x2 34.5 us: block_forward(): hidden_pre = jnp.dot(normed_b, w_up, preferred_element_type=jnp.float32)]
    unnamed x345 -> x6, local copies, waits for them, and re-layouts: 129 us -> 0.02 us
    reshape x24 -> x0, local copies, waits for them, and re-layouts: 82.6 us -> none  [the longest x7 34.5 us: unflatten(): flat_vec[offset:offset + entry_size].reshape(entry_shape)]
    psum x1 -> x0, blocking collectives: 40 us -> none  [shards(): lax.psum((jnp.sum(grad_shard * grad_shard), loss_local), ('seq', 'dp'))]
  transfers between devices with their start and end apart: 5 -> 0, of which waited for: 2 -> 0; matrix products, arithmetic and copies ran while one was open for 4% -> 0% of each run, Pallas kernels for 0% -> 0%
where the time goes in v1:
time: 545 us; the launch traced here: 544 us
  Pallas kernels  531 us (97%)
  other arithmetic  6.25 us (1%)
    pallas_call x1, Pallas kernels, gather_weights(): pl.pallas_call(gather_kernel, out_shape=[jax.ShapeDtypeStruct(s, jnp.bflo...  220 us
    pallas_call x1, Pallas kernels, reduce_gradients(): pl.pallas_call(reduce_kernel, out_shape=[jax.ShapeDtypeStruct((PAD_ROWS,...  124 us
    pallas_call x1, Pallas kernels, decoder_step(): pl.pallas_call(partial(decoder_kernel, mask_total=mask_total), out_shape=...  108 us
    pallas_call x1, Pallas kernels, encoder_backward(): pl.pallas_call(encoder_backward_kernel, out_shape=jax.ShapeDtypeStruct(fl...  55.4 us
    pallas_call x1, Pallas kernels, encoder_forward(): pl.pallas_call(encoder_forward_kernel, out_shape=[low(ROWS, PIX), full(RO...  22.6 us

profile of v1, /device:TPU:0, one launch (start us, length us, event | category | flops | bytes accessed | tf_op | source)
XLA Modules:
  0.0 544.3 jit_solution(3140572220751332088)
XLA Ops:
  0.6 0.0 copy-start.2
  0.6 220.2 %gather_weights.1 = (bf16[768,768]{1,0:T(8,128)(2,1)}, bf16[768,2304]{1,0:T(8,128)(2,1)}, bf16[768,768]{1,0:T(8,128)(2,1)}, bf16[768,3072]{1,0:T(8,128)(2,1)}, b...) custom-call(f32[2834,128]{1,0:T(8,128)} %bitcast.11), custom_call_target="tpu_custom_call" | custom-call | tf_op jit(solution)/shard_map/gather_weights/pallas_call | solution.py:366
  220.9 0.0 copy-done.2
  220.9 2.7 all-gather
  223.5 22.6 %encoder_forward.1 = (bf16[256,768]{1,0:T(8,128)(2,1)}, f32[256,768]{1,0:T(8,128)}, bf16[256,768]{1,0:T(8,128)(2,1)}, bf16[256,2304]{1,0:T(8,128)(2,1)}, bf16[25...) custom-call(s32[1]{0:T(128)} %bitcast.part_ref, ...), custom_call_target="tpu_custom_call" | custom-call | tf_op jit(solution)/shard_map/encoder_forward/pallas_call | solution.py:1061
  246.2 108.2 %decoder_step.1 = (bf16[90688,128]{1,0:T(8,128)(2,1)}, bf16[256,512]{1,0:T(8,128)(2,1)}, f32[8,512]{1,0:T(8,128)}, f32[1,128]{1,0:T(1,128)}) custom-call(s32[1]{0:T(128)} %bitcast.part_ref, bf16[256,512]{1,0:T(8,128)(2,1)} %get-tuple-element.59.projected, f32[16,256]{1,0:T(8,128)} %get-tuple-element.57.row_facts, bf16[5,196,768]{2,1,0:T(8,128)(2,1)} %bitcast.13, ...), custom_call_target="tpu_custom_call" | custom-call | tf_op jit(solution)/shard_map/decoder_step/pallas_call | solution.py:1395
  354.4 55.4 %encoder_backward.1.grad_ref = bf16[90688,128]{1,0:T(8,128)(2,1)} custom-call(bf16[256,768]{1,0:T(8,128)(2,1)} %get-tuple-element.46.vis_rows, f32[256,768]{1,0:T(8,128)} %get-tuple-element.47.embedded, bf16[256,768]{1,0:T(8,128)(2,1)} %get-tuple-element.48.normed_a, bf16[256,2304]{1,0:T(8,128)(2,1)} %get-tuple-element.49.qkv_rows, ...), custom_call_target="tpu_custom_call", output_to_operand_aliasing={{}: (21, {})} | custom-call | tf_op jit(solution)/shard_map/encoder_backward/pallas_call | solution.py:1203
  409.8 0.0 copy-start
  409.8 0.0 copy-start.1
  409.8 124.4 %reduce_gradients.1 = (f32[2848,128]{1,0:T(8,128)}, f32[2,8,128]{2,1,0:T(8,128)}) custom-call(bf16[90688,128]{1,0:T(8,128)(2,1)} %encoder_backward.1.grad_ref, f32[1,128]{1,0:T(1,128)} %get-tuple-element.69.loss_ref), custom_call_target="tpu_custom_call" | custom-call | tf_op jit(solution)/shard_map/reduce_gradients/pallas_call | solution.py:677
  534.3 1.3 slice_reduce_fusion
  537.0 0.0 copy-done
  537.0 0.0 copy-done.1
  537.0 5.0 fusion.1
  542.0 1.2 slice.11
Async XLA Ops:
  0.6 220.2 %copy-start.2 = (bf16[1,256,768]{2,1,0:T(8,128)(2,1)S(1)}, bf16[1,256,768]{2,1,0:T(8,128)(2,1)}, u32[]{:S(2)}) copy-start(bf16[1,256,768]{2,1,0:T(8,128)(2,1)} %param.10) | copy-start | bytes 1179652
  409.8 127.2 %copy-start = (f32[362752]{0:T(1024)S(1)}, f32[362752]{0:T(1024)}, u32[]{:S(2)}) copy-start(f32[362752]{0:T(1024)} %param.14) | copy-start | bytes 4353028
  409.8 127.2 %copy-start.1 = (f32[362752]{0:T(1024)S(1)}, f32[362752]{0:T(1024)}, u32[]{:S(2)}) copy-start(f32[362752]{0:T(1024)} %param.16) | copy-start | bytes 4353028

commit v2 on v1

v2 whole, which is shorter than its diff:
```python
from functools import partial
import math

import jax
import jax.numpy as jnp
import ml_dtypes
import numpy as np
from jax import lax
from jax.experimental import pallas as pl
from jax.experimental.pallas import tpu as pltpu
from jax.sharding import PartitionSpec as P

D = 768
HEADS = 12
FF = 3072
DD = 512
DHEADS = 16
DFF = 2048
PIX = 768
PATCHES = 196
VIS = 49
IMG_SEQ = 10


norm_eps = 1e-06
neg_big = -1000000000.0
clip_limit = 0.0001
learn_rate = 0.03
decay_rate = 0.05
adam_eps = 1e-08
beta_mom = 0.5


def layout():
    return [
        ("embed", (PIX, D)),
        ("enc_qkv", (D, 3 * D)),
        ("enc_out", (D, D)),
        ("enc_up", (D, FF)),
        ("enc_down", (FF, D)),
        ("project", (D, DD)),
        ("dec_qkv", (DD, 3 * DD)),
        ("dec_out", (DD, DD)),
        ("dec_up", (DD, DFF)),
        ("dec_down", (DFF, DD)),
        ("pixel", (DD, PIX)),
        ("enc_vecs", (6, D)),
        ("dec_vecs", (7, DD)),
    ]


def unflatten(flat_vec):
    params = {}
    offset = 0
    for entry_name, entry_shape in layout():
        entry_size = entry_shape[0] * entry_shape[1]
        params[entry_name] = flat_vec[offset : offset + entry_size].reshape(entry_shape)
        offset += entry_size
    return params


LOW = jnp.bfloat16
FULL = jnp.float32
TILE = 256
TALL = 16
LANES = 128
NEG = neg_big
ROOT_HALF = math.sqrt(0.5)
BELL = 1.0 / math.sqrt(2.0 * math.pi)


def dot_nn(left, right):
    return lax.dot_general(left, right, (((1,), (0,)), ((), ())), preferred_element_type=FULL)


def dot_nt(left, right):
    return lax.dot_general(left, right, (((1,), (1,)), ((), ())), preferred_element_type=FULL)


def dot_tn(left, right):
    return lax.dot_general(left, right, (((0,), (0,)), ((), ())), preferred_element_type=FULL)


def loop(count, body):
    def one(step, carry):
        body(step)
        return carry

    lax.fori_loop(0, count, one, 0)


def span(step, size):
    return pl.ds(pl.multiple_of(step * size, size), size)


def norm_parts(rows):
    average = jnp.mean(rows, axis=-1, keepdims=True)
    centered = rows - average
    scale = lax.rsqrt(jnp.mean(centered * centered, axis=-1, keepdims=True) + norm_eps)
    return centered * scale, scale


def norm_into(dst, src, gain, shift, rows, chunk):
    def one(step):
        at = span(step, chunk)
        unit, _ = norm_parts(src[at, :])
        dst[at, :] = (unit * gain + shift).astype(LOW)

    loop(rows // chunk, one)


def norm_back(dst, src, grad, residual, gain, gain_grad, shift_grad, rows, chunk):
    width = src.shape[1]

    def one(step, carry):
        at = span(step, chunk)
        unit, scale = norm_parts(src[at, :])
        upper = grad[at, :]
        gains = carry[0] + jnp.sum((upper * unit).reshape(chunk // 8, 8, width), axis=0)
        shifts = carry[1] + jnp.sum(upper.reshape(chunk // 8, 8, width), axis=0)
        upper = upper * gain
        lower = scale * (
            upper
            - jnp.mean(upper, axis=-1, keepdims=True)
            - unit * jnp.mean(upper * unit, axis=-1, keepdims=True)
        )
        if residual is not None:
            lower = lower + residual[at, :]
        dst[at, :] = lower
        return gains, shifts

    zero = jnp.zeros((8, width), FULL)
    gains, shifts = lax.fori_loop(0, rows // chunk, one, (zero, zero))
    gain_grad[...] = jnp.sum(gains, axis=0, keepdims=True)
    shift_grad[...] = jnp.sum(shifts, axis=0, keepdims=True)


class Blocked:
    def __init__(self, ref, rows, columns):
        self.rows, self.groups = rows, columns // LANES
        self.ref = ref.reshape(rows // TALL, self.groups, TALL, LANES)

    def piece(self, first_row, rows, first_group, groups):
        tall = pl.ds(first_row // TALL, rows // TALL)
        parts = [
            self.ref[tall, first_group + index].reshape(rows, LANES) for index in range(groups)
        ]
        return parts[0] if groups == 1 else jnp.concatenate(parts, axis=1)

    def column_tile(self, step, tile):
        count = tile // LANES
        return self.piece(0, self.rows, step * count, count)

    def row_tile(self, step, tile):
        return self.piece(step * tile, tile, 0, self.groups)


def product_into(dst, left, right, columns, tile=TILE, residual=None):
    def one(step):
        at = span(step, tile)
        value = dot_nn(left[...], right.column_tile(step, tile))
        if residual is not None:
            value = value + residual[:, at]
        dst[:, at] = value.astype(dst.dtype)

    loop(columns // tile, one)


def product_t_into(dst, left, right, columns, tile=TILE):
    def one(step):
        dst[:, span(step, tile)] = dot_nt(left[...], right.row_tile(step, tile)).astype(dst.dtype)

    loop(columns // tile, one)


def up_into(act, slope, left, w_up, columns, tile):
    def one(step):
        at = span(step, tile)
        hidden = dot_nn(left[...], w_up.column_tile(step, tile))
        share = 0.5 * (1.0 + lax.erf(hidden * ROOT_HALF))
        act[:, at] = (hidden * share).astype(LOW)
        slope[:, at] = share + hidden * (BELL * jnp.exp(-0.5 * hidden * hidden))

    loop(columns // tile, one)


def down_back_into(grad_pre, branch, w_down, slope, columns, tile):
    def one(step):
        at = span(step, tile)
        grad_pre[:, at] = (dot_nt(branch[...], w_down.row_tile(step, tile)) * slope[:, at]).astype(LOW)

    loop(columns // tile, one)


def weight_grad(out, out_tile, left, right, turned, stage, stage_sem):
    rows, columns = left.shape[1], right.shape[1]
    groups = columns // LANES
    steps = rows // TILE
    high = TILE // TALL
    count = high * groups

    def copy(slot, step):
        return pltpu.make_async_copy(
            stage.at[slot, pl.ds(0, count)],
            out.at[pl.ds(out_tile + step * count, count)],
            stage_sem.at[slot],
        )

    def one(step):
        slot = step % 2
        turned[...] = left[:, span(step, TILE)].T

        @pl.when(step >= 2)
        def _():
            copy(slot, step - 2).wait()

        tiles = stage.at[slot, pl.ds(0, count)].reshape(high, groups, TALL, LANES)

        def across(tile):
            value = dot_nn(turned[...], right[:, span(tile, TILE)]).astype(LOW)
            for half in range(2):
                tiles[:, tile * 2 + half] = value[:, half * LANES : (half + 1) * LANES].reshape(
                    high, TALL, LANES
                )

        loop(columns // TILE, across)
        copy(slot, step).start()

    loop(steps, one)
    for step in range(max(steps - 2, 0), steps):
        copy(step % 2, step).wait()


def head_masks(head_size, dtype):
    lane = lax.broadcasted_iota(jnp.int32, (1, LANES), 1) // head_size
    return [(lane == head).astype(dtype) for head in range(LANES // head_size)]


def stacked(rows, masks):
    return jnp.concatenate([rows * mask for mask in masks], axis=0)


def unstacked(rows, masks, size):
    total = None
    for index, mask in enumerate(masks):
        piece = rows[index * size : (index + 1) * size] * mask
        total = piece if total is None else total + piece
    return total


def soft_rows(queries, keys, allowed, scale):
    scores = jnp.where(allowed, dot_nt(queries, keys) * scale, NEG)
    scores = scores - jnp.max(scores, axis=-1, keepdims=True)
    powers = jnp.exp(scores)
    return powers / jnp.sum(powers, axis=-1, keepdims=True)


def attend_into(dst, qkv, rows, at, width, allowed, head_size):
    masks = head_masks(head_size, LOW)
    size = rows.size
    column = lambda part: pl.ds(pl.multiple_of(part * width + at * LANES, LANES), LANES)
    queries = stacked(qkv[rows, column(0)], masks)
    probs = soft_rows(queries, qkv[rows, column(1)], allowed, head_size**-0.5).astype(LOW)
    values = dot_nn(probs, qkv[rows, column(2)])
    dst[rows, column(0)] = unstacked(values, head_masks(head_size, FULL), size).astype(LOW)


def attend_back_into(dst, grad, qkv, rows, at, width, allowed, head_size):
    masks = head_masks(head_size, LOW)
    lanes = head_masks(head_size, FULL)
    size = rows.size
    scale = head_size**-0.5
    column = lambda part: pl.ds(pl.multiple_of(part * width + at * LANES, LANES), LANES)
    queries = stacked(qkv[rows, column(0)], masks)
    keys = qkv[rows, column(1)]
    probs = soft_rows(queries, keys, allowed, scale)
    grads = stacked(grad[rows, column(0)], masks)
    slopes = dot_nt(grads, qkv[rows, column(2)])
    slopes = probs * (slopes - jnp.sum(slopes * probs, axis=-1, keepdims=True))
    slopes = slopes.astype(LOW)
    dst[rows, column(0)] = (unstacked(dot_nn(slopes, keys), lanes, size) * scale).astype(LOW)
    dst[rows, column(1)] = (dot_tn(slopes, queries) * scale).astype(LOW)
    dst[rows, column(2)] = dot_tn(probs.astype(LOW), grads).astype(LOW)


def entry_tiles():
    tiles, offset = {}, 0
    for entry_name, (rows, columns) in layout():
        tiles[entry_name] = (offset // (TALL * LANES), rows, columns)
        offset += rows * columns
    tiles["vecs"] = (tiles["enc_vecs"][0], 4 * TALL, LANES)
    return tiles


def vec_reader(buffer, first, groups):
    rows = buffer[...].reshape(4 * TALL, LANES).astype(FULL)

    def vec(index):
        start = first + index * groups
        return jnp.concatenate([rows[start + g : start + g + 1] for g in range(groups)], axis=1)

    return vec


def fetch(flat, names, buffers, sems):
    tiles = entry_tiles()

    def build(index):
        start, rows, columns = tiles[names[index]]
        count = rows * columns // (TALL * LANES)
        return pltpu.make_async_copy(flat.at[pl.ds(start, count)], buffers[index], sems.at[index])

    for index in range(len(names)):
        build(index).start()

    def ready(index):
        build(index).wait()
        _, rows, columns = tiles[names[index]]
        return Blocked(buffers[index], rows, columns)

    return ready


def tile_buffers(names):
    tiles = entry_tiles()
    return [
        pltpu.VMEM((tiles[entry][1] * tiles[entry][2] // (TALL * LANES), TALL, LANES), LOW)
        for entry in names
    ]


def position_table(columns, padded):
    half = columns // 2
    frequency = np.exp(
        np.float32(-math.log(10000.0)) * np.arange(half, dtype=np.float32) / np.float32(half)
    ).astype(np.float32)
    angles = np.arange(PATCHES, dtype=np.float32)[:, None] * frequency
    table = np.zeros((padded, columns), np.float32)
    table[:PATCHES] = np.concatenate(
        [np.sin(angles.astype(np.float64)), np.cos(angles.astype(np.float64))], axis=-1
    )
    return table


def split_low(table):
    parts, rest = [], table.astype(np.float64)
    for _ in range(3):
        part = rest.astype(ml_dtypes.bfloat16)
        parts.append(part)
        rest = rest - part.astype(np.float64)
    return np.stack(parts)


MESH = pl.DeviceIdType.MESH
A_HALF = 1104
A_ROWS = 2 * A_HALF
B_HALF = 320
B_ROWS = 2 * B_HALF
SHARD_ROWS = 2834
PAD_ROWS = A_ROWS + B_ROWS
B_TRUE = SHARD_ROWS - A_ROWS
HALO = 384
WIDE_ROWS = SHARD_ROWS + 2 * HALO
PARTS = {
    "a1": (0, A_HALF),
    "a2": (A_HALF, A_HALF),
    "b": (A_ROWS, B_ROWS),
    "b1": (A_ROWS, B_HALF),
    "b2": (A_ROWS + B_HALF, B_HALF),
}
TRUE_PARTS = {**PARTS, "b": (A_ROWS, B_TRUE), "b2": (A_ROWS + B_HALF, B_TRUE - B_HALF)}
SLOTS = {"a1": 0, "a2": 1, "b": 2, "b1": 2, "b2": 3}
COLUMNS = "oxyd"
ARRIVALS = {
    0: (
        12, 22, 102, 10, 20, 100, 11, 21, 101, 33, 34, 112, 122, 30, 110, 202, 120, 31, 200, 121,
        111, 201, 132, 130, 210, 212, 220, 131, 222, 302, 221, 211, 300, 230, 231, 301, 320, 310,
        232, 312, 321, 311, 322, 332, 330, 331,
    ),
    1: (
        2, 112, 122, 202, 0, 110, 120, 200, 1, 111, 121, 201, 133, 134, 12, 212, 22, 222, 20, 10,
        32, 302, 130, 210, 300, 220, 11, 301, 232, 21, 131, 312, 221, 211, 322, 332, 30, 310,
        230, 311, 320, 31, 321, 231, 330, 331,
    ),
}


def item_of(code):
    return code // 100, COLUMNS[code // 10 % 10], list(PARTS)[code % 10]


def own_item(inner, part):
    return 100 * inner + list(PARTS).index(part)


class Place:
    def __init__(self):
        self.core = lax.axis_index("seq")
        self.chip = lax.axis_index("dp")
        chip = self.chip
        self.z = chip // 4
        y, x = (chip // 2) % 2, chip % 2
        self.col = chip % 4
        self.col_x = self.col + 1 - 2 * x
        self.col_y = self.col + 2 - 4 * y
        self.col_d = self.col_x + 2 - 4 * y
        self.columns = {"o": self.col, "x": self.col_x, "y": self.col_y, "d": self.col_d}
        self.side = self.z // 2
        sign = 1 - 2 * self.side
        self.inner = self.z + self.side * (3 - 2 * self.z)
        self.me = 16 * self.core + chip
        self.devices = {
            "x": (self.core, 4 * self.z + self.col_x),
            "y": (self.core, 4 * self.z + self.col_y),
            "far": (self.core, chip + 4 * sign),
            "near": (self.core, chip - 4 * sign * self.inner),
            "core": (1 - self.core, chip),
            "next": self.ring(1),
            "back": self.ring(31),
        }

    def ring(self, step):
        peer = (self.me + step) % 32
        return (peer // 16, peer % 16)

    def plane(self, mirrored):
        return mirrored + self.side * (3 - 2 * mirrored)

    def greet(self):
        barrier = pltpu.get_barrier_semaphore()
        for link in ("x", "y", "far", "core", "next", "back"):
            pl.semaphore_signal(
                barrier, inc=1, device_id=self.devices[link], device_id_type=MESH
            )

        @pl.when(self.inner == 1)
        def _():
            pl.semaphore_signal(
                barrier, inc=1, device_id=self.devices["near"], device_id_type=MESH
            )

        pl.semaphore_wait(barrier, 6 + self.inner)


class Outbox:
    def __init__(self):
        self.sent = []

    def send(self, src, dst, send_sem, recv_sem, device):
        def build():
            return pltpu.make_async_remote_copy(
                src_ref=src,
                dst_ref=dst,
                send_sem=send_sem,
                recv_sem=recv_sem,
                device_id=device,
                device_id_type=MESH,
            )

        build().start()
        self.sent.append(build)

    def finish(self):
        for build in self.sent:
            build().wait_send()


def arrived(ref, sem, device):
    pltpu.make_async_remote_copy(
        src_ref=ref, dst_ref=ref, send_sem=sem, recv_sem=sem, device_id=device, device_id_type=MESH
    ).wait_recv()


def by_place(at, body):
    for inner in (0, 1):
        pl.when(at.inner == inner)(partial(body, inner))


def onward(inner, item):
    mirrored, column, part = item_of(item)
    line = ["far", "near"][: 1 + inner]
    if mirrored != inner:
        line = [] if inner == 0 else ["far" if mirrored == 0 else "near"]
    if part[0] == "a":
        if column == "o":
            return [(link, part) for link in [*line, "x", "y"]]
        if (column, part) in (("x", "a1"), ("y", "a2")):
            return [("y" if column == "x" else "x", part)]
        return []
    links = [(link, "b") for link in line]
    if mirrored == inner:
        links = {
            "o": [("x", "b"), ("y", "b")],
            "x": [("y", "b1")],
            "y": [("x", "b2")],
            "d": [],
        }[column] + links
    return links


def gather_exchange(at, flat, source, recv, core_recv, sends, core_send):
    def block(chip, part, core):
        first, size = TRUE_PARTS[part]
        return flat.at[pl.ds((core * 16 + chip) * SHARD_ROWS + first, size)]

    def body(inner):
        out = Outbox()
        diagonal = []

        def pass_on(item):
            mirrored, column, part = item_of(item)
            chip = 4 * at.plane(mirrored) + at.columns[column]
            own = mirrored == inner and column == "o"
            links = onward(inner, item)
            if mirrored == inner and column == "d" and part[0] == "b":
                diagonal.append(part)
                links = links if len(diagonal) == 2 else []
            for link, piece in [*links, ("core", part)]:
                slot = SLOTS[piece]
                ref = block(chip, piece, at.core)
                sent, got = (core_send, core_recv) if link == "core" else (sends[link], recv)
                out.send(
                    source(piece) if own else ref,
                    ref,
                    sent.at[chip, slot],
                    got.at[chip, slot],
                    at.devices[link],
                )

        for part in ("b", "a1", "a2"):
            pass_on(own_item(inner, part))
        for item in ARRIVALS[inner]:
            mirrored, column, part = item_of(item)
            chip = 4 * at.plane(mirrored) + at.columns[column]
            arrived(block(chip, part, at.core), recv.at[chip, SLOTS[part]], at.devices["x"])
            pass_on(item)
        for part in ("b", "a1", "a2"):
            arrived(
                block(at.chip, part, 1 - at.core),
                core_recv.at[at.chip, SLOTS[part]],
                at.devices["x"],
            )
        for item in ARRIVALS[inner]:
            mirrored, column, part = item_of(item)
            chip = 4 * at.plane(mirrored) + at.columns[column]
            ref = block(chip, part, 1 - at.core)
            arrived(ref, core_recv.at[chip, SLOTS[part]], at.devices["x"])
        out.finish()

    by_place(at, body)


def entry_blocks(me, body):
    first = me * SHARD_ROWS
    offset = 0
    for _, (rows, columns) in layout()[:11]:
        groups, blocks = columns // LANES, rows // TALL
        unit = TALL * groups
        low = jnp.minimum(jnp.maximum(first - offset, 0) // unit, blocks)
        high = jnp.minimum(
            (jnp.maximum(first + SHARD_ROWS - offset, 0) + unit - 1) // unit, blocks
        )

        def one(block, carry, offset=offset, unit=unit, groups=groups):
            body(offset + block * unit, groups)
            return carry

        lax.fori_loop(low, high, one, 0)
        offset += unit * blocks
    return offset


VEC_ROWS = 64


def gather_kernel(master_ref, flat_ref, wide, turned, own_sem, halo_send, halo_recv, *sems):
    recv, core_recv, send_x, send_y, send_far, send_near, core_send = sems
    at = Place()
    first = at.me * SHARD_ROWS
    skew = (at.me * 2) % TALL
    own = pltpu.make_async_copy(master_ref, wide.at[pl.ds(HALO, SHARD_ROWS)], own_sem.at[0])
    own.start()
    at.greet()
    out = Outbox()
    tail = wide.at[pl.ds(HALO + SHARD_ROWS, HALO)]
    head = wide.at[pl.ds(0, HALO)]
    out.send(
        master_ref.at[pl.ds(0, HALO)],
        tail,
        halo_send.at[0],
        halo_recv.at[0],
        at.devices["back"],
    )
    out.send(
        master_ref.at[pl.ds(SHARD_ROWS - HALO, HALO)],
        head,
        halo_send.at[1],
        halo_recv.at[1],
        at.devices["next"],
    )
    own.wait()
    arrived(tail, halo_recv.at[0], at.devices["x"])
    arrived(head, halo_recv.at[1], at.devices["x"])

    def turn(row, groups):
        start = row - first + HALO
        spot = row - (first - skew) + HALO
        for group in range(groups):
            turned[pl.ds(pl.multiple_of(spot + group * TALL, TALL), TALL), :] = wide[
                pl.ds(start + group, TALL, stride=groups), :
            ].astype(LOW)

    vec_start = entry_blocks(at.me, turn)

    @pl.when(at.me == 31)
    def _():
        start = vec_start - 31 * SHARD_ROWS + HALO
        spot = start + (31 * 2) % TALL
        turned[pl.ds(spot, VEC_ROWS), :] = wide[pl.ds(start, VEC_ROWS), :].astype(LOW)

    mine = pltpu.make_async_copy(
        turned.at[pl.ds(HALO + skew, SHARD_ROWS)],
        flat_ref.at[pl.ds(first, SHARD_ROWS)],
        own_sem.at[1],
    )
    mine.start()

    def source(part):
        start, size = TRUE_PARTS[part]
        return turned.at[pl.ds(HALO + skew + start, size)]

    sends = {"x": send_x, "y": send_y, "far": send_far, "near": send_near}
    gather_exchange(at, flat_ref, source, recv, core_recv, sends, core_send)
    mine.wait()
    out.finish()


def gather_weights(master_rows):
    hbm = pl.BlockSpec(memory_space=pl.ANY)
    pairs = pltpu.SemaphoreType.DMA((2,))
    return pl.pallas_call(
        gather_kernel,
        out_shape=jax.ShapeDtypeStruct((32 * SHARD_ROWS, LANES), LOW),
        in_specs=[hbm],
        out_specs=hbm,
        scratch_shapes=[
            pltpu.VMEM((WIDE_ROWS + 6, LANES), FULL),
            pltpu.VMEM((WIDE_ROWS + 30, LANES), LOW),
            pairs,
            pairs,
            pairs,
        ]
        + [pltpu.SemaphoreType.DMA((16, 4))] * 7,
        compiler_params=pltpu.CompilerParams(
            collective_id=0, has_side_effects=True, vmem_limit_bytes=16 * 1024 * 1024
        ),
        name="gather_weights",
    )(master_rows)


def add_into(dst, start, terms, size, chunk):
    def one(step):
        row = step * chunk
        total = None
        for ref, first in terms:
            piece = ref[pl.ds(pl.multiple_of(first + row, TALL), chunk), :].astype(FULL)
            total = piece if total is None else total + piece
        dst[pl.ds(pl.multiple_of(start + row, TALL), chunk), :] = total.astype(dst.dtype)

    loop(size // chunk, one)


def reduce_kernel(
    grad_ref,
    loss_ref,
    shard_ref,
    total_ref,
    own,
    theirs,
    from_x,
    from_y,
    pass_x,
    pass_y,
    far_a,
    near_a,
    far_b,
    near_b,
    wide,
    plain,
    scalars,
    load_sem,
    core_send,
    core_recv,
    send_x,
    send_y,
    send_far,
    send_near,
    recv_x,
    recv_y,
    recv_far,
    recv_near,
    halo_send,
    halo_recv,
    tiny_send,
    tiny_recv,
):
    at = Place()
    tail = pl.ds(SHARD_ROWS - 2, TALL)
    for index in range(16):
        own[index, tail, :] = jnp.zeros((TALL, LANES), LOW)
        theirs[index, tail, :] = jnp.zeros((TALL, LANES), LOW)
    body = pl.ds(0, SHARD_ROWS)

    def shard_rows(core, chip):
        return grad_ref.at[pl.ds((core * 16 + chip) * SHARD_ROWS, SHARD_ROWS)]

    def load(chip):
        return pltpu.make_async_copy(
            shard_rows(at.core, chip), own.at[chip, body], load_sem.at[chip]
        )

    at.greet()
    pairs = Outbox()
    for mirrored in (3, 2, 1 - at.inner, at.inner):
        for column in ("d", "y", "x", "o"):
            chip = 4 * at.plane(mirrored) + at.columns[column]
            pairs.send(
                shard_rows(1 - at.core, chip),
                theirs.at[chip, body],
                core_send.at[chip],
                core_recv.at[chip],
                at.devices["core"],
            )
            load(chip).start()
    sends = {"x": send_x, "y": send_y, "far": send_far, "near": send_near}
    recvs = {"x": recv_x, "y": recv_y, "far": recv_far, "near": recv_near}
    relayed = {"x": pass_x, "y": pass_y}
    direct = {"x": from_x, "y": from_y}
    lines = {"far": (far_a, far_b), "near": (near_a, near_b)}

    def reduce_parts(inner):
        out = Outbox()
        paired, joined = set(), set()

        def pair(chip, key):
            if key in paired:
                return
            paired.add(key)
            load(chip).wait()
            arrived(theirs.at[chip, body], core_recv.at[chip], at.devices["x"])
            add_into(own.at[chip], 0, [(own.at[chip], 0), (theirs.at[chip], 0)], PAD_ROWS, 32)

        def landing(link, plane, chip, part, relay):
            first, size = PARTS[part]
            if link in lines and part == "b":
                return lines[link][1].at[chip], 0, size, (chip, SLOTS[part])
            if link in lines:
                return lines[link][0].at[plane], first, size, (chip, SLOTS[part])
            if relay:
                return relayed[link].at[plane], first, size, (plane, 3 + (part[0] == "b"))
            return direct[link].at[plane], first, size, (plane, SLOTS[part])

        def step(item):
            mirrored, column, part = item_of(item)
            plane = at.plane(mirrored)
            chip = 4 * plane + at.columns[column]
            pair(chip, (mirrored, column))
            first, size = PARTS[part]
            terms = []
            links = onward(inner, item)
            if mirrored == inner and column == "d" and part[0] == "b":
                links = [] if joined else links
                joined.add(part)
            own_item = mirrored == inner and column == "o"
            for link, piece in links:
                relay = column in ("x", "y")
                buffer, start, count, index = landing(link, plane, chip, piece, relay)
                arrived(buffer.at[pl.ds(start, count)], recvs[link].at[*index], at.devices["x"])
                terms.append((buffer, start, count))
            if own_item:
                whole = [(own.at[chip], first)] + [(buffer, start) for buffer, start, _ in terms]
                if part == "b":
                    add_into(plain, 0, whole, size, size // 4)
                    wide[pl.ds(HALO + A_ROWS, B_TRUE), :] = plain[pl.ds(0, B_TRUE), :]
                else:
                    add_into(wide, HALO + first, whole, size, size // 3)
                return
            full_size = B_ROWS if part[0] == "b" else size
            full_first = PARTS["b"][0] if part[0] == "b" else first
            whole = [(buffer, start) for buffer, start, count in terms if count == full_size]
            halves = [(buffer, start, count) for buffer, start, count in terms if count != full_size]
            if whole:
                add_into(
                    own.at[chip],
                    full_first,
                    [(own.at[chip], full_first), *whole],
                    full_size,
                    full_size // (4 if part[0] == "b" else 3),
                )
            for buffer, start, count in halves:
                add_into(
                    own.at[chip], start, [(own.at[chip], start), (buffer, start)], count, count // 2
                )
            if column == "o" or (part == "b" and mirrored != inner):
                link = "near" if inner == 1 and mirrored == 0 else "far"
                target = "near" if inner == 0 else "far"
                buffer, start, _, index = landing(target, plane, chip, part, False)
                arrive_sem = recvs[target]
            else:
                link = {"x": "x", "y": "y", "d": "y" if part in ("a1", "b1") else "x"}[column]
                buffer, start, _, index = landing(link, plane, chip, part, column == "d")
                arrive_sem = recvs[link]
            out.send(
                own.at[chip, pl.ds(first, size)],
                buffer.at[pl.ds(start, size)],
                sends[link].at[*index],
                arrive_sem.at[*index],
                at.devices[link],
            )

        for item in reversed(ARRIVALS[inner]):
            step(item)
        for part in ("a2", "a1", "b"):
            step(own_item(inner, part))
        out.finish()

    by_place(at, reduce_parts)
    pairs.finish()

    halo = Outbox()
    head, after = wide.at[pl.ds(0, HALO)], wide.at[pl.ds(HALO + SHARD_ROWS, HALO)]
    halo.send(
        wide.at[pl.ds(HALO, HALO)], after, halo_send.at[0], halo_recv.at[0], at.devices["back"]
    )
    halo.send(
        wide.at[pl.ds(SHARD_ROWS, HALO)], head, halo_send.at[1], halo_recv.at[1], at.devices["next"]
    )
    whole_steps = SHARD_ROWS // 32

    def squares(index, carry):
        piece = wide[pl.ds(pl.multiple_of(HALO + index * 32, 8), 32), :]
        piece = piece * piece
        return carry + jnp.sum(piece.reshape(4, 8, LANES), axis=0)

    square = lax.fori_loop(0, whole_steps, squares, jnp.zeros((8, LANES), FULL))
    rest = wide[pl.ds(HALO + whole_steps * 32, SHARD_ROWS - whole_steps * 32), :]
    square = square + 0.125 * jnp.sum(rest * rest, axis=0, keepdims=True)
    scalars[at.me, 0] = square
    scalars[at.me, 1] = jnp.broadcast_to(loss_ref[...], (8, LANES))
    for index in range(1, 32):
        halo.send(
            scalars.at[at.me],
            scalars.at[at.me],
            tiny_send.at[index],
            tiny_recv.at[at.me],
            at.ring(index),
        )
    arrived(after, halo_recv.at[0], at.devices["x"])
    arrived(head, halo_recv.at[1], at.devices["x"])

    def turn_back(row, groups):
        start = row - at.me * SHARD_ROWS + HALO
        for group in range(groups):
            plain[pl.ds(start + group, TALL, stride=groups), :] = wide[
                pl.ds(start + group * TALL, TALL), :
            ]

    vec_start = entry_blocks(at.me, turn_back)

    @pl.when(at.me == 31)
    def _():
        spot = pl.ds(vec_start - 31 * SHARD_ROWS + HALO, VEC_ROWS)
        plain[spot, :] = wide[spot, :]

    shard_ref[...] = plain[pl.ds(HALO, SHARD_ROWS), :]
    for index in range(1, 32):
        peer = (at.me + index) % 32
        arrived(scalars.at[peer], tiny_recv.at[peer], at.devices["x"])
    total_ref[...] = jnp.sum(scalars[...], axis=0)
    halo.finish()


def reduce_gradients(grad_rows, loss_row):
    hbm = pl.BlockSpec(memory_space=pl.ANY)
    vmem = pl.BlockSpec(memory_space=pltpu.VMEM)
    dma = pltpu.SemaphoreType.DMA
    shard_total, totals = pl.pallas_call(
        reduce_kernel,
        out_shape=[
            jax.ShapeDtypeStruct((SHARD_ROWS, LANES), FULL),
            jax.ShapeDtypeStruct((2, 8, LANES), FULL),
        ],
        in_specs=[hbm, vmem],
        out_specs=[vmem, vmem],
        scratch_shapes=[pltpu.VMEM((16, PAD_ROWS, LANES), LOW)] * 2
        + [pltpu.VMEM((4, PAD_ROWS, LANES), LOW)] * 4
        + [pltpu.VMEM((4, A_ROWS, LANES), LOW)] * 2
        + [pltpu.VMEM((16, B_ROWS, LANES), LOW)] * 2
        + [pltpu.VMEM((WIDE_ROWS + 6, LANES), FULL)] * 2
        + [pltpu.VMEM((32, 2, 8, LANES), FULL)]
        + [dma((16,))] * 3
        + [dma((4, 5))] * 2
        + [dma((16, 4))] * 2
        + [dma((4, 5))] * 2
        + [dma((16, 4))] * 2
        + [dma((2,))] * 2
        + [dma((32,))] * 2,
        compiler_params=pltpu.CompilerParams(
            collective_id=1, has_side_effects=True, vmem_limit_bytes=56 * 1024 * 1024
        ),
        name="reduce_gradients",
    )(grad_rows, loss_row)
    return shard_total.reshape(-1), jnp.sum(totals[0]), totals[1, 0, 0]


ROWS = 256
ENC_CHUNK = 64
FETCHED = ("vecs", "embed", "enc_qkv", "enc_out", "enc_up", "enc_down", "project")
BACKWARD_FETCHED = ("vecs", "project", "enc_down", "enc_up", "enc_out", "enc_qkv")


def encoder_forward_kernel(
    part_ref,
    visible_ref,
    segments_ref,
    patches_ref,
    table_ref,
    flat_ref,
    vis_rows,
    embedded,
    normed_a,
    qkv_rows,
    attn_out,
    after_attn,
    normed_b,
    slope,
    hidden_act,
    encoded,
    final_enc,
    projected,
    row_facts,
    column_facts,
    sems,
    *buffers,
):
    ready = fetch(flat_ref, FETCHED, buffers, sems)
    part = part_ref[0]
    total = segments_ref.shape[1]
    images = IMG_SEQ // 2
    spare = ROWS - images * VIS
    segments = segments_ref[...]
    image = segments - part * images
    inside = (image >= 0) & (image < images)
    padding = segments == IMG_SEQ
    flags = jnp.concatenate(
        [
            inside.astype(FULL),
            padding.astype(FULL),
            jnp.zeros((6, total), FULL),
        ],
        axis=0,
    ).astype(LOW)
    row = lax.broadcasted_iota(jnp.int32, (total, total), 0)
    column = lax.broadcasted_iota(jnp.int32, (total, total), 1)
    counts = dot_nn(flags, (row <= column).astype(FULL).astype(LOW)).astype(jnp.int32)
    inside_count, padding_count = counts[0:1], counts[1:2]
    padding_slot = padding_count - part * spare
    chosen = inside | (padding & (padding_slot >= 1) & (padding_slot <= spare))
    slot = inside_count + jnp.clip(padding_slot, 0, spare) - 1
    slot = jnp.where(chosen, slot, -1)
    select = (lax.broadcasted_iota(jnp.int32, (ROWS, total), 0) == slot).astype(FULL).astype(LOW)
    facts = jnp.concatenate(
        [segments.astype(FULL), patches_ref[...].astype(FULL), jnp.zeros((LANES - 2, total), FULL)],
        axis=0,
    ).astype(LOW)
    row_facts[...] = dot_nt(facts[0:16], select)
    column_facts[...] = dot_nt(select, facts)
    vis_rows[...] = dot_nn(select, visible_ref[...]).astype(LOW)
    patch = column_facts[:, 1:2].astype(jnp.int32)
    spot = (lax.broadcasted_iota(jnp.int32, (ROWS, table_ref.shape[1]), 1) == patch).astype(FULL).astype(LOW)
    embedded[...] = dot_nn(spot, table_ref[0]) + dot_nn(spot, table_ref[1]) + dot_nn(spot, table_ref[2])
    w_embed = ready(1)
    product_into(embedded, vis_rows, w_embed, D, residual=embedded)
    ready(0)
    vec = vec_reader(buffers[0], 0, D // LANES)
    norm_into(normed_a, embedded, vec(0), vec(1), ROWS, ENC_CHUNK)
    w_qkv = ready(2)
    product_into(qkv_rows, normed_a, w_qkv, 3 * D)
    allowed = column_facts[:, 0:1] == row_facts[0:1, :]
    allowed = jnp.concatenate([allowed.astype(FULL)] * 2, axis=0) > 0.5
    loop(
        D // LANES,
        lambda at: attend_into(attn_out, qkv_rows, pl.ds(0, ROWS), at, D, allowed, D // HEADS),
    )
    w_out = ready(3)
    product_into(after_attn, attn_out, w_out, D, residual=embedded)
    norm_into(normed_b, after_attn, vec(2), vec(3), ROWS, ENC_CHUNK)
    w_up = ready(4)
    up_into(hidden_act, slope, normed_b, w_up, FF, 512)
    w_down = ready(5)
    product_into(encoded, hidden_act, w_down, D, residual=after_attn)
    norm_into(final_enc, encoded, vec(4), vec(5), ROWS, ENC_CHUNK)
    w_proj = ready(6)
    product_into(projected, final_enc, w_proj, DD)


def encoder_forward(part, visible_rows, segments, patch_ids, flat_weights):
    hbm = pl.BlockSpec(memory_space=pl.ANY)
    vmem = pl.BlockSpec(memory_space=pltpu.VMEM)
    smem = pl.BlockSpec(memory_space=pltpu.SMEM)
    table = jnp.asarray(split_low(position_table(D, 256)))
    low, full = (lambda *s: jax.ShapeDtypeStruct(s, LOW)), (lambda *s: jax.ShapeDtypeStruct(s, FULL))
    return pl.pallas_call(
        encoder_forward_kernel,
        out_shape=[
            low(ROWS, PIX),
            full(ROWS, D),
            low(ROWS, D),
            low(ROWS, 3 * D),
            low(ROWS, D),
            full(ROWS, D),
            low(ROWS, D),
            full(ROWS, FF),
            low(ROWS, FF),
            full(ROWS, D),
            low(ROWS, D),
            low(ROWS, DD),
            full(16, ROWS),
            full(ROWS, LANES),
        ],
        in_specs=[smem] + [vmem] * 4 + [hbm],
        out_specs=[vmem] * 14,
        scratch_shapes=[pltpu.SemaphoreType.DMA((7,))] + tile_buffers(FETCHED),
        compiler_params=pltpu.CompilerParams(vmem_limit_bytes=56 * 1024 * 1024),
        name="encoder_forward",
    )(part, visible_rows, segments, patch_ids, table, flat_weights)


def encoder_backward_kernel(
    vis_rows,
    embedded,
    normed_a,
    qkv_rows,
    attn_out,
    after_attn,
    normed_b,
    slope,
    hidden_act,
    encoded,
    final_enc,
    row_facts,
    column_facts,
    grad_projected,
    decoder_vecs,
    weights_ref,
    partial_ref,
    flat_ref,
    grad_rows,
    upper,
    branch,
    grad_pre,
    middle,
    grad_attn,
    grad_qkv,
    vec_grads,
    turned,
    stage,
    vec_full,
    vec_stage,
    stage_sem,
    sems,
    *buffers,
):
    del partial_ref
    ready = fetch(weights_ref, BACKWARD_FETCHED, buffers, sems)
    tiles = entry_tiles()
    ready(0)
    vec = vec_reader(buffers[0], 0, D // LANES)
    grad_of = lambda index: vec_grads.at[pl.ds(index, 1), :]

    def emit(entry, left, right):
        weight_grad(flat_ref, tiles[entry][0], left, right, turned, stage, stage_sem)

    emit("project", final_enc, grad_projected)
    w_proj = ready(1)
    product_t_into(upper, grad_projected, w_proj, D)
    norm_back(grad_rows, encoded, upper, None, vec(4), grad_of(4), grad_of(5), ROWS, ENC_CHUNK)
    branch[...] = grad_rows[...].astype(LOW)
    emit("enc_down", hidden_act, branch)
    w_down = ready(2)
    down_back_into(grad_pre, branch, w_down, slope, FF, 512)
    emit("enc_up", normed_b, grad_pre)
    w_up = ready(3)
    product_t_into(upper, grad_pre, w_up, D)
    norm_back(grad_rows, after_attn, upper, grad_rows, vec(2), grad_of(2), grad_of(3), ROWS, ENC_CHUNK)
    middle[...] = grad_rows[...].astype(LOW)
    emit("enc_out", attn_out, middle)
    w_out = ready(4)
    product_t_into(grad_attn, middle, w_out, D)
    allowed = column_facts[:, 0:1] == row_facts[0:1, :]
    allowed = jnp.concatenate([allowed.astype(FULL)] * 2, axis=0) > 0.5
    loop(
        D // LANES,
        lambda at: attend_back_into(
            grad_qkv, grad_attn, qkv_rows, pl.ds(0, ROWS), at, D, allowed, D // HEADS
        ),
    )
    emit("enc_qkv", normed_a, grad_qkv)
    w_qkv = ready(5)
    product_t_into(upper, grad_qkv, w_qkv, D)
    norm_back(grad_rows, embedded, upper, grad_rows, vec(0), grad_of(0), grad_of(1), ROWS, ENC_CHUNK)
    branch[...] = grad_rows[...].astype(LOW)
    emit("embed", vis_rows, branch)
    groups = D // LANES
    for index in range(6):
        for group in range(groups):
            vec_full[pl.ds(index * groups + group, 1), :] = vec_grads[
                pl.ds(index, 1), pl.ds(group * LANES, LANES)
            ]
    base, groups = 6 * groups, DD // LANES
    for index in range(7):
        for group in range(groups):
            vec_full[pl.ds(base + index * groups + group, 1), :] = decoder_vecs[
                pl.ds(index, 1), pl.ds(group * LANES, LANES)
            ]
    vec_stage[...] = vec_full[...].astype(LOW).reshape(4, TALL, LANES)
    copy = pltpu.make_async_copy(vec_stage, flat_ref.at[pl.ds(tiles["enc_vecs"][0], 4)], stage_sem.at[0])
    copy.start()
    copy.wait()


def encoder_backward(saved, grad_projected, flat_weights, decoder_vec_grads, flat):
    hbm = pl.BlockSpec(memory_space=pl.ANY)
    vmem = pl.BlockSpec(memory_space=pltpu.VMEM)
    inputs = [*saved, grad_projected, decoder_vec_grads, flat_weights, flat]
    low, full = (lambda *s: pltpu.VMEM(s, LOW)), (lambda *s: pltpu.VMEM(s, FULL))
    return pl.pallas_call(
        encoder_backward_kernel,
        out_shape=jax.ShapeDtypeStruct(flat.shape, LOW),
        in_specs=[vmem] * 15 + [hbm] * 2,
        out_specs=hbm,
        input_output_aliases={len(inputs) - 1: 0},
        scratch_shapes=[
            full(ROWS, D),
            full(ROWS, D),
            low(ROWS, D),
            low(ROWS, FF),
            low(ROWS, D),
            low(ROWS, D),
            low(ROWS, 3 * D),
            full(8, D),
            low(TILE, ROWS),
            low(2, TILE // TALL * FF // LANES, TALL, LANES),
            full(64, LANES),
            low(4, TALL, LANES),
            pltpu.SemaphoreType.DMA((2,)),
            pltpu.SemaphoreType.DMA((6,)),
        ]
        + tile_buffers(BACKWARD_FETCHED),
        compiler_params=pltpu.CompilerParams(vmem_limit_bytes=60 * 1024 * 1024),
        name="encoder_backward",
    )(*inputs)


IMAGES = 5
DECODER_FETCHED = ("vecs", "dec_qkv", "dec_out", "dec_up", "dec_down", "pixel")
IMG_ROWS = 208
DEC_ROWS = IMAGES * IMG_ROWS


def decoder_kernel(
    part_ref,
    projected,
    row_facts,
    targets_ref,
    table_ref,
    weights_ref,
    flat_ref,
    grad_projected,
    vec_grads,
    loss_ref,
    dec_in,
    low_rows,
    qkv_rows,
    attn_out,
    after_attn,
    normed_b,
    slope,
    hidden_act,
    decoded,
    final_dec,
    grad_pred,
    upper,
    masked,
    turned,
    stage,
    stage_sem,
    sems,
    *buffers,
    mask_total,
):
    ready = fetch(weights_ref, DECODER_FETCHED, buffers, sems)
    tiles = entry_tiles()
    ready(0)
    vec = vec_reader(buffers[0], 6 * D // LANES, DD // LANES)
    grad_of = lambda index: vec_grads.at[pl.ds(index, 1), :]
    part = part_ref[0]
    image_of = row_facts[0:1, :].astype(jnp.int32) - part * IMAGES
    patch_of = row_facts[1:2, :].astype(jnp.int32)
    patch = lax.broadcasted_iota(jnp.int32, (IMG_ROWS, ROWS), 0)

    def selector(index):
        return ((patch_of == patch) & (image_of == index)).astype(FULL)

    def place(index):
        at = span(index, IMG_ROWS)
        select = selector(index)
        real = (patch[:, 0:1] < PATCHES).astype(FULL)
        hidden = real * (1.0 - jnp.sum(select, axis=-1, keepdims=True))
        masked[at, :] = jnp.broadcast_to(hidden, (IMG_ROWS, LANES))
        dec_in[at, :] = dot_nn(select.astype(LOW), projected[...]) + hidden * vec(6) + table_ref[...]

    loop(IMAGES, place)
    norm_into(low_rows, dec_in, vec(0), vec(1), DEC_ROWS, IMG_ROWS)
    w_qkv = ready(1)
    product_into(qkv_rows, low_rows, w_qkv, 3 * DD)
    head_size = DD // DHEADS
    heads = LANES // head_size
    allowed = lax.broadcasted_iota(jnp.int32, (heads * IMG_ROWS, IMG_ROWS), 1) < PATCHES
    groups = DD // LANES

    def attend(step):
        rows = span(step // groups, IMG_ROWS)
        attend_into(attn_out, qkv_rows, rows, step % groups, DD, allowed, head_size)

    loop(IMAGES * groups, attend)
    w_out = ready(2)
    product_into(after_attn, attn_out, w_out, DD, residual=dec_in)
    norm_into(normed_b, after_attn, vec(2), vec(3), DEC_ROWS, IMG_ROWS)
    w_up = ready(3)
    up_into(hidden_act, slope, normed_b, w_up, DFF, TILE)
    w_down = ready(4)
    product_into(decoded, hidden_act, w_down, DD, residual=after_attn)
    norm_into(final_dec, decoded, vec(4), vec(5), DEC_ROWS, IMG_ROWS)
    w_pix = ready(5)
    loss_ref[...] = jnp.zeros_like(loss_ref)

    def compare(index):
        at = span(index, IMG_ROWS)
        image = pl.ds(0, PATCHES)
        goal, _ = norm_parts(targets_ref[index].astype(FULL))
        goal = jnp.concatenate([goal, jnp.zeros((IMG_ROWS - PATCHES, PIX), FULL)], axis=0)
        error = dot_nn(final_dec[at, :], w_pix.column_tile(0, PIX)) - goal
        weight = masked[at, 0:1]
        rows = jnp.mean(error * error, axis=-1, keepdims=True) * weight
        loss_ref[...] = loss_ref[...] + jnp.sum(rows) * (1.0 / mask_total)
        grad_pred[at, :] = (weight * error * (2.0 / (PIX * mask_total))).astype(LOW)

    loop(IMAGES, compare)

    def emit(entry, left, right):
        weight_grad(flat_ref, tiles[entry][0], left, right, turned, stage, stage_sem)

    emit("pixel", final_dec, grad_pred)
    product_t_into(upper, grad_pred, w_pix, DD)
    grad_rows, branch = decoded, final_dec
    norm_back(grad_rows, decoded, upper, None, vec(4), grad_of(4), grad_of(5), DEC_ROWS, IMG_ROWS)
    branch[...] = grad_rows[...].astype(LOW)
    emit("dec_down", hidden_act, branch)
    grad_pre = hidden_act
    down_back_into(grad_pre, branch, w_down, slope, DFF, TILE)
    emit("dec_up", normed_b, grad_pre)
    product_t_into(upper, grad_pre, w_up, DD)
    norm_back(grad_rows, after_attn, upper, grad_rows, vec(2), grad_of(2), grad_of(3), DEC_ROWS, IMG_ROWS)
    branch[...] = grad_rows[...].astype(LOW)
    emit("dec_out", attn_out, branch)
    grad_attn, grad_qkv = normed_b, grad_pre.at[:, pl.ds(0, 3 * DD)]
    product_t_into(grad_attn, branch, w_out, DD)

    def attend_back(step):
        rows = span(step // groups, IMG_ROWS)
        attend_back_into(grad_qkv, grad_attn, qkv_rows, rows, step % groups, DD, allowed, head_size)

    loop(IMAGES * groups, attend_back)
    emit("dec_qkv", low_rows, grad_qkv)
    product_t_into(upper, grad_qkv, w_qkv, DD)
    norm_back(grad_rows, dec_in, upper, grad_rows, vec(0), grad_of(0), grad_of(1), DEC_ROWS, IMG_ROWS)
    upper[pl.ds(0, ROWS), :] = jnp.zeros((ROWS, DD), FULL)

    def collect(index, token):
        at = span(index, IMG_ROWS)
        rows = grad_rows[at, :]
        token = token + jnp.sum((rows * masked[at, 0:1]).reshape(IMG_ROWS // 8, 8, DD), axis=0)
        upper[pl.ds(0, ROWS), :] = upper[pl.ds(0, ROWS), :] + dot_tn(
            selector(index).astype(LOW), rows.astype(LOW)
        )
        return token

    token = lax.fori_loop(0, IMAGES, collect, jnp.zeros((8, DD), FULL))
    grad_of(6)[...] = jnp.sum(token, axis=0, keepdims=True)
    grad_projected[...] = upper[pl.ds(0, ROWS), :].astype(LOW)


def decoder_step(part, projected, row_facts, targets, flat_weights, mask_total):
    hbm = pl.BlockSpec(memory_space=pl.ANY)
    vmem = pl.BlockSpec(memory_space=pltpu.VMEM)
    smem = pl.BlockSpec(memory_space=pltpu.SMEM)
    table = jnp.asarray(position_table(DD, IMG_ROWS))
    low, full = (lambda *s: pltpu.VMEM(s, LOW)), (lambda *s: pltpu.VMEM(s, FULL))
    return pl.pallas_call(
        partial(decoder_kernel, mask_total=mask_total),
        out_shape=[
            jax.ShapeDtypeStruct(flat_weights.shape, LOW),
            jax.ShapeDtypeStruct((ROWS, DD), LOW),
            jax.ShapeDtypeStruct((8, DD), FULL),
            jax.ShapeDtypeStruct((1, LANES), FULL),
        ],
        in_specs=[smem] + [vmem] * 4 + [hbm],
        out_specs=[hbm] + [vmem] * 3,
        scratch_shapes=[
            full(DEC_ROWS, DD),
            low(DEC_ROWS, DD),
            low(DEC_ROWS, 3 * DD),
            low(DEC_ROWS, DD),
            full(DEC_ROWS, DD),
            low(DEC_ROWS, DD),
            full(DEC_ROWS, DFF),
            low(DEC_ROWS, DFF),
            full(DEC_ROWS, DD),
            low(DEC_ROWS, DD),
            low(DEC_ROWS, PIX),
            full(DEC_ROWS, DD),
            full(DEC_ROWS, LANES),
            low(TILE, DEC_ROWS),
            low(2, TILE // TALL * DFF // LANES, TALL, LANES),
            pltpu.SemaphoreType.DMA((2,)),
            pltpu.SemaphoreType.DMA((6,)),
        ]
        + tile_buffers(DECODER_FETCHED),
        compiler_params=pltpu.CompilerParams(vmem_limit_bytes=62 * 1024 * 1024),
        name="decoder_step",
    )(part, projected, row_facts, targets, table, flat_weights)


def to_tiles(full_flat):
    pieces, offset = [], 0
    for _, (rows, columns) in layout()[:11]:
        piece = full_flat[offset : offset + rows * columns]
        piece = piece.reshape(rows // TALL, TALL, columns // LANES, LANES)
        pieces.append(piece.transpose(0, 2, 1, 3).reshape(-1, LANES))
        offset += rows * columns
    return jnp.concatenate([*pieces, full_flat[offset:].reshape(-1, LANES)])


def from_tiles(rows_flat):
    pieces, offset = [], 0
    for _, (rows, columns) in layout()[:11]:
        count = rows * columns // LANES
        piece = rows_flat[offset : offset + count]
        piece = piece.reshape(rows // TALL, columns // LANES, TALL, LANES)
        pieces.append(piece.transpose(0, 2, 1, 3).reshape(-1))
        offset += count
    return jnp.concatenate([*pieces, rows_flat[offset:].reshape(-1)])


def shards(visible, segments, patch_ids, targets, master, moment_one, moment_two, step_count):
    part = lax.axis_index("seq")
    in_kernels = master.shape[0] == SHARD_ROWS * LANES and lax.axis_size("dp") == 16
    if in_kernels:
        flat_weights = gather_weights(master.reshape(SHARD_ROWS, LANES))
    else:
        full_flat = lax.all_gather(master.astype(LOW), ("seq", "dp"), axis=0, tiled=True)
        flat_weights = to_tiles(full_flat)
    flat_weights = flat_weights.reshape(-1, TALL, LANES)
    visible_rows = lax.all_gather(visible[0], "seq", axis=0, tiled=True)
    part_row = part.reshape(1).astype(jnp.int32)
    mask_total = (PATCHES - VIS) * IMG_SEQ * visible.shape[0] * lax.axis_size("dp")
    *saved, projected, row_facts, column_facts = encoder_forward(
        part_row, visible_rows, segments, patch_ids, flat_weights
    )
    flat_grads, grad_projected, decoder_vec_grads, loss_row = decoder_step(
        part_row, projected, row_facts, targets[0], flat_weights, mask_total
    )
    flat_grads = encoder_backward(
        [*saved, row_facts, column_facts],
        grad_projected,
        flat_weights,
        decoder_vec_grads,
        flat_grads,
    )
    flat_grads = flat_grads.reshape(-1, LANES)
    if in_kernels:
        grad_shard, square_sum, loss_sum = reduce_gradients(flat_grads, loss_row)
    else:
        grad_flat = from_tiles(flat_grads.astype(FULL))
        grad_shard = lax.psum_scatter(grad_flat, ("seq", "dp"), scatter_dimension=0, tiled=True)
        square_sum, loss_sum = lax.psum(
            (jnp.sum(grad_shard * grad_shard), loss_row[0, 0]), ("seq", "dp")
        )
    grad_norm = jnp.sqrt(square_sum)
    clipped = grad_shard * jnp.minimum(1.0, clip_limit / (grad_norm + 1e-06))
    new_one = beta_mom * moment_one + (1.0 - beta_mom) * clipped
    new_two = beta_mom * moment_two + (1.0 - beta_mom) * clipped * clipped
    correction = 1.0 - jnp.power(jnp.float32(beta_mom), step_count[0].astype(jnp.float32))
    new_master = master - learn_rate * (
        new_one / correction / (jnp.sqrt(new_two / correction) + adam_eps) + decay_rate * master
    )
    return (new_one, new_two, new_master, new_master.astype(jnp.bfloat16), grad_norm, loss_sum)


def solution(mesh):
    in_specs = (
        P("dp", "seq", None),
        P("dp", None),
        P("dp", None),
        P("dp", "seq", None, None),
        P(("seq", "dp")),
        P(("seq", "dp")),
        P(("seq", "dp")),
        P(),
    )
    out_specs = (P(("seq", "dp")), P(("seq", "dp")), P(("seq", "dp")), P(("seq", "dp")), P(), P())
    return jax.shard_map(shards, mesh=mesh, in_specs=in_specs, out_specs=out_specs, check_vma=False)
```

time: 545 us -> 414 us (0.76)
  Pallas kernels: 531 us -> 391 us
  local copies, waits for them, and re-layouts: 1.2 us -> 10.3 us
    pallas_call x2, Pallas kernels: 345 us -> 208 us  [the longest x1 107 us: reduce_gradients(): pl.pallas_call(reduce_kernel, out_shape=[jax.ShapeDtypeStruct((SHARD_ROWS...]
    unnamed x6 -> x10, local copies, waits for them, and re-layouts: 0.02 us -> 9.07 us
where the time goes in v2:
time: 414 us; the launch traced here: 413 us
  Pallas kernels  391 us (94%)
  local copies, waits for them, and re-layouts  10.3 us (2%)
  other arithmetic  6.25 us (2%)
    pallas_call x1, Pallas kernels, decoder_step(): pl.pallas_call(partial(decoder_kernel, mask_total=mask_total), out_shape=...  107 us
    pallas_call x1, Pallas kernels, reduce_gradients(): pl.pallas_call(reduce_kernel, out_shape=[jax.ShapeDtypeStruct((SHARD_ROWS...  107 us
    pallas_call x1, Pallas kernels, gather_weights(): pl.pallas_call(gather_kernel, out_shape=jax.ShapeDtypeStruct((32 * SHARD_...  101 us
    pallas_call x1, Pallas kernels, encoder_backward(): pl.pallas_call(encoder_backward_kernel, out_shape=jax.ShapeDtypeStruct(fl...  53.7 us
    pallas_call x1, Pallas kernels, encoder_forward(): pl.pallas_call(encoder_forward_kernel, out_shape=[low(ROWS, PIX), full(RO...  22.5 us
    unnamed x10, local copies, waits for them, and re-layouts  9.07 us

profile of v2, /device:TPU:0, one launch (start us, length us, event | category | flops | bytes accessed | tf_op | source)
XLA Modules:
  0.0 413.3 jit_solution(9753023050900730028)
XLA Ops:
  0.6 0.0 copy-start.1
  0.6 1.4 copy-done.1
  2.0 0.0 copy-start.4
  2.0 101.0 %gather_weights.1 = bf16[90688,128]{1,0:T(8,128)(2,1)S(1)} custom-call(f32[2834,128]{1,0:T(8,128)S(1)} %bitcast.16), custom_call_target="tpu_custom_call" | custom-call | tf_op jit(solution)/shard_map/gather_weights/pallas_call | solution.py:641
  103.0 0.0 copy-start
  103.0 7.7 %copy-done = bf16[90688,128]{1,0:T(8,128)(2,1)} copy-done((bf16[90688,128]{1,0:T(8,128)(2,1)}, bf16[90688,128]{1,0:T(8,128)(2,1)S(1)}, u32[]{:S(2)}) %copy-start) | copy-done | bytes 23216152
  110.7 0.0 copy-done.4
  110.7 2.6 all-gather
  113.3 22.5 %encoder_forward.1 = (bf16[256,768]{1,0:T(8,128)(2,1)}, f32[256,768]{1,0:T(8,128)}, bf16[256,768]{1,0:T(8,128)(2,1)}, bf16[256,2304]{1,0:T(8,128)(2,1)}, bf16[25...) custom-call(s32[1]{0:T(128)} %bitcast.part_ref, ...), custom_call_target="tpu_custom_call" | custom-call | tf_op jit(solution)/shard_map/encoder_forward/pallas_call | solution.py:1013
  135.8 107.0 %decoder_step.1 = (bf16[5668,16,128]{2,1,0:T(8,128)(2,1)}, bf16[256,512]{1,0:T(8,128)(2,1)}, f32[8,512]{1,0:T(8,128)}, f32[1,128]{1,0:T(1,128)}) custom-call(s32[1]{0:T(128)} %bitcast.part_ref, bf16[256,512]{1,0:T(8,128)(2,1)} %get-tuple-element.39.projected, f32[16,256]{1,0:T(8,128)} %get-tuple-element.37.row_facts, bf16[5,196,768]{2,1,0:T(8,128)(2,1)} %bitcast.19, ...), custom_call_target="tpu_custom_call" | custom-call | tf_op jit(solution)/shard_map/decoder_step/pallas_call | solution.py:1310
  242.8 53.7 %encoder_backward.1 = bf16[5668,16,128]{2,1,0:T(8,128)(2,1)} custom-call(bf16[256,768]{1,0:T(8,128)(2,1)} %get-tuple-element.26.vis_rows, f32[256,768]{1,0:T(8,128)} %get-tuple-element.27.embedded, bf16[256,768]{1,0:T(8,128)(2,1)} %get-tuple-element.28.normed_a, bf16[256,2304]{1,0:T(8,128)(2,1)} %get-tuple-element.29.qkv_rows, ...), custom_call_target="tpu_custom_call", output_to_operand_aliasing={{}: (16, {})} | custom-call | tf_op jit(solution)/shard_map/encoder_backward/pallas_call | solution.py:1137
  296.5 0.0 copy-start.2
  296.6 0.0 copy-start.3
  296.6 106.7 %reduce_gradients.1 = (f32[2834,128]{1,0:T(8,128)}, f32[2,8,128]{2,1,0:T(8,128)}) custom-call(bf16[90688,128]{1,0:T(8,128)(2,1)} %bitcast.17, f32[1,128]{1,0:T(1,128)} %get-tuple-element.43.loss_ref), custom_call_target="tpu_custom_call" | custom-call | tf_op jit(solution)/shard_map/reduce_gradients/pallas_call | solution.py:887
  403.3 1.3 slice_reduce_fusion
  406.0 0.0 copy-done.2
  406.0 0.0 copy-done.3
  406.0 5.0 %fusion.1 = (bf16[362752]{0:T(1024)(128)(2,1)}, f32[362752]{0:T(1024)}, f32[362752]{0:T(1024)}, f32[362752]{0:T(1024)}) fusion(f32[362752]{0:T(1024)S(1)} %copy-done.2, f32[]{:T(128)} %bitcast.7, f32[2834,128]{1,0:T(8,128)} %get-tuple-element.44, f32[]{:T(128)S(6)} %min.3, f32[362752]{0:T(1024)S(1)} %copy-done.3, f32[362752]{0:T(1024)} %param.15), kind=kLoop, calls=%fused_computation.5 | loop fusion | flops 5804032 | bytes 10882568 | tf_op jit(solution)/shard_map/convert_element_type | solution.py:1408
  411.0 1.2 slice.7
Async XLA Ops:
  0.6 1.4 copy-start.1
  2.0 108.7 %copy-start.4 = (bf16[1,256,768]{2,1,0:T(8,128)(2,1)S(1)}, bf16[1,256,768]{2,1,0:T(8,128)(2,1)}, u32[]{:S(2)}) copy-start(bf16[1,256,768]{2,1,0:T(8,128)(2,1)} %param.10) | copy-start | bytes 1179652
  103.0 7.7 %copy-start = (bf16[90688,128]{1,0:T(8,128)(2,1)}, bf16[90688,128]{1,0:T(8,128)(2,1)S(1)}, u32[]{:S(2)}) copy-start(bf16[90688,128]{1,0:T(8,128)(2,1)S(1)} %gather_weights.1) | copy-start | bytes 69648384
  296.5 109.4 %copy-start.2 = (f32[362752]{0:T(1024)S(1)}, f32[362752]{0:T(1024)}, u32[]{:S(2)}) copy-start(f32[362752]{0:T(1024)} %param.14) | copy-start | bytes 4353028
  296.6 109.4 %copy-start.3 = (f32[362752]{0:T(1024)S(1)}, f32[362752]{0:T(1024)}, u32[]{:S(2)}) copy-start(f32[362752]{0:T(1024)} %param.16) | copy-start | bytes 4353028

commit v3 on v2

--- a/solution.py
+++ b/solution.py
@@ -66,6 +66,7 @@
 LANES = 128
 NEG = neg_big
 ROOT_HALF = math.sqrt(0.5)
+LOG2_E = 1.0 / math.log(2.0)
 BELL = 1.0 / math.sqrt(2.0 * math.pi)
 
 
@@ -87,6 +88,16 @@
         return carry
 
     lax.fori_loop(0, count, one, 0)
+
+
+def unrolled(count, body):
+    size = next(size for size in (3, 2, 1) if count % size == 0)
+
+    def one(step):
+        for part in range(size):
+            body(step * size + part)
+
+    loop(count // size, one)
 
 
 def span(step, size):
@@ -163,14 +174,14 @@
             value = value + residual[:, at]
         dst[:, at] = value.astype(dst.dtype)
 
-    loop(columns // tile, one)
+    unrolled(columns // tile, one)
 
 
 def product_t_into(dst, left, right, columns, tile=TILE):
     def one(step):
         dst[:, span(step, tile)] = dot_nt(left[...], right.row_tile(step, tile)).astype(dst.dtype)
 
-    loop(columns // tile, one)
+    unrolled(columns // tile, one)
 
 
 def up_into(act, slope, left, w_up, columns, tile):
@@ -181,7 +192,7 @@
         act[:, at] = (hidden * share).astype(LOW)
         slope[:, at] = share + hidden * (BELL * jnp.exp(-0.5 * hidden * hidden))
 
-    loop(columns // tile, one)
+    unrolled(columns // tile, one)
 
 
 def down_back_into(grad_pre, branch, w_down, slope, columns, tile):
@@ -189,46 +200,57 @@
         at = span(step, tile)
         grad_pre[:, at] = (dot_nt(branch[...], w_down.row_tile(step, tile)) * slope[:, at]).astype(LOW)
 
-    loop(columns // tile, one)
-
-
-def weight_grad(out, out_tile, left, right, turned, stage, stage_sem):
+    unrolled(columns // tile, one)
+
+
+def weight_grad(out, out_tile, left, right, turned, stage, stage_sem, slot=0, before=None):
     rows, columns = left.shape[1], right.shape[1]
     groups = columns // LANES
-    steps = rows // TILE
-    high = TILE // TALL
+    high = rows // TALL
     count = high * groups
 
-    def copy(slot, step):
-        return pltpu.make_async_copy(
-            stage.at[slot, pl.ds(0, count)],
-            out.at[pl.ds(out_tile + step * count, count)],
-            stage_sem.at[slot],
-        )
-
-    def one(step):
-        slot = step % 2
-        turned[...] = left[:, span(step, TILE)].T
-
-        @pl.when(step >= 2)
-        def _():
-            copy(slot, step - 2).wait()
-
-        tiles = stage.at[slot, pl.ds(0, count)].reshape(high, groups, TALL, LANES)
-
-        def across(tile):
-            value = dot_nn(turned[...], right[:, span(tile, TILE)]).astype(LOW)
+    def turn(step):
+        turned[span(step, TILE), :] = left[:, span(step, TILE)].T
+
+    loop(rows // TILE, turn)
+    if before is not None:
+        before()
+    tiles = stage.at[slot, pl.ds(0, count)].reshape(high, groups, TALL, LANES)
+    piece = columns // TILE
+    unroll = next(u for u in (3, 2, 1) if piece % u == 0)
+
+    def across(step):
+        for part in range(unroll):
+            tile = step * unroll + part
+            value = dot_nn(turned[pl.ds(0, rows), :], right[:, span(tile, TILE)]).astype(LOW)
             for half in range(2):
                 tiles[:, tile * 2 + half] = value[:, half * LANES : (half + 1) * LANES].reshape(
                     high, TALL, LANES
                 )
 
-        loop(columns // TILE, across)
-        copy(slot, step).start()
-
-    loop(steps, one)
-    for step in range(max(steps - 2, 0), steps):
-        copy(step % 2, step).wait()
+    loop(piece // unroll, across)
+    copy = lambda: pltpu.make_async_copy(
+        stage.at[slot, pl.ds(0, count)], out.at[pl.ds(out_tile, count)], stage_sem.at[slot]
+    )
+    copy().start()
+    return lambda: copy().wait()
+
+
+class Emitter:
+    def __init__(self, out, turned, stage, stage_sem):
+        self.args = turned, stage, stage_sem
+        self.out, self.tiles, self.waits = out, entry_tiles(), []
+
+    def __call__(self, entry, left, right):
+        index = len(self.waits)
+        before = self.waits[index - 2] if index >= 2 else None
+        self.waits.append(
+            weight_grad(self.out, self.tiles[entry][0], left, right, *self.args, index % 2, before)
+        )
+
+    def finish(self):
+        for wait in self.waits[-2:]:
+            wait()
 
 
 def head_masks(head_size, dtype):
@@ -249,10 +271,10 @@
 
 
 def soft_rows(queries, keys, allowed, scale):
-    scores = jnp.where(allowed, dot_nt(queries, keys) * scale, NEG)
+    scores = jnp.where(allowed, dot_nt(queries, keys), NEG)
     scores = scores - jnp.max(scores, axis=-1, keepdims=True)
-    powers = jnp.exp(scores)
-    return powers / jnp.sum(powers, axis=-1, keepdims=True)
+    powers = jnp.exp2(scores * (scale * LOG2_E))
+    return powers * (1.0 / jnp.sum(powers, axis=-1, keepdims=True))
 
 
 def attend_into(dst, qkv, rows, at, width, allowed, head_size):
@@ -573,7 +595,9 @@
 VEC_ROWS = 64
 
 
-def gather_kernel(master_ref, flat_ref, wide, turned, own_sem, halo_send, halo_recv, *sems):
+def gather_kernel(
+    master_ref, visible_ref, flat_ref, both_ref, wide, turned, own_sem, halo_send, halo_recv, *sems
+):
     recv, core_recv, send_x, send_y, send_far, send_near, core_send = sems
     at = Place()
     first = at.me * SHARD_ROWS
@@ -598,6 +622,12 @@
         halo_recv.at[1],
         at.devices["next"],
     )
+    half = visible_ref.shape[0]
+    rows_here = both_ref.at[pl.ds(pl.multiple_of(at.core * half, half), half)]
+    rows_there = both_ref.at[pl.ds(pl.multiple_of((1 - at.core) * half, half), half)]
+    out.send(visible_ref, rows_here, halo_send.at[2], halo_recv.at[2], at.devices["core"])
+    keep = pltpu.make_async_copy(visible_ref, rows_here, own_sem.at[2])
+    keep.start()
     own.wait()
     arrived(tail, halo_recv.at[0], at.devices["x"])
     arrived(head, halo_recv.at[1], at.devices["x"])
@@ -632,30 +662,36 @@
     sends = {"x": send_x, "y": send_y, "far": send_far, "near": send_near}
     gather_exchange(at, flat_ref, source, recv, core_recv, sends, core_send)
     mine.wait()
+    keep.wait()
+    arrived(rows_there, halo_recv.at[2], at.devices["x"])
     out.finish()
 
 
-def gather_weights(master_rows):
-    hbm = pl.BlockSpec(memory_space=pl.ANY)
-    pairs = pltpu.SemaphoreType.DMA((2,))
+def gather_weights(master_rows, visible_rows):
+    hbm = pl.BlockSpec(memory_space=pltpu.HBM)
+    threes = pltpu.SemaphoreType.DMA((3,))
+    half, width = visible_rows.shape
     return pl.pallas_call(
         gather_kernel,
-        out_shape=jax.ShapeDtypeStruct((32 * SHARD_ROWS, LANES), LOW),
-        in_specs=[hbm],
-        out_specs=hbm,
+        out_shape=[
+            jax.ShapeDtypeStruct((32 * SHARD_ROWS, LANES), LOW),
+            jax.ShapeDtypeStruct((2 * half, width), LOW),
+        ],
+        in_specs=[hbm, hbm],
+        out_specs=[hbm, hbm],
         scratch_shapes=[
             pltpu.VMEM((WIDE_ROWS + 6, LANES), FULL),
             pltpu.VMEM((WIDE_ROWS + 30, LANES), LOW),
-            pairs,
-            pairs,
-            pairs,
+            threes,
+            threes,
+            threes,
         ]
         + [pltpu.SemaphoreType.DMA((16, 4))] * 7,
         compiler_params=pltpu.CompilerParams(
-            collective_id=0, has_side_effects=True, vmem_limit_bytes=16 * 1024 * 1024
+            collective_id=0, has_side_effects=True, vmem_limit_bytes=60 * 1024 * 1024
         ),
         name="gather_weights",
-    )(master_rows)
+    )(master_rows, visible_rows)
 
 
 def add_into(dst, start, terms, size, chunk):
@@ -881,7 +917,7 @@
 
 
 def reduce_gradients(grad_rows, loss_row):
-    hbm = pl.BlockSpec(memory_space=pl.ANY)
+    hbm = pl.BlockSpec(memory_space=pltpu.HBM)
     vmem = pl.BlockSpec(memory_space=pltpu.VMEM)
     dma = pltpu.SemaphoreType.DMA
     shard_total, totals = pl.pallas_call(
@@ -906,7 +942,7 @@
         + [dma((2,))] * 2
         + [dma((32,))] * 2,
         compiler_params=pltpu.CompilerParams(
-            collective_id=1, has_side_effects=True, vmem_limit_bytes=56 * 1024 * 1024
+            collective_id=1, has_side_effects=True, vmem_limit_bytes=60 * 1024 * 1024
         ),
         name="reduce_gradients",
     )(grad_rows, loss_row)
@@ -988,10 +1024,14 @@
     product_into(qkv_rows, normed_a, w_qkv, 3 * D)
     allowed = column_facts[:, 0:1] == row_facts[0:1, :]
     allowed = jnp.concatenate([allowed.astype(FULL)] * 2, axis=0) > 0.5
-    loop(
-        D // LANES,
-        lambda at: attend_into(attn_out, qkv_rows, pl.ds(0, ROWS), at, D, allowed, D // HEADS),
-    )
+
+    def attend(step):
+        for part in range(2):
+            attend_into(
+                attn_out, qkv_rows, pl.ds(0, ROWS), 2 * step + part, D, allowed, D // HEADS
+            )
+
+    loop(D // LANES // 2, attend)
     w_out = ready(3)
     product_into(after_attn, attn_out, w_out, D, residual=embedded)
     norm_into(normed_b, after_attn, vec(2), vec(3), ROWS, ENC_CHUNK)
@@ -1005,7 +1045,7 @@
 
 
 def encoder_forward(part, visible_rows, segments, patch_ids, flat_weights):
-    hbm = pl.BlockSpec(memory_space=pl.ANY)
+    hbm = pl.BlockSpec(memory_space=pltpu.HBM)
     vmem = pl.BlockSpec(memory_space=pltpu.VMEM)
     smem = pl.BlockSpec(memory_space=pltpu.SMEM)
     table = jnp.asarray(split_low(position_table(D, 256)))
@@ -1031,7 +1071,7 @@
         in_specs=[smem] + [vmem] * 4 + [hbm],
         out_specs=[vmem] * 14,
         scratch_shapes=[pltpu.SemaphoreType.DMA((7,))] + tile_buffers(FETCHED),
-        compiler_params=pltpu.CompilerParams(vmem_limit_bytes=56 * 1024 * 1024),
+        compiler_params=pltpu.CompilerParams(vmem_limit_bytes=60 * 1024 * 1024),
         name="encoder_forward",
     )(part, visible_rows, segments, patch_ids, table, flat_weights)
 
@@ -1078,8 +1118,7 @@
     vec = vec_reader(buffers[0], 0, D // LANES)
     grad_of = lambda index: vec_grads.at[pl.ds(index, 1), :]
 
-    def emit(entry, left, right):
-        weight_grad(flat_ref, tiles[entry][0], left, right, turned, stage, stage_sem)
+    emit = Emitter(flat_ref, turned, stage, stage_sem)
 
     emit("project", final_enc, grad_projected)
     w_proj = ready(1)
@@ -1099,18 +1138,28 @@
     product_t_into(grad_attn, middle, w_out, D)
     allowed = column_facts[:, 0:1] == row_facts[0:1, :]
     allowed = jnp.concatenate([allowed.astype(FULL)] * 2, axis=0) > 0.5
-    loop(
-        D // LANES,
-        lambda at: attend_back_into(
-            grad_qkv, grad_attn, qkv_rows, pl.ds(0, ROWS), at, D, allowed, D // HEADS
-        ),
-    )
+
+    def attend_back(step):
+        for part in range(2):
+            attend_back_into(
+                grad_qkv,
+                grad_attn,
+                qkv_rows,
+                pl.ds(0, ROWS),
+                2 * step + part,
+                D,
+                allowed,
+                D // HEADS,
+            )
+
+    loop(D // LANES // 2, attend_back)
     emit("enc_qkv", normed_a, grad_qkv)
     w_qkv = ready(5)
     product_t_into(upper, grad_qkv, w_qkv, D)
     norm_back(grad_rows, embedded, upper, grad_rows, vec(0), grad_of(0), grad_of(1), ROWS, ENC_CHUNK)
     branch[...] = grad_rows[...].astype(LOW)
     emit("embed", vis_rows, branch)
+    emit.finish()
     groups = D // LANES
     for index in range(6):
         for group in range(groups):
@@ -1130,7 +1179,7 @@
 
 
 def encoder_backward(saved, grad_projected, flat_weights, decoder_vec_grads, flat):
-    hbm = pl.BlockSpec(memory_space=pl.ANY)
+    hbm = pl.BlockSpec(memory_space=pltpu.HBM)
     vmem = pl.BlockSpec(memory_space=pltpu.VMEM)
     inputs = [*saved, grad_projected, decoder_vec_grads, flat_weights, flat]
     low, full = (lambda *s: pltpu.VMEM(s, LOW)), (lambda *s: pltpu.VMEM(s, FULL))
@@ -1149,8 +1198,8 @@
             low(ROWS, D),
             low(ROWS, 3 * D),
             full(8, D),
-            low(TILE, ROWS),
-            low(2, TILE // TALL * FF // LANES, TALL, LANES),
+            low(FF, ROWS),
+            low(2, FF * D // (TALL * LANES), TALL, LANES),
             full(64, LANES),
             low(4, TALL, LANES),
             pltpu.SemaphoreType.DMA((2,)),
@@ -1230,10 +1279,11 @@
     groups = DD // LANES
 
     def attend(step):
-        rows = span(step // groups, IMG_ROWS)
-        attend_into(attn_out, qkv_rows, rows, step % groups, DD, allowed, head_size)
-
-    loop(IMAGES * groups, attend)
+        rows = span(step, IMG_ROWS)
+        for at in range(groups):
+            attend_into(attn_out, qkv_rows, rows, at, DD, allowed, head_size)
+
+    loop(IMAGES, attend)
     w_out = ready(2)
     product_into(after_attn, attn_out, w_out, DD, residual=dec_in)
     norm_into(normed_b, after_attn, vec(2), vec(3), DEC_ROWS, IMG_ROWS)
@@ -1258,8 +1308,7 @@
 
     loop(IMAGES, compare)
 
-    def emit(entry, left, right):
-        weight_grad(flat_ref, tiles[entry][0], left, right, turned, stage, stage_sem)
+    emit = Emitter(flat_ref, turned, stage, stage_sem)
 
     emit("pixel", final_dec, grad_pred)
     product_t_into(upper, grad_pred, w_pix, DD)
@@ -1278,11 +1327,13 @@
     product_t_into(grad_attn, branch, w_out, DD)
 
     def attend_back(step):
-        rows = span(step // groups, IMG_ROWS)
-        attend_back_into(grad_qkv, grad_attn, qkv_rows, rows, step % groups, DD, allowed, head_size)
-
-    loop(IMAGES * groups, attend_back)
+        rows = span(step, IMG_ROWS)
+        for at in range(groups):
+            attend_back_into(grad_qkv, grad_attn, qkv_rows, rows, at, DD, allowed, head_size)
+
+    loop(IMAGES, attend_back)
     emit("dec_qkv", low_rows, grad_qkv)
+    emit.finish()
     product_t_into(upper, grad_qkv, w_qkv, DD)
     norm_back(grad_rows, dec_in, upper, grad_rows, vec(0), grad_of(0), grad_of(1), DEC_ROWS, IMG_ROWS)
     upper[pl.ds(0, ROWS), :] = jnp.zeros((ROWS, DD), FULL)
@@ -1302,7 +1353,7 @@
 
 
 def decoder_step(part, projected, row_facts, targets, flat_weights, mask_total):
-    hbm = pl.BlockSpec(memory_space=pl.ANY)
+    hbm = pl.BlockSpec(memory_space=pltpu.HBM)
     vmem = pl.BlockSpec(memory_space=pltpu.VMEM)
     smem = pl.BlockSpec(memory_space=pltpu.SMEM)
     table = jnp.asarray(position_table(DD, IMG_ROWS))
@@ -1331,8 +1382,8 @@
             low(DEC_ROWS, PIX),
             full(DEC_ROWS, DD),
             full(DEC_ROWS, LANES),
-            low(TILE, DEC_ROWS),
-            low(2, TILE // TALL * DFF // LANES, TALL, LANES),
+            low(DFF, DEC_ROWS),
+            low(2, DFF * DD // (TALL * LANES), TALL, LANES),
             pltpu.SemaphoreType.DMA((2,)),
             pltpu.SemaphoreType.DMA((6,)),
         ]
@@ -1367,12 +1418,14 @@
     part = lax.axis_index("seq")
     in_kernels = master.shape[0] == SHARD_ROWS * LANES and lax.axis_size("dp") == 16
     if in_kernels:
-        flat_weights = gather_weights(master.reshape(SHARD_ROWS, LANES))
+        flat_weights, visible_rows = gather_weights(
+            master.reshape(SHARD_ROWS, LANES), visible[0]
+        )
     else:
         full_flat = lax.all_gather(master.astype(LOW), ("seq", "dp"), axis=0, tiled=True)
         flat_weights = to_tiles(full_flat)
+        visible_rows = lax.all_gather(visible[0], "seq", axis=0, tiled=True)
     flat_weights = flat_weights.reshape(-1, TALL, LANES)
-    visible_rows = lax.all_gather(visible[0], "seq", axis=0, tiled=True)
     part_row = part.reshape(1).astype(jnp.int32)
     mask_total = (PATCHES - VIS) * IMG_SEQ * visible.shape[0] * lax.axis_size("dp")
     *saved, projected, row_facts, column_facts = encoder_forward(

time: 414 us -> 357 us (0.86)
  Pallas kernels: 391 us -> 341 us
  local copies, waits for them, and re-layouts: 10.3 us -> 1.2 us
    pallas_call x1, Pallas kernels: 53.7 us -> 30 us  [encoder_backward(): pl.pallas_call(encoder_backward_kernel, out_shape=jax.ShapeDtypeStruct(fl...]
    pallas_call x1, Pallas kernels: 107 us -> 84.1 us  [decoder_step(): pl.pallas_call(partial(decoder_kernel, mask_total=mask_total), out_shape=...]
    unnamed x10 -> x4, local copies, waits for them, and re-layouts: 9.07 us -> 0.01 us
where the time goes in v3:
time: 357 us; the launch traced here: 352 us
  Pallas kernels  341 us (96%)
  other arithmetic  6.25 us (2%)
    pallas_call x1, Pallas kernels, reduce_gradients(): pl.pallas_call(reduce_kernel, out_shape=[jax.ShapeDtypeStruct((SHARD_ROWS...  107 us
    pallas_call x1, Pallas kernels, gather_weights(): pl.pallas_call(gather_kernel, out_shape=[jax.ShapeDtypeStruct((32 * SHARD...  102 us
    pallas_call x1, Pallas kernels, decoder_step(): pl.pallas_call(partial(decoder_kernel, mask_total=mask_total), out_shape=...  84.1 us
    pallas_call x1, Pallas kernels, encoder_backward(): pl.pallas_call(encoder_backward_kernel, out_shape=jax.ShapeDtypeStruct(fl...  30 us
    pallas_call x1, Pallas kernels, encoder_forward(): pl.pallas_call(encoder_forward_kernel, out_shape=[low(ROWS, PIX), full(RO...  18.6 us

profile of v3, /device:TPU:0, one launch (start us, length us, event | category | flops | bytes accessed | tf_op | source)
XLA Modules:
  0.0 352.2 jit_solution(6700378780974507073)
XLA Ops:
  0.6 101.9 %gather_weights.1 = (bf16[90688,128]{1,0:T(8,128)(2,1)}, bf16[512,768]{1,0:T(8,128)(2,1)}) custom-call(f32[2834,128]{1,0:T(8,128)} %bitcast.17, bf16[256,768]{1,0:T(8,128)(2,1)} %bitcast.19), custom_call_target="tpu_custom_call" | custom-call | tf_op jit(solution)/shard_map/gather_weights/pallas_call | solution.py:674
  102.5 18.6 %encoder_forward.1 = (bf16[256,768]{1,0:T(8,128)(2,1)}, f32[256,768]{1,0:T(8,128)}, bf16[256,768]{1,0:T(8,128)(2,1)}, bf16[256,2304]{1,0:T(8,128)(2,1)}, bf16[25...) custom-call(s32[1]{0:T(128)} %bitcast.part_ref, ...), custom_call_target="tpu_custom_call" | custom-call | tf_op jit(solution)/shard_map/encoder_forward/pallas_call | solution.py:1053
  121.1 84.1 %decoder_step.1 = (bf16[5668,16,128]{2,1,0:T(8,128)(2,1)}, bf16[256,512]{1,0:T(8,128)(2,1)}, f32[8,512]{1,0:T(8,128)}, f32[1,128]{1,0:T(1,128)}) custom-call(s32[1]{0:T(128)} %bitcast.part_ref, bf16[256,512]{1,0:T(8,128)(2,1)} %get-tuple-element.43.projected, f32[16,256]{1,0:T(8,128)} %get-tuple-element.41.row_facts, bf16[5,196,768]{2,1,0:T(8,128)(2,1)} %bitcast.18, ...), custom_call_target="tpu_custom_call" | custom-call | tf_op jit(solution)/shard_map/decoder_step/pallas_call | solution.py:1361
  205.3 30.0 %encoder_backward.1 = bf16[5668,16,128]{2,1,0:T(8,128)(2,1)} custom-call(bf16[256,768]{1,0:T(8,128)(2,1)} %get-tuple-element.30.vis_rows, f32[256,768]{1,0:T(8,128)} %get-tuple-element.31.embedded, bf16[256,768]{1,0:T(8,128)(2,1)} %get-tuple-element.32.normed_a, bf16[256,2304]{1,0:T(8,128)(2,1)} %get-tuple-element.33.qkv_rows, ...), custom_call_target="tpu_custom_call", output_to_operand_aliasing={{}: (16, {})} | custom-call | tf_op jit(solution)/shard_map/encoder_backward/pallas_call | solution.py:1186
  235.2 0.0 copy-start
  235.3 0.0 copy-start.1
  235.3 106.7 %reduce_gradients.1 = (f32[2834,128]{1,0:T(8,128)}, f32[2,8,128]{2,1,0:T(8,128)}) custom-call(bf16[90688,128]{1,0:T(8,128)(2,1)} %bitcast.16, f32[1,128]{1,0:T(1,128)} %get-tuple-element.47.loss_ref), custom_call_target="tpu_custom_call" | custom-call | tf_op jit(solution)/shard_map/reduce_gradients/pallas_call | solution.py:923
  342.0 1.3 slice_reduce_fusion
  344.7 0.0 copy-done
  344.7 0.0 copy-done.1
  344.7 5.0 %fusion.1 = (bf16[362752]{0:T(1024)(128)(2,1)}, f32[362752]{0:T(1024)}, f32[362752]{0:T(1024)}, f32[362752]{0:T(1024)}) fusion(f32[362752]{0:T(1024)S(1)} %copy-done, f32[]{:T(128)} %bitcast.7, f32[2834,128]{1,0:T(8,128)} %get-tuple-element.48, f32[]{:T(128)S(6)} %min.3, f32[362752]{0:T(1024)S(1)} %copy-done.1, f32[362752]{0:T(1024)} %param.15), kind=kLoop, calls=%fused_computation.5 | loop fusion | flops 5804032 | bytes 10882568 | tf_op jit(solution)/shard_map/convert_element_type | solution.py:1461
  349.7 1.2 slice.7
Async XLA Ops:
  235.2 109.4 %copy-start = (f32[362752]{0:T(1024)S(1)}, f32[362752]{0:T(1024)}, u32[]{:S(2)}) copy-start(f32[362752]{0:T(1024)} %param.14) | copy-start | bytes 4353028
  235.3 109.4 %copy-start.1 = (f32[362752]{0:T(1024)S(1)}, f32[362752]{0:T(1024)}, u32[]{:S(2)}) copy-start(f32[362752]{0:T(1024)} %param.16) | copy-start | bytes 4353028

commit v4 on v3

--- a/solution.py
+++ b/solution.py
@@ -287,22 +287,31 @@
     dst[rows, column(0)] = unstacked(values, head_masks(head_size, FULL), size).astype(LOW)
 
 
+def soft_columns(keys, queries, allowed, scale, heads):
+    scores = jnp.where(allowed, dot_nt(keys, queries), NEG)
+    scores = scores.reshape(heads, scores.shape[0] // heads, scores.shape[1])
+    scores = scores - jnp.max(scores, axis=1, keepdims=True)
+    powers = jnp.exp2(scores * (scale * LOG2_E))
+    return powers * (1.0 / jnp.sum(powers, axis=1, keepdims=True))
+
+
 def attend_back_into(dst, grad, qkv, rows, at, width, allowed, head_size):
     masks = head_masks(head_size, LOW)
     lanes = head_masks(head_size, FULL)
     size = rows.size
     scale = head_size**-0.5
     column = lambda part: pl.ds(pl.multiple_of(part * width + at * LANES, LANES), LANES)
-    queries = stacked(qkv[rows, column(0)], masks)
-    keys = qkv[rows, column(1)]
-    probs = soft_rows(queries, keys, allowed, scale)
-    grads = stacked(grad[rows, column(0)], masks)
-    slopes = dot_nt(grads, qkv[rows, column(2)])
-    slopes = probs * (slopes - jnp.sum(slopes * probs, axis=-1, keepdims=True))
-    slopes = slopes.astype(LOW)
-    dst[rows, column(0)] = (unstacked(dot_nn(slopes, keys), lanes, size) * scale).astype(LOW)
-    dst[rows, column(1)] = (dot_tn(slopes, queries) * scale).astype(LOW)
-    dst[rows, column(2)] = dot_tn(probs.astype(LOW), grads).astype(LOW)
+    queries = qkv[rows, column(0)]
+    keys = stacked(qkv[rows, column(1)], masks)
+    grads = grad[rows, column(0)]
+    probs = soft_columns(keys, queries, allowed, scale, len(masks))
+    slopes = dot_nt(stacked(qkv[rows, column(2)], masks), grads).reshape(probs.shape)
+    slopes = probs * (slopes - jnp.sum(slopes * probs, axis=1, keepdims=True))
+    flat = (len(masks) * size, size)
+    slopes, probs = slopes.reshape(flat).astype(LOW), probs.reshape(flat).astype(LOW)
+    dst[rows, column(0)] = (dot_tn(keys, slopes).T * scale).astype(LOW)
+    dst[rows, column(1)] = (unstacked(dot_nn(slopes, queries), lanes, size) * scale).astype(LOW)
+    dst[rows, column(2)] = unstacked(dot_nn(probs, grads), lanes, size).astype(LOW)
 
 
 def entry_tiles():
@@ -382,6 +391,7 @@
 PAD_ROWS = A_ROWS + B_ROWS
 B_TRUE = SHARD_ROWS - A_ROWS
 HALO = 384
+HALO_STEP = 64
 WIDE_ROWS = SHARD_ROWS + 2 * HALO
 PARTS = {
     "a1": (0, A_HALF),
@@ -572,24 +582,82 @@
     by_place(at, body)
 
 
-def entry_blocks(me, body):
-    first = me * SHARD_ROWS
+def entry_blocks(me, body, edges=False):
+    first, stop = me * SHARD_ROWS, me * SHARD_ROWS + SHARD_ROWS
     offset = 0
     for _, (rows, columns) in layout()[:11]:
         groups, blocks = columns // LANES, rows // TALL
         unit = TALL * groups
-        low = jnp.minimum(jnp.maximum(first - offset, 0) // unit, blocks)
-        high = jnp.minimum(
-            (jnp.maximum(first + SHARD_ROWS - offset, 0) + unit - 1) // unit, blocks
+        total = unit * blocks
+        if edges:
+            for cut in (first, stop):
+                inside = jnp.maximum(cut - offset, 0)
+                block = inside // unit
+
+                @pl.when((inside < total) & (inside % unit > 0))
+                def _(block=block, offset=offset, unit=unit, groups=groups):
+                    body(offset + block * unit, groups)
+        else:
+            low = jnp.minimum((jnp.maximum(first - offset, 0) + unit - 1) // unit, blocks)
+            high = jnp.minimum(jnp.maximum(stop - offset, 0) // unit, blocks)
+
+            def one(block, carry, offset=offset, unit=unit, groups=groups):
+                body(offset + block * unit, groups)
+                return carry
+
+            lax.fori_loop(low, jnp.maximum(high, low), one, 0)
+        offset += total
+    return offset
+
+
+def cut_rows(cut):
+    before = after = 0
+    offset = 0
+    for _, (rows, columns) in layout()[:11]:
+        unit, total = TALL * (columns // LANES), rows * (columns // LANES)
+        inside = jnp.maximum(cut - offset, 0)
+        cuts = ((inside < total) & (inside % unit > 0)).astype(jnp.int32)
+        before = before + cuts * (inside % unit)
+        after = after + cuts * (unit - inside % unit)
+        offset += total
+    return before, after
+
+
+class Halo:
+    def __init__(self, at, here, start, wide, send_sem, recv_sem):
+        self.at, self.here, self.start, self.wide = at, here, start, wide
+        self.sems = send_sem, recv_sem
+        first = at.me * SHARD_ROWS
+        head, give_back = cut_rows(first)
+        give_next, tail = cut_rows(first + SHARD_ROWS)
+        self.given, self.taken = (give_back, give_next), (tail, head)
+
+    def copies(self, side, index):
+        low, high = HALO_STEP * index, HALO_STEP * (index + 1)
+        src = self.start + (low if side == 0 else SHARD_ROWS - high)
+        dst = HALO + SHARD_ROWS + low if side == 0 else HALO - high
+        return pltpu.make_async_remote_copy(
+            src_ref=self.here.at[pl.ds(src, HALO_STEP)],
+            dst_ref=self.wide.at[pl.ds(dst, HALO_STEP)],
+            send_sem=self.sems[0].at[side, index],
+            recv_sem=self.sems[1].at[side, index],
+            device_id=self.at.devices["back" if side == 0 else "next"],
+            device_id_type=MESH,
         )
 
-        def one(block, carry, offset=offset, unit=unit, groups=groups):
-            body(offset + block * unit, groups)
-            return carry
-
-        lax.fori_loop(low, high, one, 0)
-        offset += unit * blocks
-    return offset
+    def each(self, rows, action):
+        for side in range(2):
+            for index in range(HALO // HALO_STEP):
+                pl.when(rows[side] > HALO_STEP * index)(partial(action, side, index))
+
+    def start_all(self):
+        self.each(self.given, lambda side, index: self.copies(side, index).start())
+
+    def take(self):
+        self.each(self.taken, lambda side, index: self.copies(side, index).wait_recv())
+
+    def finish(self):
+        self.each(self.given, lambda side, index: self.copies(side, index).wait_send())
 
 
 VEC_ROWS = 64
@@ -606,31 +674,15 @@
     own.start()
     at.greet()
     out = Outbox()
-    tail = wide.at[pl.ds(HALO + SHARD_ROWS, HALO)]
-    head = wide.at[pl.ds(0, HALO)]
-    out.send(
-        master_ref.at[pl.ds(0, HALO)],
-        tail,
-        halo_send.at[0],
-        halo_recv.at[0],
-        at.devices["back"],
-    )
-    out.send(
-        master_ref.at[pl.ds(SHARD_ROWS - HALO, HALO)],
-        head,
-        halo_send.at[1],
-        halo_recv.at[1],
-        at.devices["next"],
-    )
+    halo = Halo(at, master_ref, 0, wide, halo_send, halo_recv)
+    halo.start_all()
     half = visible_ref.shape[0]
     rows_here = both_ref.at[pl.ds(pl.multiple_of(at.core * half, half), half)]
     rows_there = both_ref.at[pl.ds(pl.multiple_of((1 - at.core) * half, half), half)]
-    out.send(visible_ref, rows_here, halo_send.at[2], halo_recv.at[2], at.devices["core"])
+    out.send(visible_ref, rows_here, own_sem.at[3], own_sem.at[4], at.devices["core"])
     keep = pltpu.make_async_copy(visible_ref, rows_here, own_sem.at[2])
     keep.start()
     own.wait()
-    arrived(tail, halo_recv.at[0], at.devices["x"])
-    arrived(head, halo_recv.at[1], at.devices["x"])
 
     def turn(row, groups):
         start = row - first + HALO
@@ -641,6 +693,8 @@
             ].astype(LOW)
 
     vec_start = entry_blocks(at.me, turn)
+    halo.take()
+    entry_blocks(at.me, turn, edges=True)
 
     @pl.when(at.me == 31)
     def _():
@@ -663,13 +717,14 @@
     gather_exchange(at, flat_ref, source, recv, core_recv, sends, core_send)
     mine.wait()
     keep.wait()
-    arrived(rows_there, halo_recv.at[2], at.devices["x"])
+    arrived(rows_there, own_sem.at[4], at.devices["x"])
     out.finish()
+    halo.finish()
 
 
 def gather_weights(master_rows, visible_rows):
     hbm = pl.BlockSpec(memory_space=pltpu.HBM)
-    threes = pltpu.SemaphoreType.DMA((3,))
+    steps = pltpu.SemaphoreType.DMA((2, HALO // HALO_STEP))
     half, width = visible_rows.shape
     return pl.pallas_call(
         gather_kernel,
@@ -682,9 +737,9 @@
         scratch_shapes=[
             pltpu.VMEM((WIDE_ROWS + 6, LANES), FULL),
             pltpu.VMEM((WIDE_ROWS + 30, LANES), LOW),
-            threes,
-            threes,
-            threes,
+            pltpu.SemaphoreType.DMA((5,)),
+            steps,
+            steps,
         ]
         + [pltpu.SemaphoreType.DMA((16, 4))] * 7,
         compiler_params=pltpu.CompilerParams(
@@ -778,13 +833,22 @@
         out = Outbox()
         paired, joined = set(), set()
 
-        def pair(chip, key):
-            if key in paired:
-                return
-            paired.add(key)
-            load(chip).wait()
-            arrived(theirs.at[chip, body], core_recv.at[chip], at.devices["x"])
-            add_into(own.at[chip], 0, [(own.at[chip], 0), (theirs.at[chip], 0)], PAD_ROWS, 32)
+        def pair(chip, column, part):
+            if (column, "all") not in paired:
+                paired.add((column, "all"))
+                load(chip).wait()
+                arrived(theirs.at[chip, body], core_recv.at[chip], at.devices["x"])
+            name = "b" if part[0] == "b" else part
+            if (column, name) not in paired:
+                paired.add((column, name))
+                first, size = PARTS[name]
+                add_into(
+                    own.at[chip],
+                    first,
+                    [(own.at[chip], first), (theirs.at[chip], first)],
+                    size,
+                    size // (4 if name == "b" else 3),
+                )
 
         def landing(link, plane, chip, part, relay):
             first, size = PARTS[part]
@@ -800,7 +864,7 @@
             mirrored, column, part = item_of(item)
             plane = at.plane(mirrored)
             chip = 4 * plane + at.columns[column]
-            pair(chip, (mirrored, column))
+            pair(chip, (mirrored, column), part)
             first, size = PARTS[part]
             terms = []
             links = onward(inner, item)
@@ -863,37 +927,30 @@
     by_place(at, reduce_parts)
     pairs.finish()
 
-    halo = Outbox()
-    head, after = wide.at[pl.ds(0, HALO)], wide.at[pl.ds(HALO + SHARD_ROWS, HALO)]
-    halo.send(
-        wide.at[pl.ds(HALO, HALO)], after, halo_send.at[0], halo_recv.at[0], at.devices["back"]
-    )
-    halo.send(
-        wide.at[pl.ds(SHARD_ROWS, HALO)], head, halo_send.at[1], halo_recv.at[1], at.devices["next"]
-    )
-    whole_steps = SHARD_ROWS // 32
+    tiny = Outbox()
+    halo = Halo(at, wide, HALO, wide, halo_send, halo_recv)
+    halo.start_all()
+    step_rows = 352
+    whole_steps = SHARD_ROWS // step_rows
 
     def squares(index, carry):
-        piece = wide[pl.ds(pl.multiple_of(HALO + index * 32, 8), 32), :]
+        piece = wide[pl.ds(pl.multiple_of(HALO + index * step_rows, 8), step_rows), :]
         piece = piece * piece
-        return carry + jnp.sum(piece.reshape(4, 8, LANES), axis=0)
+        return carry + jnp.sum(piece.reshape(step_rows // 8, 8, LANES), axis=0)
 
     square = lax.fori_loop(0, whole_steps, squares, jnp.zeros((8, LANES), FULL))
-    rest = wide[pl.ds(HALO + whole_steps * 32, SHARD_ROWS - whole_steps * 32), :]
+    rest = wide[pl.ds(HALO + whole_steps * step_rows, SHARD_ROWS - whole_steps * step_rows), :]
     square = square + 0.125 * jnp.sum(rest * rest, axis=0, keepdims=True)
     scalars[at.me, 0] = square
     scalars[at.me, 1] = jnp.broadcast_to(loss_ref[...], (8, LANES))
     for index in range(1, 32):
-        halo.send(
+        tiny.send(
             scalars.at[at.me],
             scalars.at[at.me],
             tiny_send.at[index],
             tiny_recv.at[at.me],
             at.ring(index),
         )
-    arrived(after, halo_recv.at[0], at.devices["x"])
-    arrived(head, halo_recv.at[1], at.devices["x"])
-
     def turn_back(row, groups):
         start = row - at.me * SHARD_ROWS + HALO
         for group in range(groups):
@@ -902,6 +959,8 @@
             ]
 
     vec_start = entry_blocks(at.me, turn_back)
+    halo.take()
+    entry_blocks(at.me, turn_back, edges=True)
 
     @pl.when(at.me == 31)
     def _():
@@ -914,6 +973,7 @@
         arrived(scalars.at[peer], tiny_recv.at[peer], at.devices["x"])
     total_ref[...] = jnp.sum(scalars[...], axis=0)
     halo.finish()
+    tiny.finish()
 
 
 def reduce_gradients(grad_rows, loss_row):
@@ -939,7 +999,7 @@
         + [dma((16, 4))] * 2
         + [dma((4, 5))] * 2
         + [dma((16, 4))] * 2
-        + [dma((2,))] * 2
+        + [dma((2, HALO // HALO_STEP))] * 2
         + [dma((32,))] * 2,
         compiler_params=pltpu.CompilerParams(
             collective_id=1, has_side_effects=True, vmem_limit_bytes=60 * 1024 * 1024
@@ -962,23 +1022,33 @@
     patches_ref,
     table_ref,
     flat_ref,
-    vis_rows,
-    embedded,
-    normed_a,
-    qkv_rows,
-    attn_out,
-    after_attn,
-    normed_b,
-    slope,
-    hidden_act,
-    encoded,
-    final_enc,
-    projected,
-    row_facts,
-    column_facts,
-    sems,
-    *buffers,
+    *refs,
 ):
+    results, kept, (out_sem, sems, *buffers) = refs[:14], refs[14:28], refs[28:]
+    (
+        vis_rows,
+        embedded,
+        normed_a,
+        qkv_rows,
+        attn_out,
+        after_attn,
+        normed_b,
+        slope,
+        hidden_act,
+        encoded,
+        final_enc,
+        projected,
+        row_facts,
+        column_facts,
+    ) = kept
+
+    def shipment(index):
+        return pltpu.make_async_copy(kept[index], results[index], out_sem.at[index])
+
+    def ship(*indices):
+        for index in indices:
+            shipment(index).start()
+
     ready = fetch(flat_ref, FETCHED, buffers, sems)
     part = part_ref[0]
     total = segments_ref.shape[1]
@@ -1012,16 +1082,20 @@
     row_facts[...] = dot_nt(facts[0:16], select)
     column_facts[...] = dot_nt(select, facts)
     vis_rows[...] = dot_nn(select, visible_ref[...]).astype(LOW)
+    ship(0, 12, 13)
     patch = column_facts[:, 1:2].astype(jnp.int32)
     spot = (lax.broadcasted_iota(jnp.int32, (ROWS, table_ref.shape[1]), 1) == patch).astype(FULL).astype(LOW)
     embedded[...] = dot_nn(spot, table_ref[0]) + dot_nn(spot, table_ref[1]) + dot_nn(spot, table_ref[2])
     w_embed = ready(1)
     product_into(embedded, vis_rows, w_embed, D, residual=embedded)
+    ship(1)
     ready(0)
     vec = vec_reader(buffers[0], 0, D // LANES)
     norm_into(normed_a, embedded, vec(0), vec(1), ROWS, ENC_CHUNK)
+    ship(2)
     w_qkv = ready(2)
     product_into(qkv_rows, normed_a, w_qkv, 3 * D)
+    ship(3)
     allowed = column_facts[:, 0:1] == row_facts[0:1, :]
     allowed = jnp.concatenate([allowed.astype(FULL)] * 2, axis=0) > 0.5
 
@@ -1032,16 +1106,25 @@
             )
 
     loop(D // LANES // 2, attend)
+    ship(4)
     w_out = ready(3)
     product_into(after_attn, attn_out, w_out, D, residual=embedded)
+    ship(5)
     norm_into(normed_b, after_attn, vec(2), vec(3), ROWS, ENC_CHUNK)
+    ship(6)
     w_up = ready(4)
     up_into(hidden_act, slope, normed_b, w_up, FF, 512)
+    ship(7, 8)
     w_down = ready(5)
     product_into(encoded, hidden_act, w_down, D, residual=after_attn)
+    ship(9)
     norm_into(final_enc, encoded, vec(4), vec(5), ROWS, ENC_CHUNK)
+    ship(10)
     w_proj = ready(6)
     product_into(projected, final_enc, w_proj, DD)
+    ship(11)
+    for index in range(len(kept)):
+        shipment(index).wait()
 
 
 def encoder_forward(part, visible_rows, segments, patch_ids, flat_weights):
@@ -1049,70 +1132,89 @@
     vmem = pl.BlockSpec(memory_space=pltpu.VMEM)
     smem = pl.BlockSpec(memory_space=pltpu.SMEM)
     table = jnp.asarray(split_low(position_table(D, 256)))
-    low, full = (lambda *s: jax.ShapeDtypeStruct(s, LOW)), (lambda *s: jax.ShapeDtypeStruct(s, FULL))
+    kept = [
+        ((ROWS, PIX), LOW),
+        ((ROWS, D), FULL),
+        ((ROWS, D), LOW),
+        ((ROWS, 3 * D), LOW),
+        ((ROWS, D), LOW),
+        ((ROWS, D), FULL),
+        ((ROWS, D), LOW),
+        ((ROWS, FF), FULL),
+        ((ROWS, FF), LOW),
+        ((ROWS, D), FULL),
+        ((ROWS, D), LOW),
+        ((ROWS, DD), LOW),
+        ((16, ROWS), FULL),
+        ((ROWS, LANES), FULL),
+    ]
     return pl.pallas_call(
         encoder_forward_kernel,
-        out_shape=[
-            low(ROWS, PIX),
-            full(ROWS, D),
-            low(ROWS, D),
-            low(ROWS, 3 * D),
-            low(ROWS, D),
-            full(ROWS, D),
-            low(ROWS, D),
-            full(ROWS, FF),
-            low(ROWS, FF),
-            full(ROWS, D),
-            low(ROWS, D),
-            low(ROWS, DD),
-            full(16, ROWS),
-            full(ROWS, LANES),
-        ],
+        out_shape=[jax.ShapeDtypeStruct(s, d) for s, d in kept],
         in_specs=[smem] + [vmem] * 4 + [hbm],
-        out_specs=[vmem] * 14,
-        scratch_shapes=[pltpu.SemaphoreType.DMA((7,))] + tile_buffers(FETCHED),
+        out_specs=[hbm] * 14,
+        scratch_shapes=[pltpu.VMEM(s, d) for s, d in kept]
+        + [pltpu.SemaphoreType.DMA((14,)), pltpu.SemaphoreType.DMA((7,))] + tile_buffers(FETCHED),
         compiler_params=pltpu.CompilerParams(vmem_limit_bytes=60 * 1024 * 1024),
         name="encoder_forward",
     )(part, visible_rows, segments, patch_ids, table, flat_weights)
 
 
 def encoder_backward_kernel(
-    vis_rows,
-    embedded,
-    normed_a,
-    qkv_rows,
-    attn_out,
-    after_attn,
-    normed_b,
-    slope,
-    hidden_act,
-    encoded,
-    final_enc,
-    row_facts,
-    column_facts,
     grad_projected,
     decoder_vecs,
-    weights_ref,
-    partial_ref,
-    flat_ref,
-    grad_rows,
-    upper,
-    branch,
-    grad_pre,
-    middle,
-    grad_attn,
-    grad_qkv,
-    vec_grads,
-    turned,
-    stage,
-    vec_full,
-    vec_stage,
-    stage_sem,
-    sems,
-    *buffers,
+    *refs,
 ):
+    stored, refs = refs[:13], refs[13:]
+    weights_ref, partial_ref, flat_ref, refs = *refs[:3], refs[3:]
+    kept, refs = refs[:13], refs[13:]
+    (
+        grad_rows,
+        upper,
+        branch,
+        grad_pre,
+        middle,
+        grad_attn,
+        grad_qkv,
+        vec_grads,
+        turned,
+        stage,
+        vec_full,
+        vec_stage,
+        stage_sem,
+        kept_sem,
+        sems,
+        *buffers,
+    ) = refs
+    (
+        vis_rows,
+        embedded,
+        normed_a,
+        qkv_rows,
+        attn_out,
+        after_attn,
+        normed_b,
+        slope,
+        hidden_act,
+        encoded,
+        final_enc,
+        row_facts,
+        column_facts,
+    ) = kept
+
+    def delivery(index):
+        return pltpu.make_async_copy(stored[index], kept[index], kept_sem.at[index])
+
+    def need(*indices):
+        for index in indices:
+            delivery(index).wait()
+
+    for index in (10, 9, 8):
+        delivery(index).start()
     del partial_ref
     ready = fetch(weights_ref, BACKWARD_FETCHED, buffers, sems)
+    for index in (7, 6, 5, 4, 12, 11, 3, 2, 1, 0):
+        delivery(index).start()
     tiles = entry_tiles()
     ready(0)
     vec = vec_reader(buffers[0], 0, D // LANES)
@@ -1120,22 +1222,30 @@
 
     emit = Emitter(flat_ref, turned, stage, stage_sem)
 
+    need(10)
     emit("project", final_enc, grad_projected)
     w_proj = ready(1)
     product_t_into(upper, grad_projected, w_proj, D)
+    need(9)
     norm_back(grad_rows, encoded, upper, None, vec(4), grad_of(4), grad_of(5), ROWS, ENC_CHUNK)
     branch[...] = grad_rows[...].astype(LOW)
+    need(8)
     emit("enc_down", hidden_act, branch)
+    need(7)
     w_down = ready(2)
     down_back_into(grad_pre, branch, w_down, slope, FF, 512)
+    need(6)
     emit("enc_up", normed_b, grad_pre)
     w_up = ready(3)
     product_t_into(upper, grad_pre, w_up, D)
+    need(5)
     norm_back(grad_rows, after_attn, upper, grad_rows, vec(2), grad_of(2), grad_of(3), ROWS, ENC_CHUNK)
     middle[...] = grad_rows[...].astype(LOW)
+    need(4)
     emit("enc_out", attn_out, middle)
     w_out = ready(4)
     product_t_into(grad_attn, middle, w_out, D)
+    need(12, 11, 3)
     allowed = column_facts[:, 0:1] == row_facts[0:1, :]
     allowed = jnp.concatenate([allowed.astype(FULL)] * 2, axis=0) > 0.5
 
@@ -1153,11 +1263,14 @@
             )
 
     loop(D // LANES // 2, attend_back)
+    need(2)
     emit("enc_qkv", normed_a, grad_qkv)
     w_qkv = ready(5)
     product_t_into(upper, grad_qkv, w_qkv, D)
+    need(1)
     norm_back(grad_rows, embedded, upper, grad_rows, vec(0), grad_of(0), grad_of(1), ROWS, ENC_CHUNK)
     branch[...] = grad_rows[...].astype(LOW)
+    need(0)
     emit("embed", vis_rows, branch)
     emit.finish()
     groups = D // LANES
@@ -1181,15 +1294,16 @@
 def encoder_backward(saved, grad_projected, flat_weights, decoder_vec_grads, flat):
     hbm = pl.BlockSpec(memory_space=pltpu.HBM)
     vmem = pl.BlockSpec(memory_space=pltpu.VMEM)
-    inputs = [*saved, grad_projected, decoder_vec_grads, flat_weights, flat]
+    inputs = [grad_projected, decoder_vec_grads, *saved, flat_weights, flat]
     low, full = (lambda *s: pltpu.VMEM(s, LOW)), (lambda *s: pltpu.VMEM(s, FULL))
     return pl.pallas_call(
         encoder_backward_kernel,
         out_shape=jax.ShapeDtypeStruct(flat.shape, LOW),
-        in_specs=[vmem] * 15 + [hbm] * 2,
+        in_specs=[vmem] * 2 + [hbm] * 15,
         out_specs=hbm,
         input_output_aliases={len(inputs) - 1: 0},
-        scratch_shapes=[
+        scratch_shapes=[pltpu.VMEM(array.shape, array.dtype) for array in saved]
+        + [
             full(ROWS, D),
             full(ROWS, D),
             low(ROWS, D),
@@ -1203,6 +1317,7 @@
             full(64, LANES),
             low(4, TALL, LANES),
             pltpu.SemaphoreType.DMA((2,)),
+            pltpu.SemaphoreType.DMA((13,)),
             pltpu.SemaphoreType.DMA((6,)),
         ]
         + tile_buffers(BACKWARD_FETCHED),
@@ -1326,10 +1441,13 @@
     grad_attn, grad_qkv = normed_b, grad_pre.at[:, pl.ds(0, 3 * DD)]
     product_t_into(grad_attn, branch, w_out, DD)
 
+    key_row = lax.broadcasted_iota(jnp.int32, (heads, IMG_ROWS, IMG_ROWS), 1)
+    real_keys = (key_row < PATCHES).astype(FULL).reshape(heads * IMG_ROWS, IMG_ROWS) > 0.5
+
     def attend_back(step):
         rows = span(step, IMG_ROWS)
         for at in range(groups):
-            attend_back_into(grad_qkv, grad_attn, qkv_rows, rows, at, DD, allowed, head_size)
+            attend_back_into(grad_qkv, grad_attn, qkv_rows, rows, at, DD, real_keys, head_size)
 
     loop(IMAGES, attend_back)
     emit("dec_qkv", low_rows, grad_qkv)

time: 357 us -> 340 us (0.952)
  Pallas kernels: 341 us -> 325 us
    pallas_call x1, Pallas kernels: 102 us -> 96.4 us  [gather_weights(): pl.pallas_call(gather_kernel, out_shape=[jax.ShapeDtypeStruct((32 * SHARD...]
    pallas_call x1, Pallas kernels: 107 us -> 103 us  [reduce_gradients(): pl.pallas_call(reduce_kernel, out_shape=[jax.ShapeDtypeStruct((SHARD_ROWS...]
    pallas_call x1, Pallas kernels: 84.1 us -> 80.3 us  [decoder_step(): pl.pallas_call(partial(decoder_kernel, mask_total=mask_total), out_shape=...]
where the time goes in v4:
time: 340 us; the launch traced here: 336 us
  Pallas kernels  325 us (96%)
  other arithmetic  6.25 us (2%)
  between operations  3.76 us (1%)
    pallas_call x1, Pallas kernels, reduce_gradients(): pl.pallas_call(reduce_kernel, out_shape=[jax.ShapeDtypeStruct((SHARD_ROWS...  103 us
    pallas_call x1, Pallas kernels, gather_weights(): pl.pallas_call(gather_kernel, out_shape=[jax.ShapeDtypeStruct((32 * SHARD...  96.4 us
    pallas_call x1, Pallas kernels, decoder_step(): pl.pallas_call(partial(decoder_kernel, mask_total=mask_total), out_shape=...  80.3 us
    pallas_call x1, Pallas kernels, encoder_backward(): pl.pallas_call(encoder_backward_kernel, out_shape=jax.ShapeDtypeStruct(fl...  29 us
    pallas_call x1, Pallas kernels, encoder_forward(): pl.pallas_call(encoder_forward_kernel, out_shape=[jax.ShapeDtypeStruct(s,...  16.4 us

profile of v4, /device:TPU:0, one launch (start us, length us, event | category | flops | bytes accessed | tf_op | source)
XLA Modules:
  0.0 335.9 jit_solution(5205489544931703006)
XLA Ops:
  0.6 96.4 %gather_weights.1 = (bf16[90688,128]{1,0:T(8,128)(2,1)}, bf16[512,768]{1,0:T(8,128)(2,1)}) custom-call(f32[2834,128]{1,0:T(8,128)} %bitcast.17, bf16[256,768]{1,0:T(8,128)(2,1)} %bitcast.19), custom_call_target="tpu_custom_call" | custom-call | tf_op jit(solution)/shard_map/gather_weights/pallas_call | solution.py:729
  97.0 16.4 %encoder_forward.1 = (bf16[256,768]{1,0:T(8,128)(2,1)}, f32[256,768]{1,0:T(8,128)}, bf16[256,768]{1,0:T(8,128)(2,1)}, bf16[256,2304]{1,0:T(8,128)(2,1)}, bf16[25...) custom-call(s32[1]{0:T(128)} %bitcast.part_ref, ...), custom_call_target="tpu_custom_call" | custom-call | tf_op jit(solution)/shard_map/encoder_forward/pallas_call | solution.py:1151
  113.4 80.3 %decoder_step.1 = (bf16[5668,16,128]{2,1,0:T(8,128)(2,1)}, bf16[256,512]{1,0:T(8,128)(2,1)}, f32[8,512]{1,0:T(8,128)}, f32[1,128]{1,0:T(1,128)}) custom-call(s32[1]{0:T(128)} %bitcast.part_ref, bf16[256,512]{1,0:T(8,128)(2,1)} %get-tuple-element.30.projected, f32[16,256]{1,0:T(8,128)} %get-tuple-element.31.row_facts.refs_11_, bf16[5,196,768]{2,1,0:T(8,128)(2,1)} %bitcast.18, ...), custom_call_target="tpu_custom_call" | custom-call | tf_op jit(solution)/shard_map/decoder_step/pallas_call | solution.py:1479
  193.8 29.0 %encoder_backward.1 = bf16[5668,16,128]{2,1,0:T(8,128)(2,1)} custom-call(bf16[256,512]{1,0:T(8,128)(2,1)} %get-tuple-element.32.grad_projected, f32[8,512]{1,0:T(8,128)} %get-tuple-element.33.decoder_vecs, bf16[256,768]{1,0:T(8,128)(2,1)} %get-tuple-element.34.refs_0_, f32[256,768]{1,0:T(8,128)} %get-tuple-element.35.refs_1_, ...), custom_call_target="tpu_custom_call", output_to_operand_aliasing={{}: (16, {})} | custom-call | tf_op jit(solution)/shard_map/encoder_backward/pallas_call | solution.py:1299
  222.7 0.0 copy-start
  222.8 0.0 copy-start.1
  222.8 102.6 %reduce_gradients.1 = (f32[2834,128]{1,0:T(8,128)}, f32[2,8,128]{2,1,0:T(8,128)}) custom-call(bf16[90688,128]{1,0:T(8,128)(2,1)} %bitcast.16, f32[1,128]{1,0:T(1,128)} %get-tuple-element.47.loss_ref), custom_call_target="tpu_custom_call" | custom-call | tf_op jit(solution)/shard_map/reduce_gradients/pallas_call | solution.py:983
  325.4 1.3 slice_reduce_fusion
  328.1 0.0 copy-done
  328.1 0.0 copy-done.1
  328.1 5.0 %fusion.1 = (bf16[362752]{0:T(1024)(128)(2,1)}, f32[362752]{0:T(1024)}, f32[362752]{0:T(1024)}, f32[362752]{0:T(1024)}) fusion(f32[362752]{0:T(1024)S(1)} %copy-done, f32[]{:T(128)} %bitcast.7, f32[2834,128]{1,0:T(8,128)} %get-tuple-element.48, f32[]{:T(128)S(6)} %min.3, f32[362752]{0:T(1024)S(1)} %copy-done.1, f32[362752]{0:T(1024)} %param.15), kind=kLoop, calls=%fused_computation.5 | loop fusion | flops 5804032 | bytes 10882568 | tf_op jit(solution)/shard_map/convert_element_type | solution.py:1579
  333.1 1.2 slice.7
Async XLA Ops:
  222.7 105.3 %copy-start = (f32[362752]{0:T(1024)S(1)}, f32[362752]{0:T(1024)}, u32[]{:S(2)}) copy-start(f32[362752]{0:T(1024)} %param.14) | copy-start | bytes 4353028
  222.8 105.3 %copy-start.1 = (f32[362752]{0:T(1024)S(1)}, f32[362752]{0:T(1024)}, u32[]{:S(2)}) copy-start(f32[362752]{0:T(1024)} %param.16) | copy-start | bytes 4353028

commit v5 on v4

--- a/solution.py
+++ b/solution.py
@@ -91,7 +91,7 @@
 
 
 def unrolled(count, body):
-    size = next(size for size in (3, 2, 1) if count % size == 0)
+    size = next(size for size in (4, 3, 2, 1) if count % size == 0)
 
     def one(step):
         for part in range(size):
@@ -217,7 +217,7 @@
         before()
     tiles = stage.at[slot, pl.ds(0, count)].reshape(high, groups, TALL, LANES)
     piece = columns // TILE
-    unroll = next(u for u in (3, 2, 1) if piece % u == 0)
+    unroll = next(u for u in (6, 4, 3, 2, 1) if piece % u == 0)
 
     def across(step):
         for part in range(unroll):
@@ -287,27 +287,53 @@
     dst[rows, column(0)] = unstacked(values, head_masks(head_size, FULL), size).astype(LOW)
 
 
-def soft_columns(keys, queries, allowed, scale, heads):
-    scores = jnp.where(allowed, dot_nt(keys, queries), NEG)
-    scores = scores.reshape(heads, scores.shape[0] // heads, scores.shape[1])
-    scores = scores - jnp.max(scores, axis=1, keepdims=True)
-    powers = jnp.exp2(scores * (scale * LOG2_E))
-    return powers * (1.0 / jnp.sum(powers, axis=1, keepdims=True))
-
-
-def attend_back_into(dst, grad, qkv, rows, at, width, allowed, head_size):
+def only_real(scores, real, allowed):
+    if real is None:
+        return jnp.where(allowed, scores, NEG)
+    whole = real // 8 * 8
+    key = whole + lax.broadcasted_iota(jnp.int32, (1, scores.shape[1] - whole, 1), 1)
+    return jnp.concatenate(
+        [scores[:, :whole], jnp.where(key < real, scores[:, whole:], NEG)], axis=1
+    )
+
+
+def column_scores(keys, queries, heads, real, allowed):
+    scores = dot_nt(keys, queries)
+    return only_real(scores.reshape(heads, scores.shape[0] // heads, scores.shape[1]), real, allowed)
+
+
+def attend_columns_into(dst, qkv, rows, at, width, real, head_size, logs):
+    masks = head_masks(head_size, LOW)
+    heads, size, scale = len(masks), rows.size, head_size**-0.5 * LOG2_E
+    column = lambda part: pl.ds(pl.multiple_of(part * width + at * LANES, LANES), LANES)
+    keys = stacked(qkv[rows, column(1)], masks)
+    scores = column_scores(keys, qkv[rows, column(0)], heads, real, None)
+    top = jnp.max(scores, axis=1, keepdims=True)
+    powers = jnp.exp2((scores - top) * scale)
+    total = jnp.sum(powers, axis=1, keepdims=True)
+    logs[...] = top * scale + jnp.log2(total)
+    probs = (powers * (1.0 / total)).reshape(heads * size, size).astype(LOW)
+    dst[rows, column(0)] = dot_tn(stacked(qkv[rows, column(2)], masks), probs).T.astype(LOW)
+
+
+def attend_back_into(dst, grad, qkv, rows, at, width, head_size, real=None, allowed=None, logs=None):
     masks = head_masks(head_size, LOW)
     lanes = head_masks(head_size, FULL)
-    size = rows.size
-    scale = head_size**-0.5
+    heads, size, scale = len(masks), rows.size, head_size**-0.5
     column = lambda part: pl.ds(pl.multiple_of(part * width + at * LANES, LANES), LANES)
     queries = qkv[rows, column(0)]
     keys = stacked(qkv[rows, column(1)], masks)
     grads = grad[rows, column(0)]
-    probs = soft_columns(keys, queries, allowed, scale, len(masks))
+    scores = column_scores(keys, queries, heads, real, allowed)
+    if logs is None:
+        scores = scores - jnp.max(scores, axis=1, keepdims=True)
+        powers = jnp.exp2(scores * (scale * LOG2_E))
+        probs = powers * (1.0 / jnp.sum(powers, axis=1, keepdims=True))
+    else:
+        probs = jnp.exp2(scores * (scale * LOG2_E) - logs[...])
     slopes = dot_nt(stacked(qkv[rows, column(2)], masks), grads).reshape(probs.shape)
     slopes = probs * (slopes - jnp.sum(slopes * probs, axis=1, keepdims=True))
-    flat = (len(masks) * size, size)
+    flat = (heads * size, size)
     slopes, probs = slopes.reshape(flat).astype(LOW), probs.reshape(flat).astype(LOW)
     dst[rows, column(0)] = (dot_tn(keys, slopes).T * scale).astype(LOW)
     dst[rows, column(1)] = (unstacked(dot_nn(slopes, queries), lanes, size) * scale).astype(LOW)
@@ -765,7 +791,8 @@
     grad_ref,
     loss_ref,
     shard_ref,
-    total_ref,
+    square_ref,
+    loss_total_ref,
     own,
     theirs,
     from_x,
@@ -971,7 +998,11 @@
     for index in range(1, 32):
         peer = (at.me + index) % 32
         arrived(scalars.at[peer], tiny_recv.at[peer], at.devices["x"])
-    total_ref[...] = jnp.sum(scalars[...], axis=0)
+    totals = jnp.sum(scalars[...], axis=0)
+    square_ref[...] = jnp.sum(
+        jnp.sum(totals[0], axis=0, keepdims=True), axis=1, keepdims=True
+    )
+    loss_total_ref[...] = totals[1, 0:1, 0:1]
     halo.finish()
     tiny.finish()
 
@@ -980,14 +1011,15 @@
     hbm = pl.BlockSpec(memory_space=pltpu.HBM)
     vmem = pl.BlockSpec(memory_space=pltpu.VMEM)
     dma = pltpu.SemaphoreType.DMA
-    shard_total, totals = pl.pallas_call(
+    shard_total, square, loss = pl.pallas_call(
         reduce_kernel,
         out_shape=[
             jax.ShapeDtypeStruct((SHARD_ROWS, LANES), FULL),
-            jax.ShapeDtypeStruct((2, 8, LANES), FULL),
+            jax.ShapeDtypeStruct((1, 1), FULL),
+            jax.ShapeDtypeStruct((1, 1), FULL),
         ],
         in_specs=[hbm, vmem],
-        out_specs=[vmem, vmem],
+        out_specs=[vmem, vmem, vmem],
         scratch_shapes=[pltpu.VMEM((16, PAD_ROWS, LANES), LOW)] * 2
         + [pltpu.VMEM((4, PAD_ROWS, LANES), LOW)] * 4
         + [pltpu.VMEM((4, A_ROWS, LANES), LOW)] * 2
@@ -1006,11 +1038,11 @@
         ),
         name="reduce_gradients",
     )(grad_rows, loss_row)
-    return shard_total.reshape(-1), jnp.sum(totals[0]), totals[1, 0, 0]
+    return shard_total.reshape(-1), square.reshape(()), loss.reshape(())
 
 
 ROWS = 256
-ENC_CHUNK = 64
+ENC_CHUNK = 256
 FETCHED = ("vecs", "embed", "enc_qkv", "enc_out", "enc_up", "enc_down", "project")
 BACKWARD_FETCHED = ("vecs", "project", "enc_down", "enc_up", "enc_out", "enc_qkv")
 
@@ -1247,7 +1279,6 @@
     product_t_into(grad_attn, middle, w_out, D)
     need(12, 11, 3)
     allowed = column_facts[:, 0:1] == row_facts[0:1, :]
-    allowed = jnp.concatenate([allowed.astype(FULL)] * 2, axis=0) > 0.5
 
     def attend_back(step):
         for part in range(2):
@@ -1258,8 +1289,8 @@
                 pl.ds(0, ROWS),
                 2 * step + part,
                 D,
-                allowed,
                 D // HEADS,
+                allowed=allowed,
             )
 
     loop(D // LANES // 2, attend_back)
@@ -1328,7 +1359,7 @@
 
 IMAGES = 5
 DECODER_FETCHED = ("vecs", "dec_qkv", "dec_out", "dec_up", "dec_down", "pixel")
-IMG_ROWS = 208
+IMG_ROWS = 200
 DEC_ROWS = IMAGES * IMG_ROWS
 
 
@@ -1356,6 +1387,7 @@
     grad_pred,
     upper,
     masked,
+    score_logs,
     turned,
     stage,
     stage_sem,
@@ -1384,29 +1416,30 @@
         masked[at, :] = jnp.broadcast_to(hidden, (IMG_ROWS, LANES))
         dec_in[at, :] = dot_nn(select.astype(LOW), projected[...]) + hidden * vec(6) + table_ref[...]
 
-    loop(IMAGES, place)
-    norm_into(low_rows, dec_in, vec(0), vec(1), DEC_ROWS, IMG_ROWS)
+    for index in range(IMAGES):
+        place(index)
+    norm_into(low_rows, dec_in, vec(0), vec(1), DEC_ROWS, DEC_ROWS)
     w_qkv = ready(1)
     product_into(qkv_rows, low_rows, w_qkv, 3 * DD)
     head_size = DD // DHEADS
     heads = LANES // head_size
-    allowed = lax.broadcasted_iota(jnp.int32, (heads * IMG_ROWS, IMG_ROWS), 1) < PATCHES
     groups = DD // LANES
 
     def attend(step):
         rows = span(step, IMG_ROWS)
         for at in range(groups):
-            attend_into(attn_out, qkv_rows, rows, at, DD, allowed, head_size)
+            logs = score_logs.at[pl.ds((step * groups + at) * heads, heads)]
+            attend_columns_into(attn_out, qkv_rows, rows, at, DD, PATCHES, head_size, logs)
 
     loop(IMAGES, attend)
     w_out = ready(2)
     product_into(after_attn, attn_out, w_out, DD, residual=dec_in)
-    norm_into(normed_b, after_attn, vec(2), vec(3), DEC_ROWS, IMG_ROWS)
+    norm_into(normed_b, after_attn, vec(2), vec(3), DEC_ROWS, DEC_ROWS)
     w_up = ready(3)
     up_into(hidden_act, slope, normed_b, w_up, DFF, TILE)
     w_down = ready(4)
     product_into(decoded, hidden_act, w_down, DD, residual=after_attn)
-    norm_into(final_dec, decoded, vec(4), vec(5), DEC_ROWS, IMG_ROWS)
+    norm_into(final_dec, decoded, vec(4), vec(5), DEC_ROWS, DEC_ROWS)
     w_pix = ready(5)
     loss_ref[...] = jnp.zeros_like(loss_ref)
 
@@ -1421,39 +1454,40 @@
         loss_ref[...] = loss_ref[...] + jnp.sum(rows) * (1.0 / mask_total)
         grad_pred[at, :] = (weight * error * (2.0 / (PIX * mask_total))).astype(LOW)
 
-    loop(IMAGES, compare)
+    for index in range(IMAGES):
+        compare(index)
 
     emit = Emitter(flat_ref, turned, stage, stage_sem)
 
     emit("pixel", final_dec, grad_pred)
     product_t_into(upper, grad_pred, w_pix, DD)
     grad_rows, branch = decoded, final_dec
-    norm_back(grad_rows, decoded, upper, None, vec(4), grad_of(4), grad_of(5), DEC_ROWS, IMG_ROWS)
+    norm_back(grad_rows, decoded, upper, None, vec(4), grad_of(4), grad_of(5), DEC_ROWS, DEC_ROWS)
     branch[...] = grad_rows[...].astype(LOW)
     emit("dec_down", hidden_act, branch)
     grad_pre = hidden_act
     down_back_into(grad_pre, branch, w_down, slope, DFF, TILE)
     emit("dec_up", normed_b, grad_pre)
     product_t_into(upper, grad_pre, w_up, DD)
-    norm_back(grad_rows, after_attn, upper, grad_rows, vec(2), grad_of(2), grad_of(3), DEC_ROWS, IMG_ROWS)
+    norm_back(grad_rows, after_attn, upper, grad_rows, vec(2), grad_of(2), grad_of(3), DEC_ROWS, DEC_ROWS)
     branch[...] = grad_rows[...].astype(LOW)
     emit("dec_out", attn_out, branch)
     grad_attn, grad_qkv = normed_b, grad_pre.at[:, pl.ds(0, 3 * DD)]
     product_t_into(grad_attn, branch, w_out, DD)
 
-    key_row = lax.broadcasted_iota(jnp.int32, (heads, IMG_ROWS, IMG_ROWS), 1)
-    real_keys = (key_row < PATCHES).astype(FULL).reshape(heads * IMG_ROWS, IMG_ROWS) > 0.5
-
     def attend_back(step):
         rows = span(step, IMG_ROWS)
         for at in range(groups):
-            attend_back_into(grad_qkv, grad_attn, qkv_rows, rows, at, DD, real_keys, head_size)
+            logs = score_logs.at[pl.ds((step * groups + at) * heads, heads)]
+            attend_back_into(
+                grad_qkv, grad_attn, qkv_rows, rows, at, DD, head_size, real=PATCHES, logs=logs
+            )
 
     loop(IMAGES, attend_back)
     emit("dec_qkv", low_rows, grad_qkv)
     emit.finish()
     product_t_into(upper, grad_qkv, w_qkv, DD)
-    norm_back(grad_rows, dec_in, upper, grad_rows, vec(0), grad_of(0), grad_of(1), DEC_ROWS, IMG_ROWS)
+    norm_back(grad_rows, dec_in, upper, grad_rows, vec(0), grad_of(0), grad_of(1), DEC_ROWS, DEC_ROWS)
     upper[pl.ds(0, ROWS), :] = jnp.zeros((ROWS, DD), FULL)
 
     def collect(index, token):
@@ -1500,6 +1534,7 @@
             low(DEC_ROWS, PIX),
             full(DEC_ROWS, DD),
             full(DEC_ROWS, LANES),
+            full(IMAGES * DHEADS, 1, IMG_ROWS),
             low(DFF, DEC_ROWS),
             low(2, DFF * DD // (TALL * LANES), TALL, LANES),
             pltpu.SemaphoreType.DMA((2,)),

time: 340 us -> 324 us (0.953)
  Pallas kernels: 325 us -> 309 us
    pallas_call x1, Pallas kernels: 80.3 us -> 67.8 us  [decoder_step(): pl.pallas_call(partial(decoder_kernel, mask_total=mask_total), out_shape=...]
where the time goes in v5:
time: 324 us; the launch traced here: 319 us
  Pallas kernels  309 us (95%)
  between operations  5.17 us (2%)
  other arithmetic  4.97 us (2%)
    pallas_call x1, Pallas kernels, reduce_gradients(): pl.pallas_call(reduce_kernel, out_shape=[jax.ShapeDtypeStruct((SHARD_ROWS...  103 us
    pallas_call x1, Pallas kernels, gather_weights(): pl.pallas_call(gather_kernel, out_shape=[jax.ShapeDtypeStruct((32 * SHARD...  96.4 us
    pallas_call x1, Pallas kernels, decoder_step(): pl.pallas_call(partial(decoder_kernel, mask_total=mask_total), out_shape=...  67.8 us
    pallas_call x1, Pallas kernels, encoder_backward(): pl.pallas_call(encoder_backward_kernel, out_shape=jax.ShapeDtypeStruct(fl...  26.8 us
    pallas_call x1, Pallas kernels, encoder_forward(): pl.pallas_call(encoder_forward_kernel, out_shape=[jax.ShapeDtypeStruct(s,...  15.1 us

profile of v5, /device:TPU:0, one launch (start us, length us, event | category | flops | bytes accessed | tf_op | source)
XLA Modules:
  0.0 319.1 jit_solution(892899739607231822)
XLA Ops:
  0.6 96.4 %gather_weights.1 = (bf16[90688,128]{1,0:T(8,128)(2,1)}, bf16[512,768]{1,0:T(8,128)(2,1)}) custom-call(f32[2834,128]{1,0:T(8,128)} %bitcast.18, bf16[256,768]{1,0:T(8,128)(2,1)} %bitcast.20), custom_call_target="tpu_custom_call" | custom-call | tf_op jit(solution)/shard_map/gather_weights/pallas_call | solution.py:755
  97.0 15.1 %encoder_forward.1 = (bf16[256,768]{1,0:T(8,128)(2,1)}, f32[256,768]{1,0:T(8,128)}, bf16[256,768]{1,0:T(8,128)(2,1)}, bf16[256,2304]{1,0:T(8,128)(2,1)}, bf16[25...) custom-call(s32[1]{0:T(128)} %bitcast.part_ref, ...), custom_call_target="tpu_custom_call" | custom-call | tf_op jit(solution)/shard_map/encoder_forward/pallas_call | solution.py:1183
  112.1 67.8 %decoder_step.1 = (bf16[5668,16,128]{2,1,0:T(8,128)(2,1)}, bf16[256,512]{1,0:T(8,128)(2,1)}, f32[8,512]{1,0:T(8,128)}, f32[1,128]{1,0:T(1,128)}) custom-call(s32[1]{0:T(128)} %bitcast.part_ref, bf16[256,512]{1,0:T(8,128)(2,1)} %get-tuple-element.31.projected, f32[16,256]{1,0:T(8,128)} %get-tuple-element.32.row_facts.refs_11_, bf16[5,196,768]{2,1,0:T(8,128)(2,1)} %bitcast.19, ...), custom_call_target="tpu_custom_call" | custom-call | tf_op jit(solution)/shard_map/decoder_step/pallas_call | solution.py:1513
  180.0 26.8 %encoder_backward.1 = bf16[5668,16,128]{2,1,0:T(8,128)(2,1)} custom-call(bf16[256,512]{1,0:T(8,128)(2,1)} %get-tuple-element.33.grad_projected, f32[8,512]{1,0:T(8,128)} %get-tuple-element.34.decoder_vecs, bf16[256,768]{1,0:T(8,128)(2,1)} %get-tuple-element.35.refs_0_, f32[256,768]{1,0:T(8,128)} %get-tuple-element.36.refs_1_, ...), custom_call_target="tpu_custom_call", output_to_operand_aliasing={{}: (16, {})} | custom-call | tf_op jit(solution)/shard_map/encoder_backward/pallas_call | solution.py:1330
  206.8 0.0 copy-start
  206.8 0.0 copy-start.1
  206.8 102.8 %reduce_gradients.1 = (f32[2834,128]{1,0:T(8,128)}, f32[1,1]{1,0:T(1,128)}, f32[1,1]{1,0:T(1,128)}) custom-call(bf16[90688,128]{1,0:T(8,128)(2,1)} %bitcast.17, f32[1,128]{1,0:T(1,128)} %get-tuple-element.48.loss_ref), custom_call_target="tpu_custom_call" | custom-call | tf_op jit(solution)/shard_map/reduce_gradients/pallas_call | solution.py:1014
  311.0 0.0 copy-done
  311.0 0.0 copy-done.1
  311.0 5.0 %fusion.1 = (bf16[362752]{0:T(1024)(128)(2,1)}, f32[362752]{0:T(1024)}, f32[362752]{0:T(1024)}, f32[362752]{0:T(1024)}) fusion(f32[362752]{0:T(1024)S(1)} %copy-done, f32[]{:T(128)} %bitcast.8, f32[2834,128]{1,0:T(8,128)} %get-tuple-element.49, f32[]{:T(128)S(6)} %min.3, f32[362752]{0:T(1024)S(1)} %copy-done.1, f32[362752]{0:T(1024)} %param.15), kind=kLoop, calls=%fused_computation.4 | loop fusion | flops 5804032 | bytes 10882568 | tf_op jit(solution)/shard_map/convert_element_type | solution.py:1614
Async XLA Ops:
  206.8 104.3 %copy-start = (f32[362752]{0:T(1024)S(1)}, f32[362752]{0:T(1024)}, u32[]{:S(2)}) copy-start(f32[362752]{0:T(1024)} %param.14) | copy-start | bytes 4353028
  206.8 104.3 %copy-start.1 = (f32[362752]{0:T(1024)S(1)}, f32[362752]{0:T(1024)}, u32[]{:S(2)}) copy-start(f32[362752]{0:T(1024)} %param.16) | copy-start | bytes 4353028

commit v6 on v5

--- a/solution.py
+++ b/solution.py
@@ -101,6 +101,8 @@
 
 
 def span(step, size):
+    if isinstance(step, int):
+        return pl.ds(step * size, size)
     return pl.ds(pl.multiple_of(step * size, size), size)
 
 
@@ -212,7 +214,8 @@
     def turn(step):
         turned[span(step, TILE), :] = left[:, span(step, TILE)].T
 
-    loop(rows // TILE, turn)
+    for index in range(rows // TILE):
+        turn(index)
     if before is not None:
         before()
     tiles = stage.at[slot, pl.ds(0, count)].reshape(high, groups, TALL, LANES)
@@ -1137,7 +1140,8 @@
                 attn_out, qkv_rows, pl.ds(0, ROWS), 2 * step + part, D, allowed, D // HEADS
             )
 
-    loop(D // LANES // 2, attend)
+    for index in range(D // LANES // 2):
+        attend(index)
     ship(4)
     w_out = ready(3)
     product_into(after_attn, attn_out, w_out, D, residual=embedded)
@@ -1293,7 +1297,8 @@
                 allowed=allowed,
             )
 
-    loop(D // LANES // 2, attend_back)
+    for index in range(D // LANES // 2):
+        attend_back(index)
     need(2)
     emit("enc_qkv", normed_a, grad_qkv)
     w_qkv = ready(5)
@@ -1431,7 +1436,8 @@
             logs = score_logs.at[pl.ds((step * groups + at) * heads, heads)]
             attend_columns_into(attn_out, qkv_rows, rows, at, DD, PATCHES, head_size, logs)
 
-    loop(IMAGES, attend)
+    for index in range(IMAGES):
+        attend(index)
     w_out = ready(2)
     product_into(after_attn, attn_out, w_out, DD, residual=dec_in)
     norm_into(normed_b, after_attn, vec(2), vec(3), DEC_ROWS, DEC_ROWS)
@@ -1483,7 +1489,8 @@
                 grad_qkv, grad_attn, qkv_rows, rows, at, DD, head_size, real=PATCHES, logs=logs
             )
 
-    loop(IMAGES, attend_back)
+    for index in range(IMAGES):
+        attend_back(index)
     emit("dec_qkv", low_rows, grad_qkv)
     emit.finish()
     product_t_into(upper, grad_qkv, w_qkv, DD)
@@ -1499,7 +1506,9 @@
         )
         return token
 
-    token = lax.fori_loop(0, IMAGES, collect, jnp.zeros((8, DD), FULL))
+    token = jnp.zeros((8, DD), FULL)
+    for index in range(IMAGES):
+        token = collect(index, token)
     grad_of(6)[...] = jnp.sum(token, axis=0, keepdims=True)
     grad_projected[...] = upper[pl.ds(0, ROWS), :].astype(LOW)
 

time: 324 us -> 313 us (0.966)
  Pallas kernels: 309 us -> 299 us
    pallas_call x1, Pallas kernels: 67.8 us -> 61.6 us  [decoder_step(): pl.pallas_call(partial(decoder_kernel, mask_total=mask_total), out_shape=...]
where the time goes in v6:
time: 313 us; the launch traced here: 309 us
  Pallas kernels  299 us (96%)
  between operations  5.21 us (2%)
  other arithmetic  4.97 us (2%)
    pallas_call x1, Pallas kernels, reduce_gradients(): pl.pallas_call(reduce_kernel, out_shape=[jax.ShapeDtypeStruct((SHARD_ROWS...  103 us
    pallas_call x1, Pallas kernels, gather_weights(): pl.pallas_call(gather_kernel, out_shape=[jax.ShapeDtypeStruct((32 * SHARD...  96.6 us
    pallas_call x1, Pallas kernels, decoder_step(): pl.pallas_call(partial(decoder_kernel, mask_total=mask_total), out_shape=...  61.6 us
    pallas_call x1, Pallas kernels, encoder_backward(): pl.pallas_call(encoder_backward_kernel, out_shape=jax.ShapeDtypeStruct(fl...  24.3 us
    pallas_call x1, Pallas kernels, encoder_forward(): pl.pallas_call(encoder_forward_kernel, out_shape=[jax.ShapeDtypeStruct(s,...  13.7 us

profile of v6, /device:TPU:0, one launch (start us, length us, event | category | flops | bytes accessed | tf_op | source)
XLA Modules:
  0.0 309.2 jit_solution(4455252091511671467)
XLA Ops:
  0.6 96.6 %gather_weights.1 = (bf16[90688,128]{1,0:T(8,128)(2,1)}, bf16[512,768]{1,0:T(8,128)(2,1)}) custom-call(f32[2834,128]{1,0:T(8,128)} %bitcast.18, bf16[256,768]{1,0:T(8,128)(2,1)} %bitcast.20), custom_call_target="tpu_custom_call" | custom-call | tf_op jit(solution)/shard_map/gather_weights/pallas_call | solution.py:758
  97.2 13.7 %encoder_forward.1 = (bf16[256,768]{1,0:T(8,128)(2,1)}, f32[256,768]{1,0:T(8,128)}, bf16[256,768]{1,0:T(8,128)(2,1)}, bf16[256,2304]{1,0:T(8,128)(2,1)}, bf16[25...) custom-call(s32[1]{0:T(128)} %bitcast.part_ref, ...), custom_call_target="tpu_custom_call" | custom-call | tf_op jit(solution)/shard_map/encoder_forward/pallas_call | solution.py:1187
  111.0 61.6 %decoder_step.1 = (bf16[5668,16,128]{2,1,0:T(8,128)(2,1)}, bf16[256,512]{1,0:T(8,128)(2,1)}, f32[8,512]{1,0:T(8,128)}, f32[1,128]{1,0:T(1,128)}) custom-call(s32[1]{0:T(128)} %bitcast.part_ref, bf16[256,512]{1,0:T(8,128)(2,1)} %get-tuple-element.31.projected, f32[16,256]{1,0:T(8,128)} %get-tuple-element.32.row_facts.refs_11_, bf16[5,196,768]{2,1,0:T(8,128)(2,1)} %bitcast.19, ...), custom_call_target="tpu_custom_call" | custom-call | tf_op jit(solution)/shard_map/decoder_step/pallas_call | solution.py:1522
  172.6 24.3 %encoder_backward.1 = bf16[5668,16,128]{2,1,0:T(8,128)(2,1)} custom-call(bf16[256,512]{1,0:T(8,128)(2,1)} %get-tuple-element.33.grad_projected, f32[8,512]{1,0:T(8,128)} %get-tuple-element.34.decoder_vecs, bf16[256,768]{1,0:T(8,128)(2,1)} %get-tuple-element.35.refs_0_, f32[256,768]{1,0:T(8,128)} %get-tuple-element.36.refs_1_, ...), custom_call_target="tpu_custom_call", output_to_operand_aliasing={{}: (16, {})} | custom-call | tf_op jit(solution)/shard_map/encoder_backward/pallas_call | solution.py:1335
  196.9 0.0 copy-start
  196.9 0.0 copy-start.1
  196.9 102.9 %reduce_gradients.1 = (f32[2834,128]{1,0:T(8,128)}, f32[1,1]{1,0:T(1,128)}, f32[1,1]{1,0:T(1,128)}) custom-call(bf16[90688,128]{1,0:T(8,128)(2,1)} %bitcast.17, f32[1,128]{1,0:T(1,128)} %get-tuple-element.48.loss_ref), custom_call_target="tpu_custom_call" | custom-call | tf_op jit(solution)/shard_map/reduce_gradients/pallas_call | solution.py:1017
  301.1 0.0 copy-done
  301.1 0.0 copy-done.1
  301.1 5.0 %fusion.1 = (bf16[362752]{0:T(1024)(128)(2,1)}, f32[362752]{0:T(1024)}, f32[362752]{0:T(1024)}, f32[362752]{0:T(1024)}) fusion(f32[362752]{0:T(1024)S(1)} %copy-done, f32[]{:T(128)} %bitcast.8, f32[2834,128]{1,0:T(8,128)} %get-tuple-element.49, f32[]{:T(128)S(6)} %min.3, f32[362752]{0:T(1024)S(1)} %copy-done.1, f32[362752]{0:T(1024)} %param.15), kind=kLoop, calls=%fused_computation.4 | loop fusion | flops 5804032 | bytes 10882568 | tf_op jit(solution)/shard_map/convert_element_type | solution.py:1623
Async XLA Ops:
  196.9 104.3 %copy-start = (f32[362752]{0:T(1024)S(1)}, f32[362752]{0:T(1024)}, u32[]{:S(2)}) copy-start(f32[362752]{0:T(1024)} %param.14) | copy-start | bytes 4353028
  196.9 104.3 %copy-start.1 = (f32[362752]{0:T(1024)S(1)}, f32[362752]{0:T(1024)}, u32[]{:S(2)}) copy-start(f32[362752]{0:T(1024)} %param.16) | copy-start | bytes 4353028

commit v7 on v6

--- a/solution.py
+++ b/solution.py
@@ -1442,7 +1442,7 @@
     product_into(after_attn, attn_out, w_out, DD, residual=dec_in)
     norm_into(normed_b, after_attn, vec(2), vec(3), DEC_ROWS, DEC_ROWS)
     w_up = ready(3)
-    up_into(hidden_act, slope, normed_b, w_up, DFF, TILE)
+    up_into(hidden_act, slope, normed_b, w_up, DFF, 512)
     w_down = ready(4)
     product_into(decoded, hidden_act, w_down, DD, residual=after_attn)
     norm_into(final_dec, decoded, vec(4), vec(5), DEC_ROWS, DEC_ROWS)
@@ -1472,7 +1472,7 @@
     branch[...] = grad_rows[...].astype(LOW)
     emit("dec_down", hidden_act, branch)
     grad_pre = hidden_act
-    down_back_into(grad_pre, branch, w_down, slope, DFF, TILE)
+    down_back_into(grad_pre, branch, w_down, slope, DFF, 512)
     emit("dec_up", normed_b, grad_pre)
     product_t_into(upper, grad_pre, w_up, DD)
     norm_back(grad_rows, after_attn, upper, grad_rows, vec(2), grad_of(2), grad_of(3), DEC_ROWS, DEC_ROWS)

time: 313 us -> 311 us (level)
  no operation moved by 1% of the time
where the time goes in v7:
time: 311 us; the launch traced here: 307 us
  Pallas kernels  297 us (95%)
  between operations  5.21 us (2%)
  other arithmetic  4.97 us (2%)
    pallas_call x1, Pallas kernels, reduce_gradients(): pl.pallas_call(reduce_kernel, out_shape=[jax.ShapeDtypeStruct((SHARD_ROWS...  103 us
    pallas_call x1, Pallas kernels, gather_weights(): pl.pallas_call(gather_kernel, out_shape=[jax.ShapeDtypeStruct((32 * SHARD...  96.6 us
    pallas_call x1, Pallas kernels, decoder_step(): pl.pallas_call(partial(decoder_kernel, mask_total=mask_total), out_shape=...  59.6 us
    pallas_call x1, Pallas kernels, encoder_backward(): pl.pallas_call(encoder_backward_kernel, out_shape=jax.ShapeDtypeStruct(fl...  24.3 us
    pallas_call x1, Pallas kernels, encoder_forward(): pl.pallas_call(encoder_forward_kernel, out_shape=[jax.ShapeDtypeStruct(s,...  13.7 us

profile of v7, /device:TPU:0, one launch (start us, length us, event | category | flops | bytes accessed | tf_op | source)
XLA Modules:
  0.0 307.2 jit_solution(12695708765173064743)
XLA Ops:
  0.6 96.6 %gather_weights.1 = (bf16[90688,128]{1,0:T(8,128)(2,1)}, bf16[512,768]{1,0:T(8,128)(2,1)}) custom-call(f32[2834,128]{1,0:T(8,128)} %bitcast.18, bf16[256,768]{1,0:T(8,128)(2,1)} %bitcast.20), custom_call_target="tpu_custom_call" | custom-call | tf_op jit(solution)/shard_map/gather_weights/pallas_call | solution.py:758
  97.2 13.7 %encoder_forward.1 = (bf16[256,768]{1,0:T(8,128)(2,1)}, f32[256,768]{1,0:T(8,128)}, bf16[256,768]{1,0:T(8,128)(2,1)}, bf16[256,2304]{1,0:T(8,128)(2,1)}, bf16[25...) custom-call(s32[1]{0:T(128)} %bitcast.part_ref, ...), custom_call_target="tpu_custom_call" | custom-call | tf_op jit(solution)/shard_map/encoder_forward/pallas_call | solution.py:1187
  111.0 59.6 %decoder_step.1 = (bf16[5668,16,128]{2,1,0:T(8,128)(2,1)}, bf16[256,512]{1,0:T(8,128)(2,1)}, f32[8,512]{1,0:T(8,128)}, f32[1,128]{1,0:T(1,128)}) custom-call(s32[1]{0:T(128)} %bitcast.part_ref, bf16[256,512]{1,0:T(8,128)(2,1)} %get-tuple-element.31.projected, f32[16,256]{1,0:T(8,128)} %get-tuple-element.32.row_facts.refs_11_, bf16[5,196,768]{2,1,0:T(8,128)(2,1)} %bitcast.19, ...), custom_call_target="tpu_custom_call" | custom-call | tf_op jit(solution)/shard_map/decoder_step/pallas_call | solution.py:1522
  170.6 24.3 %encoder_backward.1 = bf16[5668,16,128]{2,1,0:T(8,128)(2,1)} custom-call(bf16[256,512]{1,0:T(8,128)(2,1)} %get-tuple-element.33.grad_projected, f32[8,512]{1,0:T(8,128)} %get-tuple-element.34.decoder_vecs, bf16[256,768]{1,0:T(8,128)(2,1)} %get-tuple-element.35.refs_0_, f32[256,768]{1,0:T(8,128)} %get-tuple-element.36.refs_1_, ...), custom_call_target="tpu_custom_call", output_to_operand_aliasing={{}: (16, {})} | custom-call | tf_op jit(solution)/shard_map/encoder_backward/pallas_call | solution.py:1335
  194.8 0.0 copy-start
  194.9 0.0 copy-start.1
  194.9 102.9 %reduce_gradients.1 = (f32[2834,128]{1,0:T(8,128)}, f32[1,1]{1,0:T(1,128)}, f32[1,1]{1,0:T(1,128)}) custom-call(bf16[90688,128]{1,0:T(8,128)(2,1)} %bitcast.17, f32[1,128]{1,0:T(1,128)} %get-tuple-element.48.loss_ref), custom_call_target="tpu_custom_call" | custom-call | tf_op jit(solution)/shard_map/reduce_gradients/pallas_call | solution.py:1017
  299.1 0.0 copy-done
  299.1 0.0 copy-done.1
  299.1 5.0 %fusion.1 = (bf16[362752]{0:T(1024)(128)(2,1)}, f32[362752]{0:T(1024)}, f32[362752]{0:T(1024)}, f32[362752]{0:T(1024)}) fusion(f32[362752]{0:T(1024)S(1)} %copy-done, f32[]{:T(128)} %bitcast.8, f32[2834,128]{1,0:T(8,128)} %get-tuple-element.49, f32[]{:T(128)S(6)} %min.3, f32[362752]{0:T(1024)S(1)} %copy-done.1, f32[362752]{0:T(1024)} %param.15), kind=kLoop, calls=%fused_computation.4 | loop fusion | flops 5804032 | bytes 10882568 | tf_op jit(solution)/shard_map/convert_element_type | solution.py:1623
Async XLA Ops:
  194.8 104.3 %copy-start = (f32[362752]{0:T(1024)S(1)}, f32[362752]{0:T(1024)}, u32[]{:S(2)}) copy-start(f32[362752]{0:T(1024)} %param.14) | copy-start | bytes 4353028
  194.9 104.3 %copy-start.1 = (f32[362752]{0:T(1024)S(1)}, f32[362752]{0:T(1024)}, u32[]{:S(2)}) copy-start(f32[362752]{0:T(1024)} %param.16) | copy-start | bytes 4353028
